TPU v7x, 128 devices: a whole 4x4x4 slice. The times are simulated.
128 devices in a mesh: seq: 32 (over z, x, core), dp: 4 (over y).
Axes of the slice: x: 4, y: 4, z: 4, core: 2. Of those that a mesh axis runs over, the one named last changes fastest.
Arguments:
- features: bfloat16 [131072, 768], P(('dp', 'seq')), parts along dimension 0, may hold values from -6 to 6
- conv_one: bfloat16 [5, 768, 896], replicated, may hold values from -0.09375 to 0.09375
- conv_two: bfloat16 [5, 896, 1024], replicated, may hold values from -0.09375 to 0.09375
- head_vector: float32 [1024], replicated, may hold values from -5 to 5
- owner_of: int32 [32768, 1], P(('dp', 'seq')), parts along dimension 0, may hold values from 0 to 31; in each aligned block of 256 rows (0 to 255, 256 to 511, ...) at most 16 rows name the same one
- donor_row: int32 [32768], P(('dp', 'seq')), parts along dimension 0, may hold values from 0 to 255
- accept_row: int32 [32768], P(('dp', 'seq')), parts along dimension 0, may hold values from 0 to 255
- score_grad: bfloat16 [32768], P(('dp', 'seq')), parts along dimension 0, may hold values from -6 to 6
Outputs:
- grad_one: float32 [3584, 5, 768], P(('dp', 'seq')), parts along dimension 0
- grad_two: float32 [4096, 5, 896], P(('dp', 'seq')), parts along dimension 0
There are 4 independent parts, one for each index of `dp`. A program takes and returns all parts, laid end to end along the dimension named above; an argument that names none is the same for every part. Nothing has to cross between parts.
Inputs may be any that keep to these rules, and one draw needn't show every extreme that they name: `owner_of`: among the 256 junction records of one device no owner is named more than 16 times, and in some device's records one owner exactly 16 times.
All inputs are finite; a program needn't handle non-finite values.
Results may differ from a plain program's by a relative error of at most 0.0056.
Values may be sent and summed in bfloat16 or wider, within the bound.
No kernel may reach another device: no remote copies, remote signals or barrier semaphores. Data moves between devices by JAX's collectives and lax.ppermute only.
A program may use at most 192 MiB of HBM per device.

v0:
```python
import functools

import jax
import jax.numpy as jnp
from jax import lax
from jax.experimental import pallas as pl
from jax.experimental.pallas import tpu as pltpu
from jax.sharding import PartitionSpec as P


NZ, NX = 4, 4
BF = jnp.bfloat16
F32 = jnp.float32


def index_of(z, x, c):
    return ((z % NZ) * NX + (x % NX)) * 2 + c


def pairs_of(move):
    return [
        (index_of(z, x, c), index_of(*move(z, x, c)))
        for z in range(NZ)
        for x in range(NX)
        for c in range(2)
    ]


SIBLING = pairs_of(lambda z, x, c: (z, x, 1 - c))
RINGS = (
    (
        pairs_of(lambda z, x, c: (z, x + 1, c) if c == 0 else (z + 1, x, c)),
        pairs_of(lambda z, x, c: (z, x - 1, c) if c == 0 else (z - 1, x, c)),
    ),
    (
        pairs_of(lambda z, x, c: (z + 1, x, c) if c == 0 else (z, x + 1, c)),
        pairs_of(lambda z, x, c: (z - 1, x, c) if c == 0 else (z, x - 1, c)),
    ),
)
N_SEQ = NZ * NX * 2
OUTWARD = [(s, s - 1) for s in range(2, N_SEQ, 2)] + [(s, s + 1) for s in range(1, N_SEQ - 1, 2)]


def move(value, pairs):
    return lax.ppermute(value, "seq", pairs)


VM = pltpu.VMEM
IN_VMEM = pl.BlockSpec(memory_space=pltpu.VMEM)
IN_PLACE = pl.BlockSpec(memory_space=pl.ANY)
LANES = 128
PIECE = 128
TILE = 256
RIM = 16


def params(mib=52):
    return pltpu.CompilerParams(vmem_limit_bytes=mib << 20)


def cost(flops, bytes_accessed, transcendentals=0):
    return pl.CostEstimate(
        flops=flops, bytes_accessed=bytes_accessed, transcendentals=transcendentals
    )


def gelu_both(v):
    c, a = 0.7978845608028654, 0.044715
    sq = v * v
    t = jnp.tanh(c * v * (1.0 + a * sq))
    up = 0.5 * (1.0 + t)
    return v * up, up + 0.5 * v * (1.0 - t * t) * (c * (1.0 + 3.0 * a * sq))


def fill_rims(rimmed, block_ref, rim_ref):
    n = block_ref.shape[0]
    rimmed[0:RIM] = rim_ref[0:RIM]
    rimmed[RIM : RIM + n] = block_ref[...]
    rimmed[RIM + n : 2 * RIM + n] = rim_ref[RIM : 2 * RIM]


def conv_kernel(
    taps, x_ref, rim_ref, w_hbm, pooled_ref, even_ref, odd_ref, w_ref, rimmed, piece, wide, acc, sem
):
    n, f = x_ref.shape
    copies = [
        pltpu.make_async_copy(w_hbm.at[k], w_ref.at[pl.ds(k * f, f)], sem.at[k])
        for k in range(taps)
    ]
    for copy in copies:
        copy.start()
    fill_rims(rimmed, x_ref, rim_ref)

    @pl.loop(0, n // PIECE)
    def _(m):
        r = pl.multiple_of(m * PIECE, PIECE)
        piece[...] = rimmed[pl.ds(r, PIECE + 2 * RIM), :].astype(F32)
        for k in range(taps):
            low = RIM - taps // 2 + k
            wide[pl.ds(r, PIECE), k * f : (k + 1) * f] = piece[low : low + PIECE, :].astype(BF)

    for copy in copies:
        copy.wait()

    @pl.loop(0, n // TILE)
    def _(m):
        r = pl.multiple_of(m * TILE, TILE)
        q = pl.ds(pl.multiple_of(m * (TILE // 2), TILE // 2), TILE // 2)
        total = jnp.dot(wide[pl.ds(r, TILE), :], w_ref[...], preferred_element_type=F32)
        for j in range(acc.shape[0]):
            cols = slice(j * LANES, (j + 1) * LANES)
            acc[j] = total[:, cols]
            even, even_slope = gelu_both(acc[j, pl.ds(0, TILE // 2, stride=2), :])
            odd, odd_slope = gelu_both(acc[j, pl.ds(1, TILE // 2, stride=2), :])
            pooled_ref[q, cols] = ((even + odd) * 0.5).astype(BF)
            even_ref[q, cols] = (even_slope * 0.5).astype(BF)
            odd_ref[q, cols] = (odd_slope * 0.5).astype(BF)


def conv_pool(x, rim, w):
    taps, f, c = w.shape
    n = x.shape[0]
    return pl.pallas_call(
        functools.partial(conv_kernel, taps),
        out_shape=[jax.ShapeDtypeStruct((n // 2, c), BF)]
        + [jax.ShapeDtypeStruct((n // 2, c), BF)] * 2,
        in_specs=[IN_VMEM, IN_VMEM, IN_PLACE],
        out_specs=[IN_VMEM] * 3,
        scratch_shapes=[
            VM((taps * f, c), BF),
            VM((n + 2 * RIM, f), BF),
            VM((PIECE + 2 * RIM, f), F32),
            VM((n, taps * f), BF),
            VM((c // LANES, TILE, LANES), F32),
            pltpu.SemaphoreType.DMA((taps,)),
        ],
        compiler_params=params(),
        cost_estimate=cost(2 * n * f * c * taps, 2 * (n * f + taps * f * c) + 5 * n * c, n * c),
        name="conv_pool",
    )(x, rim, w)


def back_kernel(
    taps, g_ref, rim_ref, w_hbm, even_ref, odd_ref, order_ref, out_ref, w_ref, rimmed, piece, wide, pairs, flat, sem
):
    n = g_ref.shape[0]
    copies = [pltpu.make_async_copy(w_hbm.at[k], w_ref.at[k], sem.at[k]) for k in range(taps)]
    for copy in copies:
        copy.start()
    fill_rims(rimmed, g_ref, rim_ref)

    @pl.loop(0, n // PIECE)
    def _(m):
        r = pl.multiple_of(m * PIECE, PIECE)
        piece[...] = rimmed[pl.ds(r, PIECE + 2 * RIM), :].astype(F32)
        for k in range(taps):
            low = RIM + taps // 2 - k
            wide[k, pl.ds(r, PIECE), :] = piece[low : low + PIECE, :].astype(BF)

    for copy in copies:
        copy.wait()

    @pl.loop(0, n // TILE)
    def _(m):
        r = pl.multiple_of(m * TILE, TILE)
        rows = pl.ds(r, TILE)
        total = sum(
            lax.dot_general(
                wide[k, rows, :], w_ref[k], (((1,), (1,)), ((), ())), preferred_element_type=F32
            )
            for k in range(taps)
        )
        for j in range(pairs.shape[0]):
            cols = slice(j * LANES, (j + 1) * LANES)
            pairs[j, pl.ds(0, TILE, stride=2), :] = total[:, cols] * even_ref[rows, cols]
            pairs[j, pl.ds(1, TILE, stride=2), :] = total[:, cols] * odd_ref[rows, cols]
            flat[:, cols] = pairs[j].astype(BF)
        turned = lax.dot_general(
            order_ref[...], flat[...], (((1,), (1,)), ((), ())), preferred_element_type=F32
        )
        out_ref[:, pl.ds(pl.multiple_of(2 * r, 2 * TILE), 2 * TILE)] = turned.astype(BF)


def conv_back(g, rim, w, even, odd, order):
    taps, f, c = w.shape
    n = g.shape[0]
    return pl.pallas_call(
        functools.partial(back_kernel, taps),
        out_shape=jax.ShapeDtypeStruct((f, 2 * n), BF),
        in_specs=[IN_VMEM, IN_VMEM, IN_PLACE, IN_VMEM, IN_VMEM, IN_VMEM],
        out_specs=IN_VMEM,
        scratch_shapes=[
            VM((taps, f, c), BF),
            VM((n + 2 * RIM, c), BF),
            VM((PIECE + 2 * RIM, c), F32),
            VM((taps, n, c), BF),
            VM((f // LANES, 2 * TILE, LANES), F32),
            VM((2 * TILE, f), BF),
            pltpu.SemaphoreType.DMA((taps,)),
        ],
        compiler_params=params(),
        cost_estimate=cost(
            2 * n * f * c * taps + 4 * n * f * f, 2 * (n * c + taps * f * c + f * f) + 12 * n * f
        ),
        name="conv_back",
    )(g, rim, w, even, odd, order)


def head_kernel(add_ref, come_ref, head_ref, even_ref, odd_ref, order_ref, g_ref, turned_ref, pairs):
    n = add_ref.shape[0]
    total = jnp.dot(add_ref[...], come_ref[...], preferred_element_type=F32) * head_ref[...]
    for j in range(pairs.shape[0]):
        cols = slice(j * LANES, (j + 1) * LANES)
        pairs[j, pl.ds(0, n, stride=2), :] = total[:, cols] * even_ref[:, cols]
        pairs[j, pl.ds(1, n, stride=2), :] = total[:, cols] * odd_ref[:, cols]
        g_ref[:, cols] = pairs[j].astype(BF)
    turned_ref[...] = lax.dot_general(
        order_ref[...], g_ref[...], (((1,), (1,)), ((), ())), preferred_element_type=F32
    ).astype(BF)


def head_back(add, come, head, even, odd, order):
    n, c = even.shape
    return pl.pallas_call(
        head_kernel,
        out_shape=[jax.ShapeDtypeStruct((2 * n, c), BF), jax.ShapeDtypeStruct((c, 2 * n), BF)],
        in_specs=[IN_VMEM] * 6,
        out_specs=[IN_VMEM] * 2,
        scratch_shapes=[VM((c // LANES, 2 * n, LANES), F32)],
        compiler_params=params(),
        cost_estimate=cost(
            2 * n * c * come.shape[0] + 4 * n * c * c, 2 * (come.size + add.size + c * c) + 16 * n * c
        ),
        name="head_back",
    )(add, come, head, even, odd, order)


def window_kernel(taps, own_ref, own_rim, other_ref, other_rim, out_ref, rimmed, piece):
    n = own_ref.shape[0]
    step = pl.program_id(0)

    @pl.when(step == 0)
    def _():
        fill_rims(rimmed.at[0], own_ref, own_rim)
        fill_rims(rimmed.at[1], other_ref, other_rim)

    per = n // PIECE
    side, m = step // per, step % per
    r = pl.multiple_of(m * PIECE, PIECE)
    piece[...] = rimmed[side, pl.ds(r, PIECE + 2 * RIM), :].astype(F32)
    for k in range(taps):
        low = RIM - taps // 2 + k
        out_ref[k] = piece[low : low + PIECE, :].astype(BF)


def windows_of(own, own_rim, other, other_rim, taps):
    n, f = own.shape
    return pl.pallas_call(
        functools.partial(window_kernel, taps),
        grid=(2 * n // PIECE,),
        out_shape=pltpu.HBM((taps, 2 * n, f), BF),
        in_specs=[IN_VMEM] * 4,
        out_specs=pl.BlockSpec((taps, PIECE, f), lambda i: (0, i, 0)),
        scratch_shapes=[VM((2, n + 2 * RIM, f), BF), VM((PIECE + 2 * RIM, f), F32)],
        compiler_params=params(),
        cost_estimate=cost(0, 2 * (taps + 1) * 2 * n * f),
        name="windows",
    )(own, own_rim, other, other_rim)


def grad_kernel(mine_ref, got_ref, wide_ref, plus_ref, minus_ref, keep_ref, both):
    m, n = mine_ref.shape

    @pl.when(pl.program_id(0) == 0)
    def _():
        both[:, :n] = mine_ref[...]
        both[:, n:] = got_ref[...]

    total = jnp.dot(both[...], wide_ref[0], preferred_element_type=F32)
    plus_ref[0] = total[: m // 4].astype(BF)
    minus_ref[0] = total[m // 4 : m // 2].astype(BF)
    keep_ref[0] = total[m // 2 :]


def grad_parts(mine, got, wide):
    m, n = mine.shape
    taps, _, f = wide.shape
    block = lambda rows: pl.BlockSpec((1, rows, f), lambda k: (k, 0, 0))
    return pl.pallas_call(
        grad_kernel,
        grid=(taps,),
        out_shape=[
            pltpu.HBM((taps, m // 4, f), BF),
            pltpu.HBM((taps, m // 4, f), BF),
            pltpu.HBM((taps, m // 2, f), F32),
        ],
        in_specs=[IN_VMEM, IN_VMEM, block(2 * n)],
        out_specs=[block(m // 4), block(m // 4), block(m // 2)],
        scratch_shapes=[VM((m, 2 * n), BF)],
        compiler_params=params(),
        cost_estimate=cost(
            4 * m * n * f * taps, 2 * (2 * m * n + 2 * taps * n * f) + 3 * taps * m * f
        ),
        name="grad_parts",
    )(mine, got, wide)


def outer_rim(block, odd):
    return move(jnp.where(odd, block[-2:], block[:2]), OUTWARD)


def rim_of(odd, inner, outer):
    pad = jnp.zeros((RIM - 2, inner.shape[1]), inner.dtype)
    return jnp.concatenate(
        [pad, jnp.where(odd, inner, outer), jnp.where(odd, outer, inner), pad], axis=0
    )


EIGHTHS = ((2, 0), (1, 1), (2, 1), (3, 0), (1, 0), (3, 1), (0, 0), (0, 1))


def order_matrix(channels, seq):
    block = channels // N_SEQ
    core, x, z = seq % 2, (seq // 2) % NX, seq // (2 * NX)
    row = lax.broadcasted_iota(jnp.int32, (channels, 1), 0)
    half, eighth = row // (16 * block), (row // (2 * block)) % 8
    r1 = sum(jnp.where(eighth == e, r, 0) for e, (r, _) in enumerate(EIGHTHS))
    r2 = sum(jnp.where(eighth == e, 2 * h, 0) for e, (_, h) in enumerate(EIGHTHS))
    r2 = r2 + (row // block) % 2
    side = jnp.where(half == 0, core, 1 - core)
    to_x = (x + jnp.where(side == 0, r1, r2)) % NX
    to_z = (z + jnp.where(side == 0, r2, r1)) % NZ
    wanted = ((to_z * NX + to_x) * 2 + side) * block + row % block
    return (wanted == lax.broadcasted_iota(jnp.int32, (1, channels), 1)).astype(BF)


def ring_sums(plus, minus, keep):
    u = keep.shape[1] // 4
    wide = lambda v: v.astype(F32)
    got_p = move(plus, RINGS[0][0])
    got_m = move(minus, RINGS[0][1])
    late_p = move((keep[:, :u] + wide(got_p[:, :u])).astype(BF), RINGS[0][0])
    late_m = move((keep[:, u : 2 * u] + wide(got_m[:, :u])).astype(BF), RINGS[0][1])
    low = keep[:, 2 * u : 3 * u] + wide(got_m[:, u:]) + wide(late_p)
    high = keep[:, 3 * u :] + wide(got_p[:, u:]) + wide(late_m)
    b = u // 2
    near, one, two, three = low[:, :b], low[:, b:], high[:, :b], high[:, b:]
    cut = keep.shape[0] // 2
    early = lax.broadcasted_iota(jnp.int32, near.shape, 0) < cut
    join = lambda first, last: jnp.where(early, first, last)
    got_p = move(join(two, one).astype(BF), RINGS[1][0])
    got_m = move(join(three, two).astype(BF), RINGS[1][1])
    late_p = move((one[:cut] + wide(got_p[:cut])).astype(BF), RINGS[1][0])
    late_m = move((three[cut:] + wide(got_m[cut:])).astype(BF), RINGS[1][1])
    return (
        near
        + wide(join(got_m, got_p))
        + jnp.concatenate([wide(late_p), wide(late_m)], axis=0)
    )


def body(features, conv_one, conv_two, head_vector, owner_of, donor_row, accept_row, score_grad):
    seq = lax.axis_index("seq")
    odd = seq % 2 == 1
    taps = conv_one.shape[0]
    rows_one = features.shape[0]
    rows_two = rows_one // 2
    rows_c = rows_two // 2
    records = owner_of.shape[0]
    capacity = max(2, 2 * records // N_SEQ)
    slots = N_SEQ * capacity

    feat_outer = outer_rim(features, odd)
    feat_other = move(features, SIBLING)
    feat_rim = rim_of(odd, jnp.where(odd, feat_other[-2:], feat_other[:2]), feat_outer)
    owners = owner_of
    before = (owners == owners.reshape(1, records)) & (
        lax.broadcasted_iota(jnp.int32, (records, records), 1)
        < lax.broadcasted_iota(jnp.int32, (records, records), 0)
    )
    place = owners * capacity + jnp.sum(before.astype(jnp.int32), axis=1, keepdims=True)
    placed = (place == lax.broadcasted_iota(jnp.int32, (records, slots), 1)).astype(BF)
    told = jnp.stack([donor_row.astype(BF), score_grad], 0)
    sent = jnp.dot(told, placed, preferred_element_type=F32).astype(BF)
    sent = sent.reshape(2, N_SEQ, capacity).transpose(1, 0, 2)
    heard = lax.all_to_all(sent, "seq", split_axis=0, concat_axis=0, tiled=True)
    accepts = (
        accept_row[None, :] == lax.broadcasted_iota(jnp.int32, (rows_c, records), 0)
    ).astype(BF)
    accept_pick = jnp.dot(accepts, placed, preferred_element_type=F32).astype(BF)
    accept_add = jnp.dot(
        accepts * score_grad[None, :], placed, preferred_element_type=F32
    ).astype(BF)

    order_one = order_matrix(conv_one.shape[2], seq)
    order_two = order_matrix(conv_two.shape[2], seq)

    pooled, even_one, odd_one = conv_pool(features, feat_rim, conv_one)
    pool_outer = outer_rim(pooled, odd)
    pool_other = move(pooled, SIBLING)
    pool_rim = rim_of(odd, jnp.where(odd, pool_other[-2:], pool_other[:2]), pool_outer)
    embed, even_two, odd_two = conv_pool(pooled, pool_rim, conv_two)
    feat_other_rim = rim_of(
        ~odd, jnp.where(odd, features[:2], features[-2:]), move(feat_outer, SIBLING)
    )
    pool_other_rim = rim_of(
        ~odd, jnp.where(odd, pooled[:2], pooled[-2:]), move(pool_outer, SIBLING)
    )

    heard = lax.optimization_barrier((heard, pooled))[0]
    heard = heard.transpose(1, 0, 2).reshape(2, slots)
    donor_hit = heard[0:1].astype(F32) == lax.broadcasted_iota(
        jnp.int32, (rows_c, slots), 0
    ).astype(F32)
    donor_pick = donor_hit.astype(BF)
    donor_add = jnp.where(donor_hit, heard[1:2], jnp.zeros((), BF))
    pick = jnp.concatenate(
        [accept_pick.reshape(rows_c, N_SEQ, capacity), donor_pick.reshape(rows_c, N_SEQ, capacity)],
        axis=2,
    ).reshape(rows_c, 2 * slots)
    add = jnp.concatenate(
        [donor_add.reshape(rows_c, N_SEQ, capacity), accept_add.reshape(rows_c, N_SEQ, capacity)],
        axis=2,
    ).reshape(rows_c, 2 * slots)
    gone = lax.dot_general(
        pick, embed, (((0,), (0,)), ((), ())), preferred_element_type=F32
    ).astype(BF)
    come = lax.all_to_all(gone, "seq", split_axis=0, concat_axis=0, tiled=True)
    own, feat_other = lax.optimization_barrier((features, feat_other, gone))[:2]
    wide_one = windows_of(own, feat_rim, feat_other, feat_other_rim, taps)
    own, pool_other = lax.optimization_barrier((pooled, pool_other, gone))[:2]
    wide_two = windows_of(own, pool_rim, pool_other, pool_other_rim, taps)

    come, wide_one, wide_two = lax.optimization_barrier((come, wide_one, wide_two))
    grads, turned_two = head_back(add, come, head_vector[None, :], even_two, odd_two, order_two)
    grad_rim = rim_of(
        odd, move(jnp.where(odd, grads[:2], grads[-2:]), SIBLING), outer_rim(grads, odd)
    )
    half = turned_two.shape[0] // 2
    parts_two = grad_parts(turned_two[:half], move(turned_two[half:], SIBLING), wide_two)
    grads = lax.optimization_barrier((grads, parts_two))[0]
    turned_one = conv_back(grads, grad_rim, conv_two, even_one, odd_one, order_one)
    half = turned_one.shape[0] // 2
    got = move(turned_one[half:], SIBLING)
    parts_one = grad_parts(turned_one[:half], got, wide_one)
    grad_two = ring_sums(*parts_two).transpose(1, 0, 2)
    grad_one = ring_sums(*parts_one).transpose(1, 0, 2)
    return (grad_one, grad_two)


def solution(mesh):
    in_specs = (
        P(("dp", "seq"), None),
        P(),
        P(),
        P(),
        P(("dp", "seq"), None),
        P(("dp", "seq")),
        P(("dp", "seq")),
        P(("dp", "seq")),
    )
    out_specs = (P(("dp", "seq"), None, None), P(("dp", "seq"), None, None))

    return jax.shard_map(body, mesh=mesh, in_specs=in_specs, out_specs=out_specs, check_vma=False)
```

profile of v0, /device:TPU:0, one launch (start us, length us, event | category | flops | bytes accessed | tf_op | source)
XLA Modules:
  0.0 209.2 jit_solution(17198700769932391317)
XLA Ops:
  2.1 0.9 convert_reduce_fusion
  4.7 8.4 %all-to-all-start = ((bf16[32,2,16]{2,1,0:T(2,128)(2,1)}), bf16[32,2,16]{2,1,0:T(2,128)(2,1)S(1)}, u32[]{:S(2)}, u32[]{:S(2)}) async-start(bf16[32,2,16]{2,1,0:T(2,128)(2,1)} %copy.24), calls=%async_computation | async-start | bytes 32768 | tf_op jit(solution)/shard_map/all_to_all | solution.py:386
  13.1 0.7 broadcast_select_fusion.16
  14.5 1.0 convolution_convert_fusion.1
  15.5 3.8 %collective-permute-start.4 = (bf16[2,768]{1,0:T(2,128)(2,1)S(1)}, bf16[2,768]{1,0:T(2,128)(2,1)S(1)}, u32[]{:S(2)}, u32[]{:S(2)}) collective-permute-start(bf16[2,768]{1,0:T(2,128)(2,1)S(1)} %collective-permute-done.1), channel_id=1, source_target_pairs={{0,4},{4,0},{8,12},{12,8},{16,20},{20,16},{24,28},{28,24},{32,36},... | collective-permute-start | bytes 9224 | tf_op jit(solution)/shard_map/ppermute | solution.py:45
  20.1 0.7 broadcast_select_fusion.12
  20.9 0.7 pad_maximum_fusion.6
  22.0 16.3 %conv_pool.2 = (bf16[512,896]{1,0:T(8,128)(2,1)S(1)}, bf16[512,896]{1,0:T(8,128)(2,1)S(1)}, bf16[512,896]{1,0:T(8,128)(2,1)}) custom-call(bf16[1024,768]{1,0:T(8,128)(2,1)} %own_ref, bf16[32,768]{1,0:T(8,128)(2,1)S(1)} %get-tuple-element.73.rim_ref.own_rim, bf16[5,768,896]{2,1,0:T(8,128)(2,1)} %w_hbm.3), custom_call_target="tpu_custom_call" | custom-call | flops 7046430720 | bytes 13041664 | tf_op jit(solution)/shard_map/conv_pool/pallas_call | solution.py:123
  38.4 0.9 copy-done.11
  40.7 4.3 %collective-permute-start.5 = (bf16[2,896]{1,0:T(2,128)(2,1)S(1)}, bf16[2,896]{1,0:T(2,128)(2,1)S(1)}, u32[]{:S(2)}, u32[]{:S(2)}) collective-permute-start(bf16[2,896]{1,0:T(2,128)(2,1)S(1)} %collective-permute-done.3), channel_id=1, source_target_pairs={{0,4},{4,0},{8,12},{12,8},{16,20},{20,16},{24,28},{28,24},{32,36},... | collective-permute-start | bytes 10760 | tf_op jit(solution)/shard_map/ppermute | solution.py:45
  45.0 0.8 collective-permute-done.5
  45.9 11.6 %conv_pool.3 = (bf16[256,1024]{1,0:T(8,128)(2,1)S(1)}, bf16[256,1024]{1,0:T(8,128)(2,1)S(1)}, bf16[256,1024]{1,0:T(8,128)(2,1)S(1)}) custom-call(bf16[512,896]{1,0:T(8,128)(2,1)} %copy-done.1, bf16[32,896]{1,0:T(8,128)(2,1)S(1)} %get-tuple-element.71.rim_ref.own_rim, bf16[5,896,1024]{2,1,0:T(8,128)(2,1)} %w_hbm.5), custom_call_target="tpu_custom_call" | custom-call | flops 4697620480 | bytes 12713984 | tf_op jit(solution)/shard_map/conv_pool/pallas_call | solution.py:123
  57.5 2.0 convolution_convert_fusion
  59.5 11.3 %all-to-all-start.1 = ((bf16[32,32,1024]{2,1,0:T(8,128)(2,1)}), bf16[32,32,1024]{2,1,0:T(8,128)(2,1)}, u32[]{:S(2)}, u32[]{:S(2)}) async-start(bf16[32,32,1024]{2,1,0:T(8,128)(2,1)} %bitcast.11), calls=%async_computation.1 | async-start | bytes 4194304 | tf_op jit(solution)/shard_map/all_to_all | solution.py:428
  71.5 1.8 fusion.order_ref
  73.6 0.9 pad_maximum_fusion
  74.4 1.2 copy.30.add_ref
  75.7 11.7 %windows.2.wide_ref = bf16[5,2048,768]{2,1,0:T(8,128)(2,1)} custom-call(bf16[1024,768]{1,0:T(8,128)(2,1)S(1)} %copy-done, bf16[32,768]{1,0:T(8,128)(2,1)S(1)} %copy-done.5, bf16[1024,768]{1,0:T(8,128)(2,1)} %copy-done.16, bf16[32,768]{1,0:T(8,128)(2,1)S(1)} %copy-done.3), custom_call_target="tpu_custom_call" | custom-call | bytes 18874368 | tf_op jit(solution)/shard_map/windows/pallas_call | solution.py:258
  87.4 5.9 %windows.3.wide_ref = bf16[5,1024,896]{2,1,0:T(8,128)(2,1)} custom-call(bf16[512,896]{1,0:T(8,128)(2,1)S(1)} %copy-done.2, bf16[32,896]{1,0:T(8,128)(2,1)S(1)} %get-tuple-element.71.rim_ref.own_rim, bf16[512,896]{1,0:T(8,128)(2,1)S(1)} %collective-permute-done.2.other_ref, bf16[32,896]{1,0:T(8,128)(2,1)S(1)} %get-tuple-element.70.other_rim), custom_call_target="tpu_custom_call" | custom-call | bytes 11010048 | tf_op jit(solution)/shard_map/windows/pallas_call | solution.py:258
  93.3 7.3 %all-to-all-done.1 = bf16[32,32,1024]{2,1,0:T(8,128)(2,1)} async-done(((bf16[32,32,1024]{2,1,0:T(8,128)(2,1)}), bf16[32,32,1024]{2,1,0:T(8,128)(2,1)}, u32[]{:S(2)}, u32[]{:S(2)}) %all-to-all-start.1) | async-done | bytes 2097184 | tf_op jit(solution)/shard_map/all_to_all | solution.py:428
  100.7 5.1 %head_back.1 = (bf16[512,1024]{1,0:T(8,128)(2,1)}, bf16[1024,512]{1,0:T(8,128)(2,1)}) custom-call(bf16[256,1024]{1,0:T(8,128)(2,1)S(1)} %copy.30.add_ref, bf16[1024,1024]{1,0:T(8,128)(2,1)} %bitcast.12.come_ref, f32[1,1024]{1,0:T(1,128)S(1)} %bitcast.25, bf16[256,1024]{1,0:T(8,128)(2,1)S(1)} %copy-done.8, bf16[256,1024]{1,0:T(8,128)(2,1)S(1)} %copy-done.10, ...), custom_call_target="tpu_custom_call" | custom-call | flops 1610612736 | bytes 8912896 | tf_op jit(solution)/shard_map/head_back/pallas_call | solution.py:224
  105.8 1.3 fusion.89
  107.2 0.8 broadcast_select_fusion.3
  109.2 1.5 fusion.1.order_ref
  110.7 10.4 %grad_parts.2 = (bf16[5,128,896]{2,1,0:T(8,128)(2,1)}, bf16[5,128,896]{2,1,0:T(8,128)(2,1)}, f32[5,256,896]{2,1,0:T(8,128)}) custom-call(bf16[512,512]{1,0:T(8,128)(2,1)S(1)} %get-tuple-element.63.mine_ref, bf16[512,512]{1,0:T(8,128)(2,1)S(1)} %collective-permute-done.6.got_ref, bf16[5,1024,896]{2,1,0:T(8,128)(2,1)} %windows.3.wide_ref), custom_call_target="tpu_custom_call" | custom-call | flops 4697620480 | bytes 17104896 | tf_op jit(solution)/shard_map/grad_parts/pallas_call | solution.py:289
  121.2 2.9 %collective-permute-start.18 = (bf16[5,128,896]{2,1,0:T(8,128)(2,1)}, bf16[5,128,896]{2,1,0:T(8,128)(2,1)S(1)}, u32[]{:S(2)}, u32[]{:S(2)}) collective-permute-start(bf16[5,128,896]{2,1,0:T(8,128)(2,1)} %get-tuple-element.39), channel_id=1, source_target_pairs={{0,24},{4,100},{8,0},{12,108},{16,8},{20,116},{24,16},{28,124},{32... | collective-permute-start | bytes 3440648 | tf_op jit(solution)/shard_map/ppermute | solution.py:45
  124.1 15.1 %conv_back.1 = bf16[896,1024]{1,0:T(8,128)(2,1)} custom-call(bf16[512,1024]{1,0:T(8,128)(2,1)} %get-tuple-element.41.g_ref, bf16[32,1024]{1,0:T(8,128)(2,1)S(1)} %pad_maximum_fusion.10.rim_ref, bf16[5,896,1024]{2,1,0:T(8,128)(2,1)} %w_hbm.5, bf16[512,896]{1,0:T(8,128)(2,1)S(1)} %copy-done.12, bf16[512,896]{1,0:T(8,128)(2,1)S(1)} %copy-done.13, ...), custom_call_target="tpu_custom_call" | custom-call | flops 6341787648 | bytes 17334272 | tf_op jit(solution)/shard_map/conv_back/pallas_call | solution.py:187
  139.2 1.7 fusion.88
  141.6 3.0 %collective-permute-start.21 = (bf16[5,64,896]{2,1,0:T(8,128)(2,1)S(1)}, bf16[5,64,896]{2,1,0:T(8,128)(2,1)S(1)}, u32[]{:S(2)}, u32[]{:S(2)}) collective-permute-start(bf16[5,64,896]{2,1,0:T(8,128)(2,1)S(1)} %add_convert_fusion), channel_id=1, source_target_pairs={{0,24},{4,100},{8,0},{12,108},{16,8},{20,116},{24,16},{28,124},{32... | collective-permute-start | bytes 1720328 | tf_op jit(solution)/shard_map/ppermute | solution.py:45
  144.6 12.1 %grad_parts.3 = (bf16[5,112,768]{2,1,0:T(8,128)(2,1)}, bf16[5,112,768]{2,1,0:T(8,128)(2,1)}, f32[5,224,768]{2,1,0:T(8,128)}) custom-call(bf16[448,1024]{1,0:T(8,128)(2,1)S(1)} %get-tuple-element.53.mine_ref, bf16[448,1024]{1,0:T(8,128)(2,1)S(1)} %collective-permute-done.9.got_ref, bf16[5,2048,768]{2,1,0:T(8,128)(2,1)} %windows.2.wide_ref), custom_call_target="tpu_custom_call" | custom-call | flops 7046430720 | bytes 22724608 | tf_op jit(solution)/shard_map/grad_parts/pallas_call | solution.py:289
  156.7 1.4 collective-permute-start.10
  158.4 0.8 collective-permute-start.20
  159.3 10.5 %collective-permute-done.10 = bf16[5,112,768]{2,1,0:T(8,128)(2,1)S(1)} collective-permute-done((bf16[5,112,768]{2,1,0:T(8,128)(2,1)}, bf16[5,112,768]{2,1,0:T(8,128)(2,1)S(1)}, u32[]{:S(2)}, u32[]{:S(2)}) %collective-permute-start.10) | collective-permute-done | bytes 860192 | tf_op jit(solution)/shard_map/ppermute | solution.py:45
  169.9 2.6 %collective-permute-start.13 = (bf16[5,56,768]{2,1,0:T(8,128)(2,1)S(1)}, bf16[5,56,768]{2,1,0:T(8,128)(2,1)S(1)}, u32[]{:S(2)}, u32[]{:S(2)}) collective-permute-start(bf16[5,56,768]{2,1,0:T(8,128)(2,1)S(1)} %add_convert_fusion.2), channel_id=1, source_target_pairs={{0,24},{4,100},{8,0},{12,108},{16,8},{20,116},{24,16},{28,124},{32... | collective-permute-start | bytes 1290248 | tf_op jit(solution)/shard_map/ppermute | solution.py:45
  172.9 1.0 collective-permute-start.22
  173.9 4.7 %collective-permute-done.11 = bf16[5,112,768]{2,1,0:T(8,128)(2,1)S(1)} collective-permute-done((bf16[5,112,768]{2,1,0:T(8,128)(2,1)S(1)}, bf16[5,112,768]{2,1,0:T(8,128)(2,1)S(1)}, u32[]{:S(2)}, u32[]{:S(2)}) %collective-permute-start.11) | collective-permute-done | bytes 860192 | tf_op jit(solution)/shard_map/ppermute | solution.py:45
  178.7 2.6 %collective-permute-done.13 = bf16[5,56,768]{2,1,0:T(8,128)(2,1)S(1)} collective-permute-done((bf16[5,56,768]{2,1,0:T(8,128)(2,1)S(1)}, bf16[5,56,768]{2,1,0:T(8,128)(2,1)S(1)}, u32[]{:S(2)}, u32[]{:S(2)}) %collective-permute-start.13) | collective-permute-done | bytes 430112 | tf_op jit(solution)/shard_map/ppermute | solution.py:45
  181.6 1.3 collective-permute-start.23
  183.0 2.1 collective-permute-start.25
  185.0 6.2 %collective-permute-done.12 = bf16[5,56,768]{2,1,0:T(8,128)(2,1)S(1)} collective-permute-done((bf16[5,56,768]{2,1,0:T(8,128)(2,1)S(1)}, bf16[5,56,768]{2,1,0:T(8,128)(2,1)S(1)}, u32[]{:S(2)}, u32[]{:S(2)}) %collective-permute-start.12) | collective-permute-done | bytes 430112 | tf_op jit(solution)/shard_map/ppermute | solution.py:45
  191.5 2.1 collective-permute-start.14
  193.7 1.1 collective-permute-start.15
  194.7 3.0 %collective-permute-done.14 = bf16[5,28,768]{2,1,0:T(8,128)(2,1)S(1)} collective-permute-done((bf16[5,28,768]{2,1,0:T(8,128)(2,1)S(1)}, bf16[5,28,768]{2,1,0:T(8,128)(2,1)S(1)}, u32[]{:S(2)}, u32[]{:S(2)}) %collective-permute-start.14) | collective-permute-done | bytes 215072 | tf_op jit(solution)/shard_map/ppermute | solution.py:45
  197.8 3.3 %collective-permute-start.17 = (bf16[3,28,768]{2,1,0:T(8,128)(2,1)S(1)}, bf16[3,28,768]{2,1,0:T(8,128)(2,1)S(1)}, u32[]{:S(2)}, u32[]{:S(2)}) collective-permute-start(bf16[3,28,768]{2,1,0:T(8,128)(2,1)S(1)} %fusion.11), channel_id=1, source_target_pairs={{0,96},{4,28},{8,104},{12,4},{16,112},{20,12},{24,120},{28,20},{32... | collective-permute-start | bytes 387080 | tf_op jit(solution)/shard_map/ppermute | solution.py:45
  201.1 1.2 collective-permute-done.15
  202.4 1.0 fusion.5
  203.5 4.8 %collective-permute-done.16 = bf16[2,28,768]{2,1,0:T(8,128)(2,1)S(1)} collective-permute-done((bf16[2,28,768]{2,1,0:T(8,128)(2,1)S(1)}, bf16[2,28,768]{2,1,0:T(8,128)(2,1)S(1)}, u32[]{:S(2)}, u32[]{:S(2)}) %collective-permute-start.16) | collective-permute-done | bytes 86048 | tf_op jit(solution)/shard_map/ppermute | solution.py:45
  208.2 1.0 fusion.9
  (116 shorter events, 11.2 us)
Async XLA Ops:
  0.6 20.2 %collective-permute-start = (bf16[1024,768]{1,0:T(8,128)(2,1)}, bf16[1024,768]{1,0:T(8,128)(2,1)S(1)}, u32[]{:S(2)}, u32[]{:S(2)}) collective-permute-start(bf16[1024,768]{1,0:T(8,128)(2,1)} %own_ref), channel_id=1, source_target_pairs={{0,4},{4,0},{8,12},{12,8},{16,20},{20,16},{24,28},{28,24},{32,36},... | collective-permute-start | bytes 4718600 | tf_op jit(solution)/shard_map/ppermute | solution.py:45
  4.7 35.0 %all-to-all-start = ((bf16[32,2,16]{2,1,0:T(2,128)(2,1)}), bf16[32,2,16]{2,1,0:T(2,128)(2,1)S(1)}, u32[]{:S(2)}, u32[]{:S(2)}) async-start(bf16[32,2,16]{2,1,0:T(2,128)(2,1)} %copy.24), calls=%async_computation | async-start | bytes 32768 | tf_op jit(solution)/shard_map/all_to_all | solution.py:386
  13.8 1.7 collective-permute-start.1
  15.5 4.6 %collective-permute-start.4 = (bf16[2,768]{1,0:T(2,128)(2,1)S(1)}, bf16[2,768]{1,0:T(2,128)(2,1)S(1)}, u32[]{:S(2)}, u32[]{:S(2)}) collective-permute-start(bf16[2,768]{1,0:T(2,128)(2,1)S(1)} %collective-permute-done.1), channel_id=1, source_target_pairs={{0,4},{4,0},{8,12},{12,8},{16,20},{20,16},{24,28},{28,24},{32,36},... | collective-permute-start | bytes 9224 | tf_op jit(solution)/shard_map/ppermute | solution.py:45
  20.9 1.2 copy-start.16
  22.0 16.3 %copy-start.4 = (bf16[32,768]{1,0:T(8,128)(2,1)}, bf16[32,768]{1,0:T(8,128)(2,1)S(1)}, u32[]{:S(2)}) copy-start(bf16[32,768]{1,0:T(8,128)(2,1)S(1)} %get-tuple-element.73.rim_ref.own_rim) | copy-start | bytes 147460
  39.3 6.6 %copy-start.1 = (bf16[512,896]{1,0:T(8,128)(2,1)}, bf16[512,896]{1,0:T(8,128)(2,1)S(1)}, u32[]{:S(2)}) copy-start(bf16[512,896]{1,0:T(8,128)(2,1)S(1)} %get-tuple-element.30.x_ref.own_ref) | copy-start | bytes 2752516
  39.3 6.5 %collective-permute-start.2 = (bf16[512,896]{1,0:T(8,128)(2,1)S(1)}, bf16[512,896]{1,0:T(8,128)(2,1)S(1)}, u32[]{:S(2)}, u32[]{:S(2)}) collective-permute-start(bf16[512,896]{1,0:T(8,128)(2,1)S(1)} %get-tuple-element.30.x_ref.own_ref), channel_id=1, source_target_pairs={{0,4},{4,0},{8,12},{12,8},{16,20},{20,16},{24,28},{28,24},{32,36},... | collective-permute-start | bytes 2752520 | tf_op jit(solution)/shard_map/ppermute | solution.py:45
  39.8 0.8 collective-permute-start.3
  40.7 5.1 %collective-permute-start.5 = (bf16[2,896]{1,0:T(2,128)(2,1)S(1)}, bf16[2,896]{1,0:T(2,128)(2,1)S(1)}, u32[]{:S(2)}, u32[]{:S(2)}) collective-permute-start(bf16[2,896]{1,0:T(2,128)(2,1)S(1)} %collective-permute-done.3), channel_id=1, source_target_pairs={{0,4},{4,0},{8,12},{12,8},{16,20},{20,16},{24,28},{28,24},{32,36},... | collective-permute-start | bytes 10760 | tf_op jit(solution)/shard_map/ppermute | solution.py:45
  57.4 2.0 copy-start.7
  57.4 2.0 copy-start.9
  59.5 11.4 %copy-start.19 = (s32[256]{0:T(256)S(1)}, s32[256]{0:T(256)}, u32[]{:S(2)}) copy-start(s32[256]{0:T(256)} %param.14) | copy-start | bytes 3076
  59.5 11.4 %copy-start.20 = (bf16[256]{0:T(256)(128)(2,1)S(1)}, bf16[256]{0:T(256)(128)(2,1)}, u32[]{:S(2)}) copy-start(bf16[256]{0:T(256)(128)(2,1)} %param.15) | copy-start | bytes 1540
  59.5 41.2 %all-to-all-start.1 = ((bf16[32,32,1024]{2,1,0:T(8,128)(2,1)}), bf16[32,32,1024]{2,1,0:T(8,128)(2,1)}, u32[]{:S(2)}, u32[]{:S(2)}) async-start(bf16[32,32,1024]{2,1,0:T(8,128)(2,1)} %bitcast.11), calls=%async_computation.1 | async-start | bytes 4194304 | tf_op jit(solution)/shard_map/all_to_all | solution.py:428
  73.3 2.4 %copy-start = (bf16[1024,768]{1,0:T(8,128)(2,1)S(1)}, bf16[1024,768]{1,0:T(8,128)(2,1)}, u32[]{:S(2)}) copy-start(bf16[1024,768]{1,0:T(8,128)(2,1)} %own_ref) | copy-start | bytes 4718596
  73.3 2.4 %copy-start.3 = (bf16[32,768]{1,0:T(8,128)(2,1)S(1)}, bf16[32,768]{1,0:T(8,128)(2,1)}, u32[]{:S(2)}) copy-start(bf16[32,768]{1,0:T(8,128)(2,1)} %get-tuple-element.72.other_rim) | copy-start | bytes 147460
  73.3 2.4 %copy-start.5 = (bf16[32,768]{1,0:T(8,128)(2,1)S(1)}, bf16[32,768]{1,0:T(8,128)(2,1)}, u32[]{:S(2)}) copy-start(bf16[32,768]{1,0:T(8,128)(2,1)} %copy-done.4) | copy-start | bytes 147460
  75.7 11.7 %copy-start.2 = (bf16[512,896]{1,0:T(8,128)(2,1)S(1)}, bf16[512,896]{1,0:T(8,128)(2,1)}, u32[]{:S(2)}) copy-start(bf16[512,896]{1,0:T(8,128)(2,1)} %copy-done.1) | copy-start | bytes 2752516
  87.4 13.3 %copy-start.6 = (f32[1024]{0:T(1024)S(1)}, f32[1024]{0:T(1024)}, u32[]{:S(2)}) copy-start(f32[1024]{0:T(1024)} %param.11) | copy-start | bytes 12292
  87.4 13.3 %copy-start.8 = (bf16[256,1024]{1,0:T(8,128)(2,1)S(1)}, bf16[256,1024]{1,0:T(8,128)(2,1)}, u32[]{:S(2)}) copy-start(bf16[256,1024]{1,0:T(8,128)(2,1)} %copy-done.7) | copy-start | bytes 1572868
  87.4 13.3 %copy-start.10 = (bf16[256,1024]{1,0:T(8,128)(2,1)S(1)}, bf16[256,1024]{1,0:T(8,128)(2,1)}, u32[]{:S(2)}) copy-start(bf16[256,1024]{1,0:T(8,128)(2,1)} %copy-done.9) | copy-start | bytes 1572868
  107.1 3.6 %collective-permute-start.6 = (bf16[512,512]{1,0:T(8,128)(2,1)S(1)}, bf16[512,512]{1,0:T(8,128)(2,1)S(1)}, u32[]{:S(2)}, u32[]{:S(2)}) collective-permute-start(bf16[512,512]{1,0:T(8,128)(2,1)S(1)} %get-tuple-element.62), channel_id=1, source_target_pairs={{0,4},{4,0},{8,12},{12,8},{16,20},{20,16},{24,28},{28,24},{32,36},... | collective-permute-start | bytes 1572872 | tf_op jit(solution)/shard_map/ppermute | solution.py:45
  107.9 2.7 %collective-permute-start.7 = (bf16[2,1024]{1,0:T(2,128)(2,1)S(1)}, bf16[2,1024]{1,0:T(2,128)(2,1)S(1)}, u32[]{:S(2)}, u32[]{:S(2)}) collective-permute-start(bf16[2,1024]{1,0:T(2,128)(2,1)S(1)} %get-tuple-element.60), channel_id=1, source_target_pairs={{0,4},{4,0},{8,12},{12,8},{16,20},{20,16},{24,28},{28,24},{32,36},... | collective-permute-start | bytes 12296 | tf_op jit(solution)/shard_map/ppermute | solution.py:45
  108.5 2.1 %collective-permute-start.8 = (bf16[2,1024]{1,0:T(2,128)(2,1)S(1)}, bf16[2,1024]{1,0:T(2,128)(2,1)S(1)}, u32[]{:S(2)}, u32[]{:S(2)}) collective-permute-start(bf16[2,1024]{1,0:T(2,128)(2,1)S(1)} %get-tuple-element.61), channel_id=1, source_target_pairs={{8,4},{16,12},{24,20},{32,28},{40,36},{48,44},{56,52},{64,60},{72,... | collective-permute-start | bytes 12296 | tf_op jit(solution)/shard_map/ppermute | solution.py:45
  110.7 13.4 %copy-start.12 = (bf16[512,896]{1,0:T(8,128)(2,1)S(1)}, bf16[512,896]{1,0:T(8,128)(2,1)}, u32[]{:S(2)}) copy-start(bf16[512,896]{1,0:T(8,128)(2,1)} %copy-done.11) | copy-start | bytes 2752516
  110.7 13.4 %copy-start.13 = (bf16[512,896]{1,0:T(8,128)(2,1)S(1)}, bf16[512,896]{1,0:T(8,128)(2,1)}, u32[]{:S(2)}) copy-start(bf16[512,896]{1,0:T(8,128)(2,1)} %get-tuple-element.43.odd_ref) | copy-start | bytes 2752516
  121.2 20.3 %collective-permute-start.18 = (bf16[5,128,896]{2,1,0:T(8,128)(2,1)}, bf16[5,128,896]{2,1,0:T(8,128)(2,1)S(1)}, u32[]{:S(2)}, u32[]{:S(2)}) collective-permute-start(bf16[5,128,896]{2,1,0:T(8,128)(2,1)} %get-tuple-element.39), channel_id=1, source_target_pairs={{0,24},{4,100},{8,0},{12,108},{16,8},{20,116},{24,16},{28,124},{32... | collective-permute-start | bytes 3440648 | tf_op jit(solution)/shard_map/ppermute | solution.py:45
  124.1 17.4 %copy-start.14 = (f32[5,256,896]{2,1,0:T(8,128)S(1)}, f32[5,256,896]{2,1,0:T(8,128)}, u32[]{:S(2)}) copy-start(f32[5,256,896]{2,1,0:T(8,128)} %get-tuple-element.40) | copy-start | bytes 13762564
  139.2 1.8 copy-start.17
  140.9 3.6 %collective-permute-start.9 = (bf16[448,1024]{1,0:T(8,128)(2,1)S(1)}, bf16[448,1024]{1,0:T(8,128)(2,1)S(1)}, u32[]{:S(2)}, u32[]{:S(2)}) collective-permute-start(bf16[448,1024]{1,0:T(8,128)(2,1)S(1)} %get-tuple-element.52), channel_id=1, source_target_pairs={{0,4},{4,0},{8,12},{12,8},{16,20},{20,16},{24,28},{28,24},{32,36},... | collective-permute-start | bytes 2752520 | tf_op jit(solution)/shard_map/ppermute | solution.py:45
  141.0 17.1 %collective-permute-start.19 = (bf16[5,128,896]{2,1,0:T(8,128)(2,1)S(1)}, bf16[5,128,896]{2,1,0:T(8,128)(2,1)S(1)}, u32[]{:S(2)}, u32[]{:S(2)}) collective-permute-start(bf16[5,128,896]{2,1,0:T(8,128)(2,1)S(1)} %copy-done.17), channel_id=1, source_target_pairs={{0,8},{4,36},{8,16},{12,44},{16,24},{20,52},{24,0},{28,60},{32,40}... | collective-permute-start | bytes 3440648 | tf_op jit(solution)/shard_map/ppermute | solution.py:45
  141.6 16.6 %collective-permute-start.21 = (bf16[5,64,896]{2,1,0:T(8,128)(2,1)S(1)}, bf16[5,64,896]{2,1,0:T(8,128)(2,1)S(1)}, u32[]{:S(2)}, u32[]{:S(2)}) collective-permute-start(bf16[5,64,896]{2,1,0:T(8,128)(2,1)S(1)} %add_convert_fusion), channel_id=1, source_target_pairs={{0,24},{4,100},{8,0},{12,108},{16,8},{20,116},{24,16},{28,124},{32... | collective-permute-start | bytes 1720328 | tf_op jit(solution)/shard_map/ppermute | solution.py:45
  156.7 2.5 %copy-start.18 = (bf16[5,112,768]{2,1,0:T(8,128)(2,1)S(1)}, bf16[5,112,768]{2,1,0:T(8,128)(2,1)}, u32[]{:S(2)}) copy-start(bf16[5,112,768]{2,1,0:T(8,128)(2,1)} %get-tuple-element.47) | copy-start | bytes 2580484
  156.7 13.1 %copy-start.15 = (f32[5,224,768]{2,1,0:T(8,128)S(1)}, f32[5,224,768]{2,1,0:T(8,128)}, u32[]{:S(2)}) copy-start(f32[5,224,768]{2,1,0:T(8,128)} %get-tuple-element.45) | copy-start | bytes 10321924
  156.7 13.1 %collective-permute-start.10 = (bf16[5,112,768]{2,1,0:T(8,128)(2,1)}, bf16[5,112,768]{2,1,0:T(8,128)(2,1)S(1)}, u32[]{:S(2)}, u32[]{:S(2)}) collective-permute-start(bf16[5,112,768]{2,1,0:T(8,128)(2,1)} %get-tuple-element.46), channel_id=1, source_target_pairs={{0,24},{4,100},{8,0},{12,108},{16,8},{20,116},{24,16},{28,124},{32... | collective-permute-start | bytes 2580488 | tf_op jit(solution)/shard_map/ppermute | solution.py:45
  158.4 14.1 %collective-permute-start.20 = (bf16[5,64,896]{2,1,0:T(8,128)(2,1)S(1)}, bf16[5,64,896]{2,1,0:T(8,128)(2,1)S(1)}, u32[]{:S(2)}, u32[]{:S(2)}) collective-permute-start(bf16[5,64,896]{2,1,0:T(8,128)(2,1)S(1)} %get-tuple-element.49), channel_id=1, source_target_pairs={{0,8},{4,36},{8,16},{12,44},{16,24},{20,52},{24,0},{28,60},{32,40}... | collective-permute-start | bytes 1720328 | tf_op jit(solution)/shard_map/ppermute | solution.py:45
  159.2 19.4 %collective-permute-start.11 = (bf16[5,112,768]{2,1,0:T(8,128)(2,1)S(1)}, bf16[5,112,768]{2,1,0:T(8,128)(2,1)S(1)}, u32[]{:S(2)}, u32[]{:S(2)}) collective-permute-start(bf16[5,112,768]{2,1,0:T(8,128)(2,1)S(1)} %copy-done.18), channel_id=1, source_target_pairs={{0,8},{4,36},{8,16},{12,44},{16,24},{20,52},{24,0},{28,60},{32,40}... | collective-permute-start | bytes 2580488 | tf_op jit(solution)/shard_map/ppermute | solution.py:45
  169.9 11.3 %collective-permute-start.13 = (bf16[5,56,768]{2,1,0:T(8,128)(2,1)S(1)}, bf16[5,56,768]{2,1,0:T(8,128)(2,1)S(1)}, u32[]{:S(2)}, u32[]{:S(2)}) collective-permute-start(bf16[5,56,768]{2,1,0:T(8,128)(2,1)S(1)} %add_convert_fusion.2), channel_id=1, source_target_pairs={{0,24},{4,100},{8,0},{12,108},{16,8},{20,116},{24,16},{28,124},{32... | collective-permute-start | bytes 1290248 | tf_op jit(solution)/shard_map/ppermute | solution.py:45
  172.9 10.0 %collective-permute-start.22 = (bf16[5,32,896]{2,1,0:T(8,128)(2,1)S(1)}, bf16[5,32,896]{2,1,0:T(8,128)(2,1)S(1)}, u32[]{:S(2)}, u32[]{:S(2)}) collective-permute-start(bf16[5,32,896]{2,1,0:T(8,128)(2,1)S(1)} %get-tuple-element.59), channel_id=1, source_target_pairs={{0,96},{4,28},{8,104},{12,4},{16,112},{20,12},{24,120},{28,20},{32... | collective-permute-start | bytes 860168 | tf_op jit(solution)/shard_map/ppermute | solution.py:45
  181.5 9.7 %collective-permute-start.12 = (bf16[5,56,768]{2,1,0:T(8,128)(2,1)S(1)}, bf16[5,56,768]{2,1,0:T(8,128)(2,1)S(1)}, u32[]{:S(2)}, u32[]{:S(2)}) collective-permute-start(bf16[5,56,768]{2,1,0:T(8,128)(2,1)S(1)} %get-tuple-element.51), channel_id=1, source_target_pairs={{0,8},{4,36},{8,16},{12,44},{16,24},{20,52},{24,0},{28,60},{32,40}... | collective-permute-start | bytes 1290248 | tf_op jit(solution)/shard_map/ppermute | solution.py:45
  181.6 12.0 %collective-permute-start.23 = (bf16[5,32,896]{2,1,0:T(8,128)(2,1)S(1)}, bf16[5,32,896]{2,1,0:T(8,128)(2,1)S(1)}, u32[]{:S(2)}, u32[]{:S(2)}) collective-permute-start(bf16[5,32,896]{2,1,0:T(8,128)(2,1)S(1)} %get-tuple-element.58), channel_id=1, source_target_pairs={{0,32},{4,12},{8,40},{12,20},{16,48},{20,28},{24,56},{28,4},{32,64... | collective-permute-start | bytes 860168 | tf_op jit(solution)/shard_map/ppermute | solution.py:45
  183.0 19.5 %collective-permute-start.25 = (bf16[3,32,896]{2,1,0:T(8,128)(2,1)S(1)}, bf16[3,32,896]{2,1,0:T(8,128)(2,1)S(1)}, u32[]{:S(2)}, u32[]{:S(2)}) collective-permute-start(bf16[3,32,896]{2,1,0:T(8,128)(2,1)S(1)} %fusion.10), channel_id=1, source_target_pairs={{0,96},{4,28},{8,104},{12,4},{16,112},{20,12},{24,120},{28,20},{32... | collective-permute-start | bytes 516104 | tf_op jit(solution)/shard_map/ppermute | solution.py:45
  191.5 6.3 %collective-permute-start.14 = (bf16[5,28,768]{2,1,0:T(8,128)(2,1)S(1)}, bf16[5,28,768]{2,1,0:T(8,128)(2,1)S(1)}, u32[]{:S(2)}, u32[]{:S(2)}) collective-permute-start(bf16[5,28,768]{2,1,0:T(8,128)(2,1)S(1)} %get-tuple-element.69), channel_id=1, source_target_pairs={{0,96},{4,28},{8,104},{12,4},{16,112},{20,12},{24,120},{28,20},{32... | collective-permute-start | bytes 645128 | tf_op jit(solution)/shard_map/ppermute | solution.py:45
  193.6 8.8 %collective-permute-start.24 = (bf16[2,32,896]{2,1,0:T(8,128)(2,1)S(1)}, bf16[2,32,896]{2,1,0:T(8,128)(2,1)S(1)}, u32[]{:S(2)}, u32[]{:S(2)}) collective-permute-start(bf16[2,32,896]{2,1,0:T(8,128)(2,1)S(1)} %fusion.17), channel_id=1, source_target_pairs={{0,32},{4,12},{8,40},{12,20},{16,48},{20,28},{24,56},{28,4},{32,64... | collective-permute-start | bytes 344072 | tf_op jit(solution)/shard_map/ppermute | solution.py:45
  193.7 8.6 %collective-permute-start.15 = (bf16[5,28,768]{2,1,0:T(8,128)(2,1)S(1)}, bf16[5,28,768]{2,1,0:T(8,128)(2,1)S(1)}, u32[]{:S(2)}, u32[]{:S(2)}) collective-permute-start(bf16[5,28,768]{2,1,0:T(8,128)(2,1)S(1)} %get-tuple-element.68), channel_id=1, source_target_pairs={{0,32},{4,12},{8,40},{12,20},{16,48},{20,28},{24,56},{28,4},{32,64... | collective-permute-start | bytes 645128 | tf_op jit(solution)/shard_map/ppermute | solution.py:45
  197.8 10.4 %collective-permute-start.17 = (bf16[3,28,768]{2,1,0:T(8,128)(2,1)S(1)}, bf16[3,28,768]{2,1,0:T(8,128)(2,1)S(1)}, u32[]{:S(2)}, u32[]{:S(2)}) collective-permute-start(bf16[3,28,768]{2,1,0:T(8,128)(2,1)S(1)} %fusion.11), channel_id=1, source_target_pairs={{0,96},{4,28},{8,104},{12,4},{16,112},{20,12},{24,120},{28,20},{32... | collective-permute-start | bytes 387080 | tf_op jit(solution)/shard_map/ppermute | solution.py:45
  202.3 5.9 %collective-permute-start.16 = (bf16[2,28,768]{2,1,0:T(8,128)(2,1)S(1)}, bf16[2,28,768]{2,1,0:T(8,128)(2,1)S(1)}, u32[]{:S(2)}, u32[]{:S(2)}) collective-permute-start(bf16[2,28,768]{2,1,0:T(8,128)(2,1)S(1)} %fusion.18), channel_id=1, source_target_pairs={{0,32},{4,12},{8,40},{12,20},{16,48},{20,28},{24,56},{28,4},{32,64... | collective-permute-start | bytes 258056 | tf_op jit(solution)/shard_map/ppermute | solution.py:45
  (1 other events, 0.9 us)
where the time goes:
time: 210 us; the launch traced here: 209 us
  Pallas kernels  88.2 us (42%)
  starting transfers between devices  53.1 us (25%)
  waiting for transfers between devices  41.8 us (20%)
  other arithmetic  13.6 us (6%)
  local copies, waits for them, and re-layouts  7.51 us (4%)
  matrix products  3.65 us (2%)
    ppermute x26, waiting for transfers between devices, move(): return lax.ppermute(value, 'seq', pairs)  34.5 us
    ppermute x26, starting transfers between devices, move(): return lax.ppermute(value, 'seq', pairs)  33.4 us
    pallas_call x2, Pallas kernels, conv_pool(): pl.pallas_call(functools.partial(conv_kernel, taps), out_shape=[jax.Shape...  27.9 us
    pallas_call x2, Pallas kernels, grad_parts(): pl.pallas_call(grad_kernel, grid=(taps,), out_shape=[pltpu.HBM((taps, m /...  22.5 us
    pallas_call x2, Pallas kernels, windows_of(): pl.pallas_call(functools.partial(window_kernel, taps), grid=(2 * n // PIE...  17.6 us
    pallas_call x1, Pallas kernels, conv_back(): pl.pallas_call(functools.partial(back_kernel, taps), out_shape=jax.ShapeD...  15.1 us
    all_to_all x1, starting transfers between devices, body(): come = lax.all_to_all(gone, 'seq', split_axis=0, concat_axis=0, tiled=True)  11.3 us
    all_to_all x1, starting transfers between devices, body(): heard = lax.all_to_all(sent, 'seq', split_axis=0, concat_axis=0, tiled=True)  8.37 us
  transfers between devices with their start and end apart: 28, of which 10 were waited for; matrix products, arithmetic and copies ran while one was open for 9% of the time, Pallas kernels for 29%

commit v1 on v0

--- a/solution.py
+++ b/solution.py
@@ -54,7 +54,7 @@
 RIM = 16
 
 
-def params(mib=52):
+def params(mib=44):
     return pltpu.CompilerParams(vmem_limit_bytes=mib << 20)
 
 
@@ -113,8 +113,8 @@
             even, even_slope = gelu_both(acc[j, pl.ds(0, TILE // 2, stride=2), :])
             odd, odd_slope = gelu_both(acc[j, pl.ds(1, TILE // 2, stride=2), :])
             pooled_ref[q, cols] = ((even + odd) * 0.5).astype(BF)
-            even_ref[q, cols] = (even_slope * 0.5).astype(BF)
-            odd_ref[q, cols] = (odd_slope * 0.5).astype(BF)
+            even_ref[q, cols] = even_slope * 0.5
+            odd_ref[q, cols] = odd_slope * 0.5
 
 
 def conv_pool(x, rim, w):
@@ -123,7 +123,7 @@
     return pl.pallas_call(
         functools.partial(conv_kernel, taps),
         out_shape=[jax.ShapeDtypeStruct((n // 2, c), BF)]
-        + [jax.ShapeDtypeStruct((n // 2, c), BF)] * 2,
+        + [jax.ShapeDtypeStruct((n // 2, c), F32)] * 2,
         in_specs=[IN_VMEM, IN_VMEM, IN_PLACE],
         out_specs=[IN_VMEM] * 3,
         scratch_shapes=[
@@ -141,7 +141,7 @@
 
 
 def back_kernel(
-    taps, g_ref, rim_ref, w_hbm, even_ref, odd_ref, order_ref, out_ref, w_ref, rimmed, piece, wide, pairs, flat, sem
+    taps, g_ref, rim_ref, w_hbm, even_ref, odd_ref, order_ref, mine_ref, theirs_ref, w_ref, rimmed, piece, wide, pairs, flat, sem
 ):
     n = g_ref.shape[0]
     copies = [pltpu.make_async_copy(w_hbm.at[k], w_ref.at[k], sem.at[k]) for k in range(taps)]
@@ -178,7 +178,10 @@
         turned = lax.dot_general(
             order_ref[...], flat[...], (((1,), (1,)), ((), ())), preferred_element_type=F32
         )
-        out_ref[:, pl.ds(pl.multiple_of(2 * r, 2 * TILE), 2 * TILE)] = turned.astype(BF)
+        half = mine_ref.shape[0]
+        cols = pl.ds(pl.multiple_of(2 * r, 2 * TILE), 2 * TILE)
+        mine_ref[:, cols] = turned[:half].astype(BF)
+        theirs_ref[:, cols] = turned[half:].astype(BF)
 
 
 def conv_back(g, rim, w, even, odd, order):
@@ -186,9 +189,9 @@
     n = g.shape[0]
     return pl.pallas_call(
         functools.partial(back_kernel, taps),
-        out_shape=jax.ShapeDtypeStruct((f, 2 * n), BF),
+        out_shape=[jax.ShapeDtypeStruct((f // 2, 2 * n), BF)] * 2,
         in_specs=[IN_VMEM, IN_VMEM, IN_PLACE, IN_VMEM, IN_VMEM, IN_VMEM],
-        out_specs=IN_VMEM,
+        out_specs=[IN_VMEM] * 2,
         scratch_shapes=[
             VM((taps, f, c), BF),
             VM((n + 2 * RIM, c), BF),
@@ -206,7 +209,7 @@
     )(g, rim, w, even, odd, order)
 
 
-def head_kernel(add_ref, come_ref, head_ref, even_ref, odd_ref, order_ref, g_ref, turned_ref, pairs):
+def head_kernel(add_ref, come_ref, head_ref, even_ref, odd_ref, order_ref, g_ref, mine_ref, theirs_ref, pairs):
     n = add_ref.shape[0]
     total = jnp.dot(add_ref[...], come_ref[...], preferred_element_type=F32) * head_ref[...]
     for j in range(pairs.shape[0]):
@@ -214,18 +217,22 @@
         pairs[j, pl.ds(0, n, stride=2), :] = total[:, cols] * even_ref[:, cols]
         pairs[j, pl.ds(1, n, stride=2), :] = total[:, cols] * odd_ref[:, cols]
         g_ref[:, cols] = pairs[j].astype(BF)
-    turned_ref[...] = lax.dot_general(
+    turned = lax.dot_general(
         order_ref[...], g_ref[...], (((1,), (1,)), ((), ())), preferred_element_type=F32
-    ).astype(BF)
+    )
+    half = mine_ref.shape[0]
+    mine_ref[...] = turned[:half].astype(BF)
+    theirs_ref[...] = turned[half:].astype(BF)
 
 
 def head_back(add, come, head, even, odd, order):
     n, c = even.shape
     return pl.pallas_call(
         head_kernel,
-        out_shape=[jax.ShapeDtypeStruct((2 * n, c), BF), jax.ShapeDtypeStruct((c, 2 * n), BF)],
+        out_shape=[jax.ShapeDtypeStruct((2 * n, c), BF)]
+        + [jax.ShapeDtypeStruct((c // 2, 2 * n), BF)] * 2,
         in_specs=[IN_VMEM] * 6,
-        out_specs=[IN_VMEM] * 2,
+        out_specs=[IN_VMEM] * 3,
         scratch_shapes=[VM((c // LANES, 2 * n, LANES), F32)],
         compiler_params=params(),
         cost_estimate=cost(
@@ -302,7 +309,7 @@
             4 * m * n * f * taps, 2 * (2 * m * n + 2 * taps * n * f) + 3 * taps * m * f
         ),
         name="grad_parts",
-    )(mine, got, wide)
+    )(mine, got, pltpu.with_memory_space_constraint(wide, pltpu.HBM))
 
 
 def outer_rim(block, odd):
@@ -339,8 +346,14 @@
     wide = lambda v: v.astype(F32)
     got_p = move(plus, RINGS[0][0])
     got_m = move(minus, RINGS[0][1])
-    late_p = move((keep[:, :u] + wide(got_p[:, :u])).astype(BF), RINGS[0][0])
-    late_m = move((keep[:, u : 2 * u] + wide(got_m[:, :u])).astype(BF), RINGS[0][1])
+    on_p, on_m = lax.optimization_barrier(
+        (
+            (keep[:, :u] + wide(got_p[:, :u])).astype(BF),
+            (keep[:, u : 2 * u] + wide(got_m[:, :u])).astype(BF),
+        )
+    )
+    late_p = move(on_p, RINGS[0][0])
+    late_m = move(on_m, RINGS[0][1])
     low = keep[:, 2 * u : 3 * u] + wide(got_m[:, u:]) + wide(late_p)
     high = keep[:, 3 * u :] + wide(got_p[:, u:]) + wide(late_m)
     b = u // 2
@@ -348,10 +361,17 @@
     cut = keep.shape[0] // 2
     early = lax.broadcasted_iota(jnp.int32, near.shape, 0) < cut
     join = lambda first, last: jnp.where(early, first, last)
-    got_p = move(join(two, one).astype(BF), RINGS[1][0])
-    got_m = move(join(three, two).astype(BF), RINGS[1][1])
-    late_p = move((one[:cut] + wide(got_p[:cut])).astype(BF), RINGS[1][0])
-    late_m = move((three[cut:] + wide(got_m[cut:])).astype(BF), RINGS[1][1])
+    on_p, on_m = lax.optimization_barrier(
+        (join(two, one).astype(BF), join(three, two).astype(BF))
+    )
+    got_p, got_m = move(on_p, RINGS[1][0]), move(on_m, RINGS[1][1])
+    on_p, on_m = lax.optimization_barrier(
+        (
+            (one[:cut] + wide(got_p[:cut])).astype(BF),
+            (three[cut:] + wide(got_m[cut:])).astype(BF),
+        )
+    )
+    late_p, late_m = move(on_p, RINGS[1][0]), move(on_m, RINGS[1][1])
     return (
         near
         + wide(join(got_m, got_p))
@@ -400,13 +420,6 @@
     pool_other = move(pooled, SIBLING)
     pool_rim = rim_of(odd, jnp.where(odd, pool_other[-2:], pool_other[:2]), pool_outer)
     embed, even_two, odd_two = conv_pool(pooled, pool_rim, conv_two)
-    feat_other_rim = rim_of(
-        ~odd, jnp.where(odd, features[:2], features[-2:]), move(feat_outer, SIBLING)
-    )
-    pool_other_rim = rim_of(
-        ~odd, jnp.where(odd, pooled[:2], pooled[-2:]), move(pool_outer, SIBLING)
-    )
-
     heard = lax.optimization_barrier((heard, pooled))[0]
     heard = heard.transpose(1, 0, 2).reshape(2, slots)
     donor_hit = heard[0:1].astype(F32) == lax.broadcasted_iota(
@@ -426,23 +439,27 @@
         pick, embed, (((0,), (0,)), ((), ())), preferred_element_type=F32
     ).astype(BF)
     come = lax.all_to_all(gone, "seq", split_axis=0, concat_axis=0, tiled=True)
-    own, feat_other = lax.optimization_barrier((features, feat_other, gone))[:2]
-    wide_one = windows_of(own, feat_rim, feat_other, feat_other_rim, taps)
-    own, pool_other = lax.optimization_barrier((pooled, pool_other, gone))[:2]
-    wide_two = windows_of(own, pool_rim, pool_other, pool_other_rim, taps)
-
-    come, wide_one, wide_two = lax.optimization_barrier((come, wide_one, wide_two))
-    grads, turned_two = head_back(add, come, head_vector[None, :], even_two, odd_two, order_two)
+    own, feat_other, outer, pool, pool_other, outer_two, _ = lax.optimization_barrier(
+        (features, feat_other, feat_outer, pooled, pool_other, pool_outer, gone)
+    )
+    rim = rim_of(~odd, jnp.where(odd, own[:2], own[-2:]), move(outer, SIBLING))
+    wide_one = windows_of(own, feat_rim, feat_other, rim, taps)
+    rim = rim_of(~odd, jnp.where(odd, pool[:2], pool[-2:]), move(outer_two, SIBLING))
+    wide_two = windows_of(pool, pool_rim, pool_other, rim, taps)
+    come, wide_one, wide_two, order_one, order_two, add = lax.optimization_barrier(
+        (come, wide_one, wide_two, order_one, order_two, add)
+    )
+    grads, mine_two, theirs_two = head_back(add, come, head_vector[None, :], even_two, odd_two, order_two)
     grad_rim = rim_of(
         odd, move(jnp.where(odd, grads[:2], grads[-2:]), SIBLING), outer_rim(grads, odd)
     )
-    half = turned_two.shape[0] // 2
-    parts_two = grad_parts(turned_two[:half], move(turned_two[half:], SIBLING), wide_two)
+    parts_two = grad_parts(mine_two, move(theirs_two, SIBLING), wide_two)
     grads = lax.optimization_barrier((grads, parts_two))[0]
-    turned_one = conv_back(grads, grad_rim, conv_two, even_one, odd_one, order_one)
-    half = turned_one.shape[0] // 2
-    got = move(turned_one[half:], SIBLING)
-    parts_one = grad_parts(turned_one[:half], got, wide_one)
+    mine_one, theirs_one = conv_back(
+        grads, grad_rim, conv_two, even_one, odd_one, order_one
+    )
+    got = move(theirs_one, SIBLING)
+    parts_one = grad_parts(mine_one, got, wide_one)
     grad_two = ring_sums(*parts_two).transpose(1, 0, 2)
     grad_one = ring_sums(*parts_one).transpose(1, 0, 2)
     return (grad_one, grad_two)

time: 210 us -> 201 us (0.957)
  Pallas kernels: 88.2 us -> 76.6 us
  local copies, waits for them, and re-layouts: 7.51 us -> 15.4 us
  waiting for transfers between devices: 41.8 us -> 37.6 us
    unnamed x42 -> x44, local copies, waits for them, and re-layouts: 1.39 us -> 11.3 us
    all_to_all x1, waiting for transfers between devices: 7.34 us -> 3.07 us  [body(): come = lax.all_to_all(gone, 'seq', split_axis=0, concat_axis=0, tiled=True)]
    pallas_call x2, Pallas kernels: 27.9 us -> 24.4 us  [conv_pool(): pl.pallas_call(functools.partial(conv_kernel, taps), out_shape=[jax.Shape...]
    pallas_call x1, Pallas kernels: 15.1 us -> 11.8 us  [conv_back(): pl.pallas_call(functools.partial(back_kernel, taps), out_shape=[jax.Shape...]
    pallas_call x1, Pallas kernels: 5.12 us -> 1.89 us  [head_back(): pl.pallas_call(head_kernel, out_shape=[jax.ShapeDtypeStruct((2 * n, c), B...]
    slice x2 -> x0, local copies, waits for them, and re-layouts: 2.96 us -> none  [the longest x1 1.69 us: body(): got = move(turned_one[half:], SIBLING)]
    ppermute x26, starting transfers between devices: 33.4 us -> 30.7 us  [move(): return lax.ppermute(value, 'seq', pairs)]
    all_to_all x1, starting transfers between devices: 11.3 us -> 13.8 us  [body(): come = lax.all_to_all(gone, 'seq', split_axis=0, concat_axis=0, tiled=True)]
  transfers between devices with their start and end apart: 28 -> 28, of which waited for: 10 -> 11; matrix products, arithmetic and copies ran while one was open for 9% -> 8% of each run, Pallas kernels for 29% -> 27%
where the time goes in v1:
time: 201 us; the launch traced here: 200 us
  Pallas kernels  76.6 us (38%)
  starting transfers between devices  52.8 us (26%)
  waiting for transfers between devices  37.6 us (19%)
  local copies, waits for them, and re-layouts  15.4 us (8%)
  other arithmetic  12.2 us (6%)
  matrix products  4.39 us (2%)
    ppermute x26, waiting for transfers between devices, move(): return lax.ppermute(value, 'seq', pairs)  34.5 us
    ppermute x26, starting transfers between devices, move(): return lax.ppermute(value, 'seq', pairs)  30.7 us
    pallas_call x2, Pallas kernels, conv_pool(): pl.pallas_call(functools.partial(conv_kernel, taps), out_shape=[jax.Shape...  24.4 us
    pallas_call x2, Pallas kernels, grad_parts(): pl.pallas_call(grad_kernel, grid=(taps,), out_shape=[pltpu.HBM((taps, m /...  22.5 us
    pallas_call x2, Pallas kernels, windows_of(): pl.pallas_call(functools.partial(window_kernel, taps), grid=(2 * n // PIE...  16 us
    all_to_all x1, starting transfers between devices, body(): come = lax.all_to_all(gone, 'seq', split_axis=0, concat_axis=0, tiled=True)  13.8 us
    pallas_call x1, Pallas kernels, conv_back(): pl.pallas_call(functools.partial(back_kernel, taps), out_shape=[jax.Shape...  11.8 us
    unnamed x44, local copies, waits for them, and re-layouts  11.3 us
  transfers between devices with their start and end apart: 28, of which 11 were waited for; matrix products, arithmetic and copies ran while one was open for 8% of the time, Pallas kernels for 27%

profile of v1, /device:TPU:0, one launch (start us, length us, event | category | flops | bytes accessed | tf_op | source)
XLA Modules:
  0.0 200.3 jit_solution(486564661193370872)
XLA Ops:
  2.1 0.9 convert_reduce_fusion
  4.7 8.4 %all-to-all-start = ((bf16[32,2,16]{2,1,0:T(2,128)(2,1)}), bf16[32,2,16]{2,1,0:T(2,128)(2,1)S(1)}, u32[]{:S(2)}, u32[]{:S(2)}) async-start(bf16[32,2,16]{2,1,0:T(2,128)(2,1)} %copy.25), calls=%async_computation | async-start | bytes 32768 | tf_op jit(solution)/shard_map/all_to_all | solution.py:406
  14.5 1.0 convolution_convert_fusion.2
  15.6 1.9 copy-done.2
  17.5 13.8 %conv_pool.2 = (bf16[512,896]{1,0:T(8,128)(2,1)S(1)}, f32[512,896]{1,0:T(8,128)S(1)}, f32[512,896]{1,0:T(8,128)S(1)}) custom-call(bf16[1024,768]{1,0:T(8,128)(2,1)S(1)} %copy-done.2, bf16[32,768]{1,0:T(8,128)(2,1)S(1)} %pad_maximum_fusion.7.rim_ref.own_rim, bf16[5,768,896]{2,1,0:T(8,128)(2,1)} %w_hbm.3), custom_call_target="tpu_custom_call" | custom-call | flops 7046430720 | bytes 13041664 | tf_op jit(solution)/shard_map/conv_pool/pallas_call | solution.py:123
  31.4 1.2 copy-done.13
  32.6 1.3 copy-done.15
  33.9 3.8 %collective-permute-start.2 = (bf16[512,896]{1,0:T(8,128)(2,1)S(1)}, bf16[512,896]{1,0:T(8,128)(2,1)S(1)}, u32[]{:S(2)}, u32[]{:S(2)}) collective-permute-start(bf16[512,896]{1,0:T(8,128)(2,1)S(1)} %get-tuple-element.51.x_ref.own_ref), channel_id=1, source_target_pairs={{0,4},{4,0},{8,12},{12,8},{16,20},{20,16},{24,28},{28,24},{32,36},... | collective-permute-start | bytes 2752520 | tf_op jit(solution)/shard_map/ppermute | solution.py:45
  39.8 10.5 %conv_pool.3 = (bf16[256,1024]{1,0:T(8,128)(2,1)S(1)}, f32[256,1024]{1,0:T(8,128)S(1)}, f32[256,1024]{1,0:T(8,128)S(1)}) custom-call(bf16[512,896]{1,0:T(8,128)(2,1)S(1)} %get-tuple-element.51.x_ref.own_ref, bf16[32,896]{1,0:T(8,128)(2,1)S(1)} %pad_maximum_fusion.3.rim_ref.own_rim, bf16[5,896,1024]{2,1,0:T(8,128)(2,1)} %w_hbm.5), custom_call_target="tpu_custom_call" | custom-call | flops 4697620480 | bytes 12713984 | tf_op jit(solution)/shard_map/conv_pool/pallas_call | solution.py:123
  50.4 2.0 %convolution_convert_fusion = bf16[1024,1024]{1,0:T(8,128)(2,1)} fusion(bf16[256,1024]{0,1:T(8,128)(2,1)S(1)} %bitcast.31, bf16[256,1024]{1,0:T(8,128)(2,1)S(1)} %get-tuple-element.47), kind=kOutput, calls=%fused_computation.4 | convolution fusion | flops 537919488 | bytes 3145728 | tf_op jit(solution)/shard_map/dot_general | solution.py:438
  52.5 13.8 %all-to-all-start.1 = ((bf16[32,32,1024]{2,1,0:T(8,128)(2,1)}), bf16[32,32,1024]{2,1,0:T(8,128)(2,1)S(1)}, u32[]{:S(2)}, u32[]{:S(2)}) async-start(bf16[32,32,1024]{2,1,0:T(8,128)(2,1)} %bitcast.27), calls=%async_computation.1 | async-start | bytes 4194304 | tf_op jit(solution)/shard_map/all_to_all | solution.py:441
  66.3 1.1 convolution_convert_fusion.1
  67.4 1.1 copy.29
  68.5 1.5 fusion.1.order_ref
  70.0 1.8 fusion.order_ref
  72.5 0.9 pad_maximum_fusion.1
  74.4 1.4 copy-done.3
  75.8 1.4 copy-done.5
  77.2 10.1 %windows.2.wide_ref = bf16[5,2048,768]{2,1,0:T(8,128)(2,1)} custom-call(bf16[1024,768]{1,0:T(8,128)(2,1)S(1)} %copy-done.3, bf16[32,768]{1,0:T(8,128)(2,1)S(1)} %pad_maximum_fusion.7.rim_ref.own_rim, bf16[1024,768]{1,0:T(8,128)(2,1)S(1)} %copy-done.5, bf16[32,768]{1,0:T(8,128)(2,1)S(1)} %pad_maximum_fusion.6.other_rim), custom_call_target="tpu_custom_call" | custom-call | bytes 18874368 | tf_op jit(solution)/shard_map/windows/pallas_call | solution.py:265
  87.3 5.9 %windows.3.wide_ref = bf16[5,1024,896]{2,1,0:T(8,128)(2,1)} custom-call(bf16[512,896]{1,0:T(8,128)(2,1)S(1)} %get-tuple-element.51.x_ref.own_ref, bf16[32,896]{1,0:T(8,128)(2,1)S(1)} %pad_maximum_fusion.3.rim_ref.own_rim, bf16[512,896]{1,0:T(8,128)(2,1)S(1)} %copy-done.11, bf16[32,896]{1,0:T(8,128)(2,1)S(1)} %pad_maximum_fusion.2.other_rim), custom_call_target="tpu_custom_call" | custom-call | bytes 11010048 | tf_op jit(solution)/shard_map/windows/pallas_call | solution.py:265
  93.3 3.1 %all-to-all-done.1 = bf16[32,32,1024]{2,1,0:T(8,128)(2,1)S(1)} async-done(((bf16[32,32,1024]{2,1,0:T(8,128)(2,1)}), bf16[32,32,1024]{2,1,0:T(8,128)(2,1)S(1)}, u32[]{:S(2)}, u32[]{:S(2)}) %all-to-all-start.1) | async-done | bytes 2097184 | tf_op jit(solution)/shard_map/all_to_all | solution.py:441
  96.3 1.2 copy.30.add_ref
  97.6 1.6 copy-done
  99.2 1.2 copy-done.7
  100.4 1.2 copy-done.9
  101.6 1.9 head_back.1
  105.6 10.4 %grad_parts.2 = (bf16[5,128,896]{2,1,0:T(8,128)(2,1)}, bf16[5,128,896]{2,1,0:T(8,128)(2,1)}, f32[5,256,896]{2,1,0:T(8,128)}) custom-call(bf16[512,512]{1,0:T(8,128)(2,1)S(1)} %get-tuple-element.60.mine_ref, bf16[512,512]{1,0:T(8,128)(2,1)S(1)} %collective-permute-done.6.got_ref, bf16[5,1024,896]{2,1,0:T(8,128)(2,1)} %windows.3.wide_ref), custom_call_target="tpu_custom_call" | custom-call | flops 4697620480 | bytes 17104896 | tf_op jit(solution)/shard_map/grad_parts/pallas_call | solution.py:296
  116.0 3.8 %collective-permute-start.18 = (bf16[5,128,896]{2,1,0:T(8,128)(2,1)}, bf16[5,128,896]{2,1,0:T(8,128)(2,1)S(1)}, u32[]{:S(2)}, u32[]{:S(2)}) collective-permute-start(bf16[5,128,896]{2,1,0:T(8,128)(2,1)} %get-tuple-element.64), channel_id=1, source_target_pairs={{0,24},{4,100},{8,0},{12,108},{16,8},{20,116},{24,16},{28,124},{32... | collective-permute-start | bytes 3440648 | tf_op jit(solution)/shard_map/ppermute | solution.py:45
  119.8 11.8 %conv_back.1 = (bf16[448,1024]{1,0:T(8,128)(2,1)S(1)}, bf16[448,1024]{1,0:T(8,128)(2,1)S(1)}) custom-call(bf16[512,1024]{1,0:T(8,128)(2,1)S(1)} %get-tuple-element.66.g_ref, bf16[32,1024]{1,0:T(8,128)(2,1)S(1)} %pad_maximum_fusion.10.rim_ref, bf16[5,896,1024]{2,1,0:T(8,128)(2,1)} %w_hbm.5, f32[512,896]{1,0:T(8,128)S(1)} %copy-done.14, ...), custom_call_target="tpu_custom_call" | custom-call | flops 6341787648 | bytes 17334272 | tf_op jit(solution)/shard_map/conv_back/pallas_call | solution.py:190
  131.7 1.4 collective-permute-start.9
  133.6 3.5 %collective-permute-done.19 = bf16[5,128,896]{2,1,0:T(8,128)(2,1)S(1)} collective-permute-done((bf16[5,128,896]{2,1,0:T(8,128)(2,1)}, bf16[5,128,896]{2,1,0:T(8,128)(2,1)S(1)}, u32[]{:S(2)}, u32[]{:S(2)}) %collective-permute-start.19) | collective-permute-done | bytes 1146912 | tf_op jit(solution)/shard_map/ppermute | solution.py:45
  137.5 2.0 %collective-permute-start.20 = (bf16[5,64,896]{2,1,0:T(8,128)(2,1)S(1)}, bf16[5,64,896]{2,1,0:T(8,128)(2,1)S(1)}, u32[]{:S(2)}, u32[]{:S(2)}) collective-permute-start(bf16[5,64,896]{2,1,0:T(8,128)(2,1)S(1)} %get-tuple-element.82), channel_id=1, source_target_pairs={{0,8},{4,36},{8,16},{12,44},{16,24},{20,52},{24,0},{28,60},{32,40}... | collective-permute-start | bytes 1720328 | tf_op jit(solution)/shard_map/ppermute | solution.py:45
  139.5 12.1 %grad_parts.3 = (bf16[5,112,768]{2,1,0:T(8,128)(2,1)}, bf16[5,112,768]{2,1,0:T(8,128)(2,1)}, f32[5,224,768]{2,1,0:T(8,128)}) custom-call(bf16[448,1024]{1,0:T(8,128)(2,1)S(1)} %get-tuple-element.70.mine_ref, bf16[448,1024]{1,0:T(8,128)(2,1)S(1)} %collective-permute-done.9.got_ref, bf16[5,2048,768]{2,1,0:T(8,128)(2,1)} %windows.2.wide_ref), custom_call_target="tpu_custom_call" | custom-call | flops 7046430720 | bytes 22724608 | tf_op jit(solution)/shard_map/grad_parts/pallas_call | solution.py:296
  151.5 1.3 collective-permute-start.10
  154.1 2.8 %collective-permute-start.22 = (bf16[5,32,896]{2,1,0:T(8,128)(2,1)S(1)}, bf16[5,32,896]{2,1,0:T(8,128)(2,1)S(1)}, u32[]{:S(2)}, u32[]{:S(2)}) collective-permute-start(bf16[5,32,896]{2,1,0:T(8,128)(2,1)S(1)} %get-tuple-element.84), channel_id=1, source_target_pairs={{0,96},{4,28},{8,104},{12,4},{16,112},{20,12},{24,120},{28,20},{32... | collective-permute-start | bytes 860168 | tf_op jit(solution)/shard_map/ppermute | solution.py:45
  156.9 10.2 %collective-permute-done.10 = bf16[5,112,768]{2,1,0:T(8,128)(2,1)S(1)} collective-permute-done((bf16[5,112,768]{2,1,0:T(8,128)(2,1)}, bf16[5,112,768]{2,1,0:T(8,128)(2,1)S(1)}, u32[]{:S(2)}, u32[]{:S(2)}) %collective-permute-start.10) | collective-permute-done | bytes 860192 | tf_op jit(solution)/shard_map/ppermute | solution.py:45
  167.4 3.0 %collective-permute-start.13 = (bf16[5,56,768]{2,1,0:T(8,128)(2,1)S(1)}, bf16[5,56,768]{2,1,0:T(8,128)(2,1)S(1)}, u32[]{:S(2)}, u32[]{:S(2)}) collective-permute-start(bf16[5,56,768]{2,1,0:T(8,128)(2,1)S(1)} %get-tuple-element.77), channel_id=1, source_target_pairs={{0,24},{4,100},{8,0},{12,108},{16,8},{20,116},{24,16},{28,124},{32... | collective-permute-start | bytes 1290248 | tf_op jit(solution)/shard_map/ppermute | solution.py:45
  170.4 1.2 collective-permute-start.23
  171.7 4.4 %collective-permute-done.13 = bf16[5,56,768]{2,1,0:T(8,128)(2,1)S(1)} collective-permute-done((bf16[5,56,768]{2,1,0:T(8,128)(2,1)S(1)}, bf16[5,56,768]{2,1,0:T(8,128)(2,1)S(1)}, u32[]{:S(2)}, u32[]{:S(2)}) %collective-permute-start.13) | collective-permute-done | bytes 430112 | tf_op jit(solution)/shard_map/ppermute | solution.py:45
  176.1 4.0 %collective-permute-done.12 = bf16[5,56,768]{2,1,0:T(8,128)(2,1)S(1)} collective-permute-done((bf16[5,56,768]{2,1,0:T(8,128)(2,1)S(1)}, bf16[5,56,768]{2,1,0:T(8,128)(2,1)S(1)}, u32[]{:S(2)}, u32[]{:S(2)}) %collective-permute-start.12) | collective-permute-done | bytes 430112 | tf_op jit(solution)/shard_map/ppermute | solution.py:45
  180.5 3.0 %collective-permute-start.14 = (bf16[5,28,768]{2,1,0:T(8,128)(2,1)S(1)}, bf16[5,28,768]{2,1,0:T(8,128)(2,1)S(1)}, u32[]{:S(2)}, u32[]{:S(2)}) collective-permute-start(bf16[5,28,768]{2,1,0:T(8,128)(2,1)S(1)} %get-tuple-element.78), channel_id=1, source_target_pairs={{0,96},{4,28},{8,104},{12,4},{16,112},{20,12},{24,120},{28,20},{32... | collective-permute-start | bytes 645128 | tf_op jit(solution)/shard_map/ppermute | solution.py:45
  183.9 1.8 collective-permute-start.24
  185.7 1.6 collective-permute-done.14
  187.3 5.8 %collective-permute-done.15 = bf16[5,28,768]{2,1,0:T(8,128)(2,1)S(1)} collective-permute-done((bf16[5,28,768]{2,1,0:T(8,128)(2,1)S(1)}, bf16[5,28,768]{2,1,0:T(8,128)(2,1)S(1)}, u32[]{:S(2)}, u32[]{:S(2)}) %collective-permute-start.15) | collective-permute-done | bytes 215072 | tf_op jit(solution)/shard_map/ppermute | solution.py:45
  193.5 1.8 collective-permute-start.16
  195.2 1.0 fusion.5
  196.3 3.0 %collective-permute-done.16 = bf16[2,28,768]{2,1,0:T(8,128)(2,1)S(1)} collective-permute-done((bf16[2,28,768]{2,1,0:T(8,128)(2,1)S(1)}, bf16[2,28,768]{2,1,0:T(8,128)(2,1)S(1)}, u32[]{:S(2)}, u32[]{:S(2)}) %collective-permute-start.16) | collective-permute-done | bytes 86048 | tf_op jit(solution)/shard_map/ppermute | solution.py:45
  199.3 1.0 fusion.9
  (117 shorter events, 14.2 us)
Async XLA Ops:
  0.6 14.9 %collective-permute-start = (bf16[1024,768]{1,0:T(8,128)(2,1)}, bf16[1024,768]{1,0:T(8,128)(2,1)S(1)}, u32[]{:S(2)}, u32[]{:S(2)}) collective-permute-start(bf16[1024,768]{1,0:T(8,128)(2,1)} %own_ref), channel_id=1, source_target_pairs={{0,4},{4,0},{8,12},{12,8},{16,20},{20,16},{24,28},{28,24},{32,36},... | collective-permute-start | bytes 4718600 | tf_op jit(solution)/shard_map/ppermute | solution.py:45
  4.7 33.1 %all-to-all-start = ((bf16[32,2,16]{2,1,0:T(2,128)(2,1)}), bf16[32,2,16]{2,1,0:T(2,128)(2,1)S(1)}, u32[]{:S(2)}, u32[]{:S(2)}) async-start(bf16[32,2,16]{2,1,0:T(2,128)(2,1)} %copy.25), calls=%async_computation | async-start | bytes 32768 | tf_op jit(solution)/shard_map/all_to_all | solution.py:406
  13.8 1.7 collective-permute-start.1
  15.5 15.9 %copy-start.4 = (bf16[1024,768]{1,0:T(8,128)(2,1)}, bf16[1024,768]{1,0:T(8,128)(2,1)S(1)}, u32[]{:S(2)}) copy-start(bf16[1024,768]{1,0:T(8,128)(2,1)S(1)} %collective-permute-done.other_ref) | copy-start | bytes 4718596
  15.6 1.9 copy-start.2
  32.6 1.3 copy-start.15
  33.9 5.9 %collective-permute-start.2 = (bf16[512,896]{1,0:T(8,128)(2,1)S(1)}, bf16[512,896]{1,0:T(8,128)(2,1)S(1)}, u32[]{:S(2)}, u32[]{:S(2)}) collective-permute-start(bf16[512,896]{1,0:T(8,128)(2,1)S(1)} %get-tuple-element.51.x_ref.own_ref), channel_id=1, source_target_pairs={{0,4},{4,0},{8,12},{12,8},{16,20},{20,16},{24,28},{28,24},{32,36},... | collective-permute-start | bytes 2752520 | tf_op jit(solution)/shard_map/ppermute | solution.py:45
  38.0 0.9 collective-permute-start.3
  39.7 10.6 %copy-start.10 = (bf16[512,896]{1,0:T(8,128)(2,1)}, bf16[512,896]{1,0:T(8,128)(2,1)S(1)}, u32[]{:S(2)}) copy-start(bf16[512,896]{1,0:T(8,128)(2,1)S(1)} %collective-permute-done.2.other_ref) | copy-start | bytes 2752516
  50.4 2.1 %copy-start.6 = (f32[256,1024]{1,0:T(8,128)}, f32[256,1024]{1,0:T(8,128)S(1)}, u32[]{:S(2)}) copy-start(f32[256,1024]{1,0:T(8,128)S(1)} %get-tuple-element.56.even_ref) | copy-start | bytes 3145732
  50.4 2.1 %copy-start.8 = (f32[256,1024]{1,0:T(8,128)}, f32[256,1024]{1,0:T(8,128)S(1)}, u32[]{:S(2)}) copy-start(f32[256,1024]{1,0:T(8,128)S(1)} %get-tuple-element.57.odd_ref) | copy-start | bytes 3145732
  52.4 13.8 %copy-start.18 = (s32[256]{0:T(256)S(1)}, s32[256]{0:T(256)}, u32[]{:S(2)}) copy-start(s32[256]{0:T(256)} %param.14) | copy-start | bytes 3076
  52.4 13.8 %copy-start.19 = (bf16[256]{0:T(256)(128)(2,1)S(1)}, bf16[256]{0:T(256)(128)(2,1)}, u32[]{:S(2)}) copy-start(bf16[256]{0:T(256)(128)(2,1)} %param.15) | copy-start | bytes 1540
  52.5 43.9 %all-to-all-start.1 = ((bf16[32,32,1024]{2,1,0:T(8,128)(2,1)}), bf16[32,32,1024]{2,1,0:T(8,128)(2,1)S(1)}, u32[]{:S(2)}, u32[]{:S(2)}) async-start(bf16[32,32,1024]{2,1,0:T(8,128)(2,1)} %bitcast.27), calls=%async_computation.1 | async-start | bytes 4194304 | tf_op jit(solution)/shard_map/all_to_all | solution.py:441
  72.2 1.5 collective-permute-start.4
  73.4 13.9 %collective-permute-start.5 = (bf16[2,896]{1,0:T(2,128)(2,1)S(1)}, bf16[2,896]{1,0:T(2,128)(2,1)S(1)}, u32[]{:S(2)}, u32[]{:S(2)}) collective-permute-start(bf16[2,896]{1,0:T(2,128)(2,1)S(1)} %collective-permute-done.3), channel_id=1, source_target_pairs={{0,4},{4,0},{8,12},{12,8},{16,20},{20,16},{24,28},{28,24},{32,36},... | collective-permute-start | bytes 10760 | tf_op jit(solution)/shard_map/ppermute | solution.py:45
  74.4 1.4 copy-start.3
  75.8 1.4 copy-start.5
  77.2 10.1 %copy-start.11 = (bf16[512,896]{1,0:T(8,128)(2,1)S(1)}, bf16[512,896]{1,0:T(8,128)(2,1)}, u32[]{:S(2)}) copy-start(bf16[512,896]{1,0:T(8,128)(2,1)} %copy-done.10) | copy-start | bytes 2752516
  87.3 10.2 %copy-start.12 = (f32[1024]{0:T(1024)S(1)}, f32[1024]{0:T(1024)}, u32[]{:S(2)}) copy-start(f32[1024]{0:T(1024)} %param.11) | copy-start | bytes 12292
  97.6 1.6 copy-start
  99.2 1.2 copy-start.7
  103.5 2.1 %collective-permute-start.6 = (bf16[512,512]{1,0:T(8,128)(2,1)S(1)}, bf16[512,512]{1,0:T(8,128)(2,1)S(1)}, u32[]{:S(2)}, u32[]{:S(2)}) collective-permute-start(bf16[512,512]{1,0:T(8,128)(2,1)S(1)} %get-tuple-element.61), channel_id=1, source_target_pairs={{0,4},{4,0},{8,12},{12,8},{16,20},{20,16},{24,28},{28,24},{32,36},... | collective-permute-start | bytes 1572872 | tf_op jit(solution)/shard_map/ppermute | solution.py:45
  103.6 1.9 collective-permute-start.7
  104.2 1.3 collective-permute-start.8
  105.6 14.2 %copy-start.1 = (bf16[896,896]{1,0:T(8,128)(2,1)S(1)}, bf16[896,896]{1,0:T(8,128)(2,1)}, u32[]{:S(2)}) copy-start(bf16[896,896]{1,0:T(8,128)(2,1)} %fusion.1.order_ref) | copy-start | bytes 4816900
  105.6 14.2 %copy-start.14 = (f32[512,896]{1,0:T(8,128)S(1)}, f32[512,896]{1,0:T(8,128)}, u32[]{:S(2)}) copy-start(f32[512,896]{1,0:T(8,128)} %copy-done.13) | copy-start | bytes 5505028
  105.6 14.2 %copy-start.16 = (f32[512,896]{1,0:T(8,128)S(1)}, f32[512,896]{1,0:T(8,128)}, u32[]{:S(2)}) copy-start(f32[512,896]{1,0:T(8,128)} %copy-done.15) | copy-start | bytes 5505028
  116.0 17.6 %collective-permute-start.18 = (bf16[5,128,896]{2,1,0:T(8,128)(2,1)}, bf16[5,128,896]{2,1,0:T(8,128)(2,1)S(1)}, u32[]{:S(2)}, u32[]{:S(2)}) collective-permute-start(bf16[5,128,896]{2,1,0:T(8,128)(2,1)} %get-tuple-element.64), channel_id=1, source_target_pairs={{0,24},{4,100},{8,0},{12,108},{16,8},{20,116},{24,16},{28,124},{32... | collective-permute-start | bytes 3440648 | tf_op jit(solution)/shard_map/ppermute | solution.py:45
  119.8 17.3 %collective-permute-start.19 = (bf16[5,128,896]{2,1,0:T(8,128)(2,1)}, bf16[5,128,896]{2,1,0:T(8,128)(2,1)S(1)}, u32[]{:S(2)}, u32[]{:S(2)}) collective-permute-start(bf16[5,128,896]{2,1,0:T(8,128)(2,1)} %get-tuple-element.63), channel_id=1, source_target_pairs={{0,8},{4,36},{8,16},{12,44},{16,24},{20,52},{24,0},{28,60},{32,40}... | collective-permute-start | bytes 3440648 | tf_op jit(solution)/shard_map/ppermute | solution.py:45
  119.8 17.3 %slice-start = ((s8[4587520]{0:T(1024)(128)(4,1)}), s8[4194304]{0:T(1024)(128)(4,1)S(1)}, s32[]{:S(2)}) async-start(s8[4587520]{0:T(1024)(128)(4,1)} %bitcast.28), calls=%async_computation.2 | async-start | bytes 8388608
  119.8 17.3 %slice-start.1 = ((s8[4587520]{0:T(1024)(128)(4,1)}), s8[393216]{0:T(1024)(128)(4,1)S(1)}, s32[]{:S(2)}) async-start(s8[4587520]{0:T(1024)(128)(4,1)} %bitcast.28), calls=%async_computation.3 | async-start | bytes 786432
  131.7 7.8 %collective-permute-start.9 = (bf16[448,1024]{1,0:T(8,128)(2,1)S(1)}, bf16[448,1024]{1,0:T(8,128)(2,1)S(1)}, u32[]{:S(2)}, u32[]{:S(2)}) collective-permute-start(bf16[448,1024]{1,0:T(8,128)(2,1)S(1)} %get-tuple-element.71), channel_id=1, source_target_pairs={{0,4},{4,0},{8,12},{12,8},{16,20},{20,16},{24,28},{28,24},{32,36},... | collective-permute-start | bytes 2752520 | tf_op jit(solution)/shard_map/ppermute | solution.py:45
  137.4 16.2 %collective-permute-start.21 = (bf16[5,64,896]{2,1,0:T(8,128)(2,1)S(1)}, bf16[5,64,896]{2,1,0:T(8,128)(2,1)S(1)}, u32[]{:S(2)}, u32[]{:S(2)}) collective-permute-start(bf16[5,64,896]{2,1,0:T(8,128)(2,1)S(1)} %get-tuple-element.83), channel_id=1, source_target_pairs={{0,24},{4,100},{8,0},{12,108},{16,8},{20,116},{24,16},{28,124},{32... | collective-permute-start | bytes 1720328 | tf_op jit(solution)/shard_map/ppermute | solution.py:45
  137.5 16.1 %collective-permute-start.20 = (bf16[5,64,896]{2,1,0:T(8,128)(2,1)S(1)}, bf16[5,64,896]{2,1,0:T(8,128)(2,1)S(1)}, u32[]{:S(2)}, u32[]{:S(2)}) collective-permute-start(bf16[5,64,896]{2,1,0:T(8,128)(2,1)S(1)} %get-tuple-element.82), channel_id=1, source_target_pairs={{0,8},{4,36},{8,16},{12,44},{16,24},{20,52},{24,0},{28,60},{32,40}... | collective-permute-start | bytes 1720328 | tf_op jit(solution)/shard_map/ppermute | solution.py:45
  151.5 15.6 %collective-permute-start.10 = (bf16[5,112,768]{2,1,0:T(8,128)(2,1)}, bf16[5,112,768]{2,1,0:T(8,128)(2,1)S(1)}, u32[]{:S(2)}, u32[]{:S(2)}) collective-permute-start(bf16[5,112,768]{2,1,0:T(8,128)(2,1)} %get-tuple-element.74), channel_id=1, source_target_pairs={{0,24},{4,100},{8,0},{12,108},{16,8},{20,116},{24,16},{28,124},{32... | collective-permute-start | bytes 2580488 | tf_op jit(solution)/shard_map/ppermute | solution.py:45
  152.8 14.3 %collective-permute-start.11 = (bf16[5,112,768]{2,1,0:T(8,128)(2,1)}, bf16[5,112,768]{2,1,0:T(8,128)(2,1)S(1)}, u32[]{:S(2)}, u32[]{:S(2)}) collective-permute-start(bf16[5,112,768]{2,1,0:T(8,128)(2,1)} %get-tuple-element.75), channel_id=1, source_target_pairs={{0,8},{4,36},{8,16},{12,44},{16,24},{20,52},{24,0},{28,60},{32,40}... | collective-permute-start | bytes 2580488 | tf_op jit(solution)/shard_map/ppermute | solution.py:45
  153.6 13.6 %copy-start.17 = (f32[5,224,768]{2,1,0:T(8,128)S(1)}, f32[5,224,768]{2,1,0:T(8,128)}, u32[]{:S(2)}) copy-start(f32[5,224,768]{2,1,0:T(8,128)} %get-tuple-element.73) | copy-start | bytes 10321924
  154.1 17.5 %collective-permute-start.22 = (bf16[5,32,896]{2,1,0:T(8,128)(2,1)S(1)}, bf16[5,32,896]{2,1,0:T(8,128)(2,1)S(1)}, u32[]{:S(2)}, u32[]{:S(2)}) collective-permute-start(bf16[5,32,896]{2,1,0:T(8,128)(2,1)S(1)} %get-tuple-element.84), channel_id=1, source_target_pairs={{0,96},{4,28},{8,104},{12,4},{16,112},{20,12},{24,120},{28,20},{32... | collective-permute-start | bytes 860168 | tf_op jit(solution)/shard_map/ppermute | solution.py:45
  167.4 8.7 %collective-permute-start.13 = (bf16[5,56,768]{2,1,0:T(8,128)(2,1)S(1)}, bf16[5,56,768]{2,1,0:T(8,128)(2,1)S(1)}, u32[]{:S(2)}, u32[]{:S(2)}) collective-permute-start(bf16[5,56,768]{2,1,0:T(8,128)(2,1)S(1)} %get-tuple-element.77), channel_id=1, source_target_pairs={{0,24},{4,100},{8,0},{12,108},{16,8},{20,116},{24,16},{28,124},{32... | collective-permute-start | bytes 1290248 | tf_op jit(solution)/shard_map/ppermute | solution.py:45
  170.4 9.7 %collective-permute-start.12 = (bf16[5,56,768]{2,1,0:T(8,128)(2,1)S(1)}, bf16[5,56,768]{2,1,0:T(8,128)(2,1)S(1)}, u32[]{:S(2)}, u32[]{:S(2)}) collective-permute-start(bf16[5,56,768]{2,1,0:T(8,128)(2,1)S(1)} %get-tuple-element.76), channel_id=1, source_target_pairs={{0,8},{4,36},{8,16},{12,44},{16,24},{20,52},{24,0},{28,60},{32,40}... | collective-permute-start | bytes 1290248 | tf_op jit(solution)/shard_map/ppermute | solution.py:45
  170.4 13.1 %collective-permute-start.23 = (bf16[5,32,896]{2,1,0:T(8,128)(2,1)S(1)}, bf16[5,32,896]{2,1,0:T(8,128)(2,1)S(1)}, u32[]{:S(2)}, u32[]{:S(2)}) collective-permute-start(bf16[5,32,896]{2,1,0:T(8,128)(2,1)S(1)} %get-tuple-element.85), channel_id=1, source_target_pairs={{0,32},{4,12},{8,40},{12,20},{16,48},{20,28},{24,56},{28,4},{32,64... | collective-permute-start | bytes 860168 | tf_op jit(solution)/shard_map/ppermute | solution.py:45
  180.5 6.7 %collective-permute-start.14 = (bf16[5,28,768]{2,1,0:T(8,128)(2,1)S(1)}, bf16[5,28,768]{2,1,0:T(8,128)(2,1)S(1)}, u32[]{:S(2)}, u32[]{:S(2)}) collective-permute-start(bf16[5,28,768]{2,1,0:T(8,128)(2,1)S(1)} %get-tuple-element.78), channel_id=1, source_target_pairs={{0,96},{4,28},{8,104},{12,4},{16,112},{20,12},{24,120},{28,20},{32... | collective-permute-start | bytes 645128 | tf_op jit(solution)/shard_map/ppermute | solution.py:45
  183.6 11.6 %collective-permute-start.25 = (bf16[3,32,896]{2,1,0:T(8,128)(2,1)S(1)}, bf16[3,32,896]{2,1,0:T(8,128)(2,1)S(1)}, u32[]{:S(2)}, u32[]{:S(2)}) collective-permute-start(bf16[3,32,896]{2,1,0:T(8,128)(2,1)S(1)} %fusion.10), channel_id=1, source_target_pairs={{0,96},{4,28},{8,104},{12,4},{16,112},{20,12},{24,120},{28,20},{32... | collective-permute-start | bytes 516104 | tf_op jit(solution)/shard_map/ppermute | solution.py:45
  183.9 11.3 %collective-permute-start.24 = (bf16[2,32,896]{2,1,0:T(8,128)(2,1)S(1)}, bf16[2,32,896]{2,1,0:T(8,128)(2,1)S(1)}, u32[]{:S(2)}, u32[]{:S(2)}) collective-permute-start(bf16[2,32,896]{2,1,0:T(8,128)(2,1)S(1)} %fusion.17), channel_id=1, source_target_pairs={{0,32},{4,12},{8,40},{12,20},{16,48},{20,28},{24,56},{28,4},{32,64... | collective-permute-start | bytes 344072 | tf_op jit(solution)/shard_map/ppermute | solution.py:45
  185.7 7.4 %collective-permute-start.15 = (bf16[5,28,768]{2,1,0:T(8,128)(2,1)S(1)}, bf16[5,28,768]{2,1,0:T(8,128)(2,1)S(1)}, u32[]{:S(2)}, u32[]{:S(2)}) collective-permute-start(bf16[5,28,768]{2,1,0:T(8,128)(2,1)S(1)} %get-tuple-element.79), channel_id=1, source_target_pairs={{0,32},{4,12},{8,40},{12,20},{16,48},{20,28},{24,56},{28,4},{32,64... | collective-permute-start | bytes 645128 | tf_op jit(solution)/shard_map/ppermute | solution.py:45
  193.1 6.2 %collective-permute-start.17 = (bf16[3,28,768]{2,1,0:T(8,128)(2,1)S(1)}, bf16[3,28,768]{2,1,0:T(8,128)(2,1)S(1)}, u32[]{:S(2)}, u32[]{:S(2)}) collective-permute-start(bf16[3,28,768]{2,1,0:T(8,128)(2,1)S(1)} %fusion.11), channel_id=1, source_target_pairs={{0,96},{4,28},{8,104},{12,4},{16,112},{20,12},{24,120},{28,20},{32... | collective-permute-start | bytes 387080 | tf_op jit(solution)/shard_map/ppermute | solution.py:45
  193.5 5.8 %collective-permute-start.16 = (bf16[2,28,768]{2,1,0:T(8,128)(2,1)S(1)}, bf16[2,28,768]{2,1,0:T(8,128)(2,1)S(1)}, u32[]{:S(2)}, u32[]{:S(2)}) collective-permute-start(bf16[2,28,768]{2,1,0:T(8,128)(2,1)S(1)} %fusion.18), channel_id=1, source_target_pairs={{0,32},{4,12},{8,40},{12,20},{16,48},{20,28},{24,56},{28,4},{32,64... | collective-permute-start | bytes 258056 | tf_op jit(solution)/shard_map/ppermute | solution.py:45
  (2 other events, 2.4 us)

commit v2 on v1

--- a/solution.py
+++ b/solution.py
@@ -27,15 +27,11 @@
 
 
 SIBLING = pairs_of(lambda z, x, c: (z, x, 1 - c))
-RINGS = (
-    (
-        pairs_of(lambda z, x, c: (z, x + 1, c) if c == 0 else (z + 1, x, c)),
-        pairs_of(lambda z, x, c: (z, x - 1, c) if c == 0 else (z - 1, x, c)),
-    ),
-    (
-        pairs_of(lambda z, x, c: (z + 1, x, c) if c == 0 else (z, x + 1, c)),
-        pairs_of(lambda z, x, c: (z - 1, x, c) if c == 0 else (z, x - 1, c)),
-    ),
+WAYS = tuple(
+    tuple(
+        pairs_of(lambda z, x, c: (z, x + r, c) if c == first else (z + r, x, c)) for r in (1, 2, 3)
+    )
+    for first in (0, 1)
 )
 N_SEQ = NZ * NX * 2
 OUTWARD = [(s, s - 1) for s in range(2, N_SEQ, 2)] + [(s, s + 1) for s in range(1, N_SEQ - 1, 2)]
@@ -54,7 +50,11 @@
 RIM = 16
 
 
-def params(mib=44):
+def in_hbm(value):
+    return pltpu.with_memory_space_constraint(value, pltpu.HBM)
+
+
+def params(mib=28):
     return pltpu.CompilerParams(vmem_limit_bytes=mib << 20)
 
 
@@ -80,7 +80,7 @@
 
 
 def conv_kernel(
-    taps, x_ref, rim_ref, w_hbm, pooled_ref, even_ref, odd_ref, w_ref, rimmed, piece, wide, acc, sem
+    taps, x_ref, rim_ref, w_hbm, pooled_ref, even_hbm, odd_hbm, w_ref, rimmed, piece, wide, acc, slopes, sem, out_sem
 ):
     n, f = x_ref.shape
     copies = [
@@ -113,8 +113,16 @@
             even, even_slope = gelu_both(acc[j, pl.ds(0, TILE // 2, stride=2), :])
             odd, odd_slope = gelu_both(acc[j, pl.ds(1, TILE // 2, stride=2), :])
             pooled_ref[q, cols] = ((even + odd) * 0.5).astype(BF)
-            even_ref[q, cols] = even_slope * 0.5
-            odd_ref[q, cols] = odd_slope * 0.5
+            slopes[0, q, cols] = even_slope * 0.5
+            slopes[1, q, cols] = odd_slope * 0.5
+        for side, out in enumerate((even_hbm, odd_hbm)):
+            pltpu.make_async_copy(slopes.at[side, q], out.at[q], out_sem.at[side, m]).start()
+
+    @pl.loop(0, n // TILE)
+    def _(m):
+        q = pl.ds(pl.multiple_of(m * (TILE // 2), TILE // 2), TILE // 2)
+        for side, out in enumerate((even_hbm, odd_hbm)):
+            pltpu.make_async_copy(slopes.at[side, q], out.at[q], out_sem.at[side, m]).wait()
 
 
 def conv_pool(x, rim, w):
@@ -123,21 +131,23 @@
     return pl.pallas_call(
         functools.partial(conv_kernel, taps),
         out_shape=[jax.ShapeDtypeStruct((n // 2, c), BF)]
-        + [jax.ShapeDtypeStruct((n // 2, c), F32)] * 2,
+        + [pltpu.HBM((n // 2, c), F32)] * 2,
         in_specs=[IN_VMEM, IN_VMEM, IN_PLACE],
-        out_specs=[IN_VMEM] * 3,
+        out_specs=[IN_VMEM] + [pl.BlockSpec(memory_space=pltpu.HBM)] * 2,
         scratch_shapes=[
             VM((taps * f, c), BF),
             VM((n + 2 * RIM, f), BF),
             VM((PIECE + 2 * RIM, f), F32),
             VM((n, taps * f), BF),
             VM((c // LANES, TILE, LANES), F32),
+            VM((2, n // 2, c), F32),
             pltpu.SemaphoreType.DMA((taps,)),
+            pltpu.SemaphoreType.DMA((2, n // TILE)),
         ],
         compiler_params=params(),
         cost_estimate=cost(2 * n * f * c * taps, 2 * (n * f + taps * f * c) + 5 * n * c, n * c),
         name="conv_pool",
-    )(x, rim, w)
+    )(x, rim, in_hbm(w))
 
 
 def back_kernel(
@@ -206,16 +216,34 @@
             2 * n * f * c * taps + 4 * n * f * f, 2 * (n * c + taps * f * c + f * f) + 12 * n * f
         ),
         name="conv_back",
-    )(g, rim, w, even, odd, order)
-
-
-def head_kernel(add_ref, come_ref, head_ref, even_ref, odd_ref, order_ref, g_ref, mine_ref, theirs_ref, pairs):
-    n = add_ref.shape[0]
-    total = jnp.dot(add_ref[...], come_ref[...], preferred_element_type=F32) * head_ref[...]
+    )(g, rim, in_hbm(w), even, odd, order)
+
+
+def head_kernel(
+    donor_ref, accept_ref, come_ref, head_ref, even_hbm, odd_hbm, order_hbm, g_ref, mine_ref, theirs_ref, slopes, order_ref, pairs, sem
+):
+    n = donor_ref.shape[0]
+    copies = [
+        pltpu.make_async_copy(even_hbm, slopes.at[0], sem.at[0]),
+        pltpu.make_async_copy(odd_hbm, slopes.at[1], sem.at[1]),
+        pltpu.make_async_copy(order_hbm, order_ref, sem.at[2]),
+    ]
+    for copy in copies:
+        copy.start()
+    slots, c = donor_ref.shape[1], come_ref.shape[2]
+    each = come_ref.shape[1] // 2
+    total = jnp.dot(
+        donor_ref[...], come_ref[:, :each, :].reshape(slots, c), preferred_element_type=F32
+    ) + jnp.dot(
+        accept_ref[...], come_ref[:, each:, :].reshape(slots, c), preferred_element_type=F32
+    )
+    total = total * head_ref[...]
+    for copy in copies:
+        copy.wait()
     for j in range(pairs.shape[0]):
         cols = slice(j * LANES, (j + 1) * LANES)
-        pairs[j, pl.ds(0, n, stride=2), :] = total[:, cols] * even_ref[:, cols]
-        pairs[j, pl.ds(1, n, stride=2), :] = total[:, cols] * odd_ref[:, cols]
+        pairs[j, pl.ds(0, n, stride=2), :] = total[:, cols] * slopes[0, :, cols]
+        pairs[j, pl.ds(1, n, stride=2), :] = total[:, cols] * slopes[1, :, cols]
         g_ref[:, cols] = pairs[j].astype(BF)
     turned = lax.dot_general(
         order_ref[...], g_ref[...], (((1,), (1,)), ((), ())), preferred_element_type=F32
@@ -225,21 +253,26 @@
     theirs_ref[...] = turned[half:].astype(BF)
 
 
-def head_back(add, come, head, even, odd, order):
+def head_back(donor, accept, come, head, even, odd, order):
     n, c = even.shape
     return pl.pallas_call(
         head_kernel,
         out_shape=[jax.ShapeDtypeStruct((2 * n, c), BF)]
         + [jax.ShapeDtypeStruct((c // 2, 2 * n), BF)] * 2,
-        in_specs=[IN_VMEM] * 6,
+        in_specs=[IN_VMEM] * 4 + [IN_PLACE] * 3,
         out_specs=[IN_VMEM] * 3,
-        scratch_shapes=[VM((c // LANES, 2 * n, LANES), F32)],
-        compiler_params=params(),
+        scratch_shapes=[
+            VM((2, n, c), F32),
+            VM((c, c), BF),
+            VM((c // LANES, 2 * n, LANES), F32),
+            pltpu.SemaphoreType.DMA((3,)),
+        ],
+        compiler_params=params(20),
         cost_estimate=cost(
-            2 * n * c * come.shape[0] + 4 * n * c * c, 2 * (come.size + add.size + c * c) + 16 * n * c
+            4 * n * c * donor.shape[1] + 4 * n * c * c, 2 * (come.size + c * c) + 16 * n * c
         ),
         name="head_back",
-    )(add, come, head, even, odd, order)
+    )(donor, accept, come, head, in_hbm(even), in_hbm(odd), in_hbm(order))
 
 
 def window_kernel(taps, own_ref, own_rim, other_ref, other_rim, out_ref, rimmed, piece):
@@ -269,13 +302,13 @@
         in_specs=[IN_VMEM] * 4,
         out_specs=pl.BlockSpec((taps, PIECE, f), lambda i: (0, i, 0)),
         scratch_shapes=[VM((2, n + 2 * RIM, f), BF), VM((PIECE + 2 * RIM, f), F32)],
-        compiler_params=params(),
+        compiler_params=params(14),
         cost_estimate=cost(0, 2 * (taps + 1) * 2 * n * f),
         name="windows",
     )(own, own_rim, other, other_rim)
 
 
-def grad_kernel(mine_ref, got_ref, wide_ref, plus_ref, minus_ref, keep_ref, both):
+def grad_kernel(mine_ref, got_ref, wide_ref, next_ref, far_ref, prev_ref, keep_ref, both):
     m, n = mine_ref.shape
 
     @pl.when(pl.program_id(0) == 0)
@@ -284,32 +317,31 @@
         both[:, n:] = got_ref[...]
 
     total = jnp.dot(both[...], wide_ref[0], preferred_element_type=F32)
-    plus_ref[0] = total[: m // 4].astype(BF)
-    minus_ref[0] = total[m // 4 : m // 2].astype(BF)
-    keep_ref[0] = total[m // 2 :]
-
-
-def grad_parts(mine, got, wide):
+    q = m // 4
+    keep_ref[0] = total[:q]
+    next_ref[0] = total[q : 2 * q].astype(BF)
+    far_ref[0] = total[2 * q : 3 * q].astype(BF)
+    prev_ref[0] = total[3 * q :].astype(BF)
+
+
+def grad_parts(mine, got, wide, first, taps):
     m, n = mine.shape
-    taps, _, f = wide.shape
-    block = lambda rows: pl.BlockSpec((1, rows, f), lambda k: (k, 0, 0))
+    f = wide.shape[2]
+    block = lambda rows, low=0: pl.BlockSpec((1, rows, f), lambda k: (k + low, 0, 0))
     return pl.pallas_call(
         grad_kernel,
         grid=(taps,),
-        out_shape=[
-            pltpu.HBM((taps, m // 4, f), BF),
-            pltpu.HBM((taps, m // 4, f), BF),
-            pltpu.HBM((taps, m // 2, f), F32),
-        ],
-        in_specs=[IN_VMEM, IN_VMEM, block(2 * n)],
-        out_specs=[block(m // 4), block(m // 4), block(m // 2)],
+        out_shape=[jax.ShapeDtypeStruct((taps, m // 4, f), BF)] * 3
+        + [jax.ShapeDtypeStruct((taps, m // 4, f), F32)],
+        in_specs=[IN_VMEM, IN_VMEM, block(2 * n, first)],
+        out_specs=[block(m // 4)] * 4,
         scratch_shapes=[VM((m, 2 * n), BF)],
-        compiler_params=params(),
+        compiler_params=params(20),
         cost_estimate=cost(
             4 * m * n * f * taps, 2 * (2 * m * n + 2 * taps * n * f) + 3 * taps * m * f
         ),
         name="grad_parts",
-    )(mine, got, pltpu.with_memory_space_constraint(wide, pltpu.HBM))
+    )(mine, got, in_hbm(wide))
 
 
 def outer_rim(block, odd):
@@ -323,17 +355,11 @@
     )
 
 
-EIGHTHS = ((2, 0), (1, 1), (2, 1), (3, 0), (1, 0), (3, 1), (0, 0), (0, 1))
-
-
 def order_matrix(channels, seq):
     block = channels // N_SEQ
     core, x, z = seq % 2, (seq // 2) % NX, seq // (2 * NX)
     row = lax.broadcasted_iota(jnp.int32, (channels, 1), 0)
-    half, eighth = row // (16 * block), (row // (2 * block)) % 8
-    r1 = sum(jnp.where(eighth == e, r, 0) for e, (r, _) in enumerate(EIGHTHS))
-    r2 = sum(jnp.where(eighth == e, 2 * h, 0) for e, (_, h) in enumerate(EIGHTHS))
-    r2 = r2 + (row // block) % 2
+    half, r1, r2 = row // (16 * block), (row // (4 * block)) % 4, (row // block) % 4
     side = jnp.where(half == 0, core, 1 - core)
     to_x = (x + jnp.where(side == 0, r1, r2)) % NX
     to_z = (z + jnp.where(side == 0, r2, r1)) % NZ
@@ -341,42 +367,22 @@
     return (wanted == lax.broadcasted_iota(jnp.int32, (1, channels), 1)).astype(BF)
 
 
-def ring_sums(plus, minus, keep):
-    u = keep.shape[1] // 4
-    wide = lambda v: v.astype(F32)
-    got_p = move(plus, RINGS[0][0])
-    got_m = move(minus, RINGS[0][1])
-    on_p, on_m = lax.optimization_barrier(
-        (
-            (keep[:, :u] + wide(got_p[:, :u])).astype(BF),
-            (keep[:, u : 2 * u] + wide(got_m[:, :u])).astype(BF),
-        )
-    )
-    late_p = move(on_p, RINGS[0][0])
-    late_m = move(on_m, RINGS[0][1])
-    low = keep[:, 2 * u : 3 * u] + wide(got_m[:, u:]) + wide(late_p)
-    high = keep[:, 3 * u :] + wide(got_p[:, u:]) + wide(late_m)
-    b = u // 2
-    near, one, two, three = low[:, :b], low[:, b:], high[:, :b], high[:, b:]
-    cut = keep.shape[0] // 2
-    early = lax.broadcasted_iota(jnp.int32, near.shape, 0) < cut
-    join = lambda first, last: jnp.where(early, first, last)
-    on_p, on_m = lax.optimization_barrier(
-        (join(two, one).astype(BF), join(three, two).astype(BF))
-    )
-    got_p, got_m = move(on_p, RINGS[1][0]), move(on_m, RINGS[1][1])
-    on_p, on_m = lax.optimization_barrier(
-        (
-            (one[:cut] + wide(got_p[:cut])).astype(BF),
-            (three[cut:] + wide(got_m[cut:])).astype(BF),
-        )
-    )
-    late_p, late_m = move(on_p, RINGS[1][0]), move(on_m, RINGS[1][1])
-    return (
-        near
-        + wide(join(got_m, got_p))
-        + jnp.concatenate([wide(late_p), wide(late_m)], axis=0)
-    )
+def axis_sum(after, far, prev, keep, ways):
+    total = keep
+    got = []
+    for term, pairs in zip((far, after, prev), (ways[1], ways[0], ways[2])):
+        got.append(move(term, pairs))
+    for value in got:
+        total = total + value.astype(F32)
+    return total
+
+
+def last_sum(total):
+    b = total.shape[1] // 4
+    terms = lax.optimization_barrier(
+        tuple(total[:, r * b : (r + 1) * b].astype(BF) for r in (1, 2, 3))
+    )
+    return axis_sum(*terms, total[:, :b], WAYS[1])
 
 
 def body(features, conv_one, conv_two, head_vector, owner_of, donor_row, accept_row, score_grad):
@@ -431,10 +437,6 @@
         [accept_pick.reshape(rows_c, N_SEQ, capacity), donor_pick.reshape(rows_c, N_SEQ, capacity)],
         axis=2,
     ).reshape(rows_c, 2 * slots)
-    add = jnp.concatenate(
-        [donor_add.reshape(rows_c, N_SEQ, capacity), accept_add.reshape(rows_c, N_SEQ, capacity)],
-        axis=2,
-    ).reshape(rows_c, 2 * slots)
     gone = lax.dot_general(
         pick, embed, (((0,), (0,)), ((), ())), preferred_element_type=F32
     ).astype(BF)
@@ -446,22 +448,33 @@
     wide_one = windows_of(own, feat_rim, feat_other, rim, taps)
     rim = rim_of(~odd, jnp.where(odd, pool[:2], pool[-2:]), move(outer_two, SIBLING))
     wide_two = windows_of(pool, pool_rim, pool_other, rim, taps)
-    come, wide_one, wide_two, order_one, order_two, add = lax.optimization_barrier(
-        (come, wide_one, wide_two, order_one, order_two, add)
-    )
-    grads, mine_two, theirs_two = head_back(add, come, head_vector[None, :], even_two, odd_two, order_two)
+    come, wide_one, wide_two, order_one, order_two, donor_add, accept_add = (
+        lax.optimization_barrier(
+            (come, wide_one, wide_two, order_one, order_two, donor_add, accept_add)
+        )
+    )
+    come = come.reshape(N_SEQ, 2 * capacity, come.shape[1])
+    grads, mine_two, theirs_two = head_back(
+        donor_add, accept_add, come, head_vector[None, :], even_two, odd_two, order_two
+    )
     grad_rim = rim_of(
         odd, move(jnp.where(odd, grads[:2], grads[-2:]), SIBLING), outer_rim(grads, odd)
     )
-    parts_two = grad_parts(mine_two, move(theirs_two, SIBLING), wide_two)
+    parts_two = grad_parts(mine_two, move(theirs_two, SIBLING), wide_two, 0, taps)
     grads = lax.optimization_barrier((grads, parts_two))[0]
     mine_one, theirs_one = conv_back(
         grads, grad_rim, conv_two, even_one, odd_one, order_one
     )
     got = move(theirs_one, SIBLING)
-    parts_one = grad_parts(mine_one, got, wide_one)
-    grad_two = ring_sums(*parts_two).transpose(1, 0, 2)
-    grad_one = ring_sums(*parts_one).transpose(1, 0, 2)
+    cut = taps // 2 + 1
+    parts_a = grad_parts(mine_one, got, wide_one, 0, cut)
+    mine_one = lax.optimization_barrier((mine_one, parts_a))[0]
+    parts_b = grad_parts(mine_one, got, wide_one, cut, taps - cut)
+    grad_two = last_sum(axis_sum(*parts_two, WAYS[0])).transpose(1, 0, 2)
+    sums_a = axis_sum(*parts_a, WAYS[0])
+    sums_b = axis_sum(*parts_b, WAYS[0])
+    sums = jnp.concatenate([sums_a, sums_b], axis=0)
+    grad_one = last_sum(sums).transpose(1, 0, 2)
     return (grad_one, grad_two)
 
 

time: 201 us -> 194 us (0.965)
  local copies, waits for them, and re-layouts: 15.4 us -> 8.12 us
  waiting for transfers between devices: 37.6 us -> 31 us
  starting transfers between devices: 52.8 us -> 57.5 us
  Pallas kernels: 76.6 us -> 79.1 us
    ppermute x26 -> x25, waiting for transfers between devices: 34.5 us -> 28.3 us  [move(): return lax.ppermute(value, 'seq', pairs)]
    unnamed x44 -> x42, local copies, waits for them, and re-layouts: 11.3 us -> 5.67 us
    ppermute x26 -> x25, starting transfers between devices: 30.7 us -> 35.7 us  [move(): return lax.ppermute(value, 'seq', pairs)]
    pallas_call x2, Pallas kernels: 24.4 us -> 26.6 us  [conv_pool(): pl.pallas_call(functools.partial(conv_kernel, taps), out_shape=[jax.Shape...]
    pallas_call x1, Pallas kernels: 1.89 us -> 3.9 us  [head_back(): pl.pallas_call(head_kernel, out_shape=[jax.ShapeDtypeStruct((2 * n, c), B...]
    pallas_call x2 -> x3, Pallas kernels: 22.5 us -> 20.9 us  [grad_parts(): pl.pallas_call(grad_kernel, grid=(taps,), out_shape=[jax.ShapeDtypeStruct...]
  transfers between devices with their start and end apart: 28 -> 27, of which waited for: 11 -> 9; matrix products, arithmetic and copies ran while one was open for 8% -> 8% of each run, Pallas kernels for 27% -> 22%
where the time goes in v2:
time: 194 us; the launch traced here: 193 us
  Pallas kernels  79.1 us (41%)
  starting transfers between devices  57.5 us (30%)
  waiting for transfers between devices  31 us (16%)
  other arithmetic  12.7 us (7%)
  local copies, waits for them, and re-layouts  8.12 us (4%)
  matrix products  3.75 us (2%)
    ppermute x25, starting transfers between devices, move(): return lax.ppermute(value, 'seq', pairs)  35.7 us
    ppermute x25, waiting for transfers between devices, move(): return lax.ppermute(value, 'seq', pairs)  28.3 us
    pallas_call x2, Pallas kernels, conv_pool(): pl.pallas_call(functools.partial(conv_kernel, taps), out_shape=[jax.Shape...  26.6 us
    pallas_call x3, Pallas kernels, grad_parts(): pl.pallas_call(grad_kernel, grid=(taps,), out_shape=[jax.ShapeDtypeStruct...  20.9 us
    pallas_call x2, Pallas kernels, windows_of(): pl.pallas_call(functools.partial(window_kernel, taps), grid=(2 * n // PIE...  16 us
    all_to_all x1, starting transfers between devices, body(): come = lax.all_to_all(gone, 'seq', split_axis=0, concat_axis=0, tiled=True)  11.9 us
    pallas_call x1, Pallas kernels, conv_back(): pl.pallas_call(functools.partial(back_kernel, taps), out_shape=[jax.Shape...  11.8 us
    all_to_all x1, starting transfers between devices, body(): heard = lax.all_to_all(sent, 'seq', split_axis=0, concat_axis=0, tiled=True)  9.86 us
  transfers between devices with their start and end apart: 27, of which 9 were waited for; matrix products, arithmetic and copies ran while one was open for 8% of the time, Pallas kernels for 22%

profile of v2, /device:TPU:0, one launch (start us, length us, event | category | flops | bytes accessed | tf_op | source)
XLA Modules:
  0.0 193.4 jit_solution(10550598846715262412)
XLA Ops:
  0.7 0.7 broadcast_select_fusion.16
  1.5 1.3 collective-permute-start.1
  2.7 0.7 convert_element_type.106
  4.1 0.9 convert_reduce_fusion
  5.0 0.7 multiply_add_fusion
  6.7 9.9 %all-to-all-start = ((bf16[32,2,16]{2,1,0:T(2,128)(2,1)}), bf16[32,2,16]{2,1,0:T(2,128)(2,1)S(1)}, u32[]{:S(2)}, u32[]{:S(2)}) async-start(bf16[32,2,16]{2,1,0:T(2,128)(2,1)} %copy.14), calls=%async_computation | async-start | bytes 32768 | tf_op jit(solution)/shard_map/all_to_all | solution.py:412
  16.5 1.0 convolution_convert_fusion.2
  17.8 0.7 broadcast_select_fusion.15
  19.1 1.4 copy-done.1
  20.5 14.9 %conv_pool.2 = (bf16[512,896]{1,0:T(8,128)(2,1)S(1)}, f32[512,896]{1,0:T(8,128)}, f32[512,896]{1,0:T(8,128)}) custom-call(bf16[1024,768]{1,0:T(8,128)(2,1)S(1)} %copy-done.1, bf16[32,768]{1,0:T(8,128)(2,1)S(1)} %pad_maximum_fusion.7.rim_ref.own_rim, bf16[5,768,896]{2,1,0:T(8,128)(2,1)} %w_hbm.3), custom_call_target="tpu_custom_call" | custom-call | flops 7046430720 | bytes 13041664 | tf_op jit(solution)/shard_map/conv_pool/pallas_call | solution.py:131
  35.8 0.7 collective-permute-start.3
  36.8 1.2 collective-permute-done.2.other_ref
  38.1 11.7 %conv_pool.3 = (bf16[256,1024]{1,0:T(8,128)(2,1)S(1)}, f32[256,1024]{1,0:T(8,128)}, f32[256,1024]{1,0:T(8,128)}) custom-call(bf16[512,896]{1,0:T(8,128)(2,1)S(1)} %get-tuple-element.53.x_ref.own_ref, bf16[32,896]{1,0:T(8,128)(2,1)S(1)} %pad_maximum_fusion.3.rim_ref.own_rim, bf16[5,896,1024]{2,1,0:T(8,128)(2,1)} %w_hbm.5), custom_call_target="tpu_custom_call" | custom-call | flops 4697620480 | bytes 12713984 | tf_op jit(solution)/shard_map/conv_pool/pallas_call | solution.py:131
  49.8 2.1 %convolution_convert_fusion = bf16[1024,1024]{1,0:T(8,128)(2,1)} fusion(bf16[256,1024]{0,1:T(8,128)(2,1)S(1)} %bitcast.20, bf16[256,1024]{1,0:T(8,128)(2,1)S(1)} %get-tuple-element.49), kind=kOutput, calls=%fused_computation.8 | convolution fusion | flops 537919488 | bytes 3145728 | tf_op jit(solution)/shard_map/dot_general | solution.py:440
  51.9 11.9 %all-to-all-start.1 = ((bf16[32,32,1024]{2,1,0:T(8,128)(2,1)}), bf16[32,32,1024]{2,1,0:T(8,128)(2,1)S(1)}, u32[]{:S(2)}, u32[]{:S(2)}) async-start(bf16[32,32,1024]{2,1,0:T(8,128)(2,1)} %bitcast.19), calls=%async_computation.1 | async-start | bytes 4194304 | tf_op jit(solution)/shard_map/all_to_all | solution.py:443
  64.4 1.5 fusion.1.order_ref
  65.9 1.8 fusion.order_hbm
  68.7 0.8 compare_select_fusion.donor_ref
  70.0 0.7 broadcast_select_fusion.12
  70.7 0.8 pad_maximum_fusion.6.other_rim
  71.6 1.4 copy-done.2
  73.0 1.4 copy-done.4
  74.4 0.8 copy-done.10
  75.2 10.1 %windows.2.wide_ref = bf16[5,2048,768]{2,1,0:T(8,128)(2,1)} custom-call(bf16[1024,768]{1,0:T(8,128)(2,1)S(1)} %copy-done.2, bf16[32,768]{1,0:T(8,128)(2,1)S(1)} %copy-done.10, bf16[1024,768]{1,0:T(8,128)(2,1)S(1)} %copy-done.4, bf16[32,768]{1,0:T(8,128)(2,1)S(1)} %pad_maximum_fusion.6.other_rim), custom_call_target="tpu_custom_call" | custom-call | bytes 18874368 | tf_op jit(solution)/shard_map/windows/pallas_call | solution.py:298
  85.4 5.9 %windows.3.wide_ref = bf16[5,1024,896]{2,1,0:T(8,128)(2,1)} custom-call(bf16[512,896]{1,0:T(8,128)(2,1)S(1)} %get-tuple-element.53.x_ref.own_ref, bf16[32,896]{1,0:T(8,128)(2,1)S(1)} %copy-done.8, bf16[512,896]{1,0:T(8,128)(2,1)S(1)} %copy-done.6, bf16[32,896]{1,0:T(8,128)(2,1)S(1)} %pad_maximum_fusion.2.other_rim), custom_call_target="tpu_custom_call" | custom-call | bytes 11010048 | tf_op jit(solution)/shard_map/windows/pallas_call | solution.py:298
  91.3 2.7 %all-to-all-done.1 = bf16[32,32,1024]{2,1,0:T(8,128)(2,1)S(1)} async-done(((bf16[32,32,1024]{2,1,0:T(8,128)(2,1)}), bf16[32,32,1024]{2,1,0:T(8,128)(2,1)S(1)}, u32[]{:S(2)}, u32[]{:S(2)}) %all-to-all-start.1) | async-done | bytes 2097184 | tf_op jit(solution)/shard_map/all_to_all | solution.py:443
  94.0 3.9 %head_back.1 = (bf16[512,1024]{1,0:T(8,128)(2,1)S(1)}, bf16[512,512]{1,0:T(8,128)(2,1)S(1)}, bf16[512,512]{1,0:T(8,128)(2,1)S(1)}) custom-call(bf16[256,512]{1,0:T(8,128)(2,1)S(1)} %compare_select_fusion.donor_ref, bf16[256,512]{1,0:T(8,128)(2,1)S(1)} %convolution_convert_fusion.1.accept_ref, bf16[32,32,1024]{2,1,0:T(8,128)(2,1)S(1)} %all-to-all-done.1, ...), custom_call_target="tpu_custom_call" | custom-call | flops 1610612736 | bytes 8388608 | tf_op jit(solution)/shard_map/head_back/pallas_call | solution.py:258
  100.0 8.5 %grad_parts.3 = (bf16[5,128,896]{2,1,0:T(8,128)(2,1)S(1)}, bf16[5,128,896]{2,1,0:T(8,128)(2,1)S(1)}, bf16[5,128,896]{2,1,0:T(8,128)(2,1)S(1)}, f32[5,128,896]{2,1,0:T(8,128)S(1)}) custom-call(bf16[512,512]{1,0:T(8,128)(2,1)S(1)} %get-tuple-element.63.mine_ref, bf16[512,512]{1,0:T(8,128)(2,1)S(1)} %collective-permute-done.6.got_ref, ...), custom_call_target="tpu_custom_call" | custom-call | flops 4697620480 | bytes 17104896 | tf_op jit(solution)/shard_map/grad_parts/pallas_call | solution.py:331
  108.5 11.8 %conv_back.1 = (bf16[448,1024]{1,0:T(8,128)(2,1)S(1)}, bf16[448,1024]{1,0:T(8,128)(2,1)S(1)}) custom-call(bf16[512,1024]{1,0:T(8,128)(2,1)S(1)} %get-tuple-element.70.g_ref, bf16[32,1024]{1,0:T(8,128)(2,1)S(1)} %pad_maximum_fusion.10.rim_ref, bf16[5,896,1024]{2,1,0:T(8,128)(2,1)} %w_hbm.5, f32[512,896]{1,0:T(8,128)S(1)} %copy-done.12, ...), custom_call_target="tpu_custom_call" | custom-call | flops 6341787648 | bytes 17334272 | tf_op jit(solution)/shard_map/conv_back/pallas_call | solution.py:200
  120.3 3.7 %collective-permute-start.9 = (bf16[448,1024]{1,0:T(8,128)(2,1)S(1)}, bf16[448,1024]{1,0:T(8,128)(2,1)S(1)}, u32[]{:S(2)}, u32[]{:S(2)}) collective-permute-start(bf16[448,1024]{1,0:T(8,128)(2,1)S(1)} %get-tuple-element.75), channel_id=1, source_target_pairs={{0,4},{4,0},{8,12},{12,8},{16,20},{20,16},{24,28},{28,24},{32,36},... | collective-permute-start | bytes 2752520 | tf_op jit(solution)/shard_map/ppermute | solution.py:41
  124.0 0.7 collective-permute-start.19
  124.7 2.9 %collective-permute-start.20 = (bf16[5,128,896]{2,1,0:T(8,128)(2,1)S(1)}, bf16[5,128,896]{2,1,0:T(8,128)(2,1)S(1)}, u32[]{:S(2)}, u32[]{:S(2)}) collective-permute-start(bf16[5,128,896]{2,1,0:T(8,128)(2,1)S(1)} %get-tuple-element.66), channel_id=1, source_target_pairs={{0,8},{4,36},{8,16},{12,44},{16,24},{20,52},{24,0},{28,60},{32,40}... | collective-permute-start | bytes 3440648 | tf_op jit(solution)/shard_map/ppermute | solution.py:41
  127.9 7.1 %grad_parts.4 = (bf16[3,112,768]{2,1,0:T(8,128)(2,1)S(1)}, bf16[3,112,768]{2,1,0:T(8,128)(2,1)S(1)}, bf16[3,112,768]{2,1,0:T(8,128)(2,1)S(1)}, f32[3,112,768]{2,1,0:T(8,128)S(1)}) custom-call(bf16[448,1024]{1,0:T(8,128)(2,1)S(1)} %get-tuple-element.81.mine_ref, bf16[448,1024]{1,0:T(8,128)(2,1)S(1)} %collective-permute-done.9.got_ref, ...), custom_call_target="tpu_custom_call" | custom-call | flops 4227858432 | bytes 14368768 | tf_op jit(solution)/shard_map/grad_parts/pallas_call | solution.py:331
  135.1 1.8 collective-permute-start.10
  137.1 5.2 %grad_parts.5 = (bf16[2,112,768]{2,1,0:T(8,128)(2,1)S(1)}, bf16[2,112,768]{2,1,0:T(8,128)(2,1)S(1)}, bf16[2,112,768]{2,1,0:T(8,128)(2,1)S(1)}, f32[2,112,768]{2,1,0:T(8,128)S(1)}) custom-call(bf16[448,1024]{1,0:T(8,128)(2,1)S(1)} %get-tuple-element.81.mine_ref, bf16[448,1024]{1,0:T(8,128)(2,1)S(1)} %collective-permute-done.9.got_ref, ...), custom_call_target="tpu_custom_call" | custom-call | flops 2818572288 | bytes 10190848 | tf_op jit(solution)/shard_map/grad_parts/pallas_call | solution.py:331
  142.4 3.9 %collective-permute-start.13 = (bf16[2,112,768]{2,1,0:T(8,128)(2,1)S(1)}, bf16[2,112,768]{2,1,0:T(8,128)(2,1)S(1)}, u32[]{:S(2)}, u32[]{:S(2)}) collective-permute-start(bf16[2,112,768]{2,1,0:T(8,128)(2,1)S(1)} %get-tuple-element.83), channel_id=1, source_target_pairs={{0,16},{4,68},{8,24},{12,76},{16,0},{20,84},{24,8},{28,92},{32,48}... | collective-permute-start | bytes 1032200 | tf_op jit(solution)/shard_map/ppermute | solution.py:41
  146.3 7.4 %collective-permute-done.20 = bf16[5,128,896]{2,1,0:T(8,128)(2,1)S(1)} collective-permute-done((bf16[5,128,896]{2,1,0:T(8,128)(2,1)S(1)}, bf16[5,128,896]{2,1,0:T(8,128)(2,1)S(1)}, u32[]{:S(2)}, u32[]{:S(2)}) %collective-permute-start.20) | collective-permute-done | bytes 1146912 | tf_op jit(solution)/shard_map/ppermute | solution.py:41
  153.8 3.1 %collective-permute-start.15 = (bf16[2,112,768]{2,1,0:T(8,128)(2,1)S(1)}, bf16[2,112,768]{2,1,0:T(8,128)(2,1)S(1)}, u32[]{:S(2)}, u32[]{:S(2)}) collective-permute-start(bf16[2,112,768]{2,1,0:T(8,128)(2,1)S(1)} %get-tuple-element.85), channel_id=1, source_target_pairs={{0,24},{4,100},{8,0},{12,108},{16,8},{20,116},{24,16},{28,124},{32... | collective-permute-start | bytes 1032200 | tf_op jit(solution)/shard_map/ppermute | solution.py:41
  157.4 11.2 %collective-permute-done.13 = bf16[2,112,768]{2,1,0:T(8,128)(2,1)S(1)} collective-permute-done((bf16[2,112,768]{2,1,0:T(8,128)(2,1)S(1)}, bf16[2,112,768]{2,1,0:T(8,128)(2,1)S(1)}, u32[]{:S(2)}, u32[]{:S(2)}) %collective-permute-start.13) | collective-permute-done | bytes 344096 | tf_op jit(solution)/shard_map/ppermute | solution.py:41
  168.7 3.4 %collective-permute-done.14 = bf16[2,112,768]{2,1,0:T(8,128)(2,1)S(1)} collective-permute-done((bf16[2,112,768]{2,1,0:T(8,128)(2,1)S(1)}, bf16[2,112,768]{2,1,0:T(8,128)(2,1)S(1)}, u32[]{:S(2)}, u32[]{:S(2)}) %collective-permute-start.14) | collective-permute-done | bytes 344096 | tf_op jit(solution)/shard_map/ppermute | solution.py:41
  172.1 3.2 %collective-permute-start.22 = (bf16[5,32,896]{2,1,0:T(8,128)(2,1)S(1)}, bf16[5,32,896]{2,1,0:T(8,128)(2,1)S(1)}, u32[]{:S(2)}, u32[]{:S(2)}) collective-permute-start(bf16[5,32,896]{2,1,0:T(8,128)(2,1)S(1)} %get-tuple-element.89), channel_id=1, source_target_pairs={{0,64},{4,20},{8,72},{12,28},{16,80},{20,4},{24,88},{28,12},{32,96... | collective-permute-start | bytes 860168 | tf_op jit(solution)/shard_map/ppermute | solution.py:41
  175.6 3.1 %collective-permute-start.24 = (bf16[5,32,896]{2,1,0:T(8,128)(2,1)S(1)}, bf16[5,32,896]{2,1,0:T(8,128)(2,1)S(1)}, u32[]{:S(2)}, u32[]{:S(2)}) collective-permute-start(bf16[5,32,896]{2,1,0:T(8,128)(2,1)S(1)} %get-tuple-element.91), channel_id=1, source_target_pairs={{0,96},{4,28},{8,104},{12,4},{16,112},{20,12},{24,120},{28,20},{32... | collective-permute-start | bytes 860168 | tf_op jit(solution)/shard_map/ppermute | solution.py:41
  178.7 1.1 collective-permute-done.12
  180.3 4.7 %collective-permute-start.16 = (bf16[5,28,768]{2,1,0:T(8,128)(2,1)S(1)}, bf16[5,28,768]{2,1,0:T(8,128)(2,1)S(1)}, u32[]{:S(2)}, u32[]{:S(2)}) collective-permute-start(bf16[5,28,768]{2,1,0:T(8,128)(2,1)S(1)} %get-tuple-element.86), channel_id=1, source_target_pairs={{0,64},{4,20},{8,72},{12,28},{16,80},{20,4},{24,88},{28,12},{32,96... | collective-permute-start | bytes 645128 | tf_op jit(solution)/shard_map/ppermute | solution.py:41
  185.6 2.7 %collective-permute-start.18 = (bf16[5,28,768]{2,1,0:T(8,128)(2,1)S(1)}, bf16[5,28,768]{2,1,0:T(8,128)(2,1)S(1)}, u32[]{:S(2)}, u32[]{:S(2)}) collective-permute-start(bf16[5,28,768]{2,1,0:T(8,128)(2,1)S(1)} %get-tuple-element.88), channel_id=1, source_target_pairs={{0,96},{4,28},{8,104},{12,4},{16,112},{20,12},{24,120},{28,20},{32... | collective-permute-start | bytes 645128 | tf_op jit(solution)/shard_map/ppermute | solution.py:41
  188.3 0.9 fusion.5
  189.2 3.2 %collective-permute-done.17 = bf16[5,28,768]{2,1,0:T(8,128)(2,1)S(1)} collective-permute-done((bf16[5,28,768]{2,1,0:T(8,128)(2,1)S(1)}, bf16[5,28,768]{2,1,0:T(8,128)(2,1)S(1)}, u32[]{:S(2)}, u32[]{:S(2)}) %collective-permute-start.17) | collective-permute-done | bytes 215072 | tf_op jit(solution)/shard_map/ppermute | solution.py:41
  192.5 0.9 fusion.10
  (105 shorter events, 9.9 us)
Async XLA Ops:
  0.6 17.1 %collective-permute-start = (bf16[1024,768]{1,0:T(8,128)(2,1)}, bf16[1024,768]{1,0:T(8,128)(2,1)S(1)}, u32[]{:S(2)}, u32[]{:S(2)}) collective-permute-start(bf16[1024,768]{1,0:T(8,128)(2,1)} %own_ref), channel_id=1, source_target_pairs={{0,4},{4,0},{8,12},{12,8},{16,20},{20,16},{24,28},{28,24},{32,36},... | collective-permute-start | bytes 4718600 | tf_op jit(solution)/shard_map/ppermute | solution.py:41
  1.5 16.2 %collective-permute-start.1 = (bf16[2,768]{1,0:T(2,128)(2,1)S(1)}, bf16[2,768]{1,0:T(2,128)(2,1)}, u32[]{:S(2)}, u32[]{:S(2)}) collective-permute-start(bf16[2,768]{1,0:T(2,128)(2,1)S(1)} %broadcast_select_fusion.16), channel_id=1, source_target_pairs={{8,4},{16,12},{24,20},{32,28},{40,36},{48,44},{56,52},{64,60},{72,... | collective-permute-start | bytes 9224 | tf_op jit(solution)/shard_map/ppermute | solution.py:41
  6.7 29.8 %all-to-all-start = ((bf16[32,2,16]{2,1,0:T(2,128)(2,1)}), bf16[32,2,16]{2,1,0:T(2,128)(2,1)S(1)}, u32[]{:S(2)}, u32[]{:S(2)}) async-start(bf16[32,2,16]{2,1,0:T(2,128)(2,1)} %copy.14), calls=%async_computation | async-start | bytes 32768 | tf_op jit(solution)/shard_map/all_to_all | solution.py:412
  17.7 17.7 %copy-start.3 = (bf16[1024,768]{1,0:T(8,128)(2,1)}, bf16[1024,768]{1,0:T(8,128)(2,1)S(1)}, u32[]{:S(2)}) copy-start(bf16[1024,768]{1,0:T(8,128)(2,1)S(1)} %collective-permute-done.other_ref) | copy-start | bytes 4718596
  18.5 0.6 copy-start.16
  19.1 1.4 copy-start.1
  20.5 15.0 %copy-start.9 = (bf16[32,768]{1,0:T(8,128)(2,1)}, bf16[32,768]{1,0:T(8,128)(2,1)S(1)}, u32[]{:S(2)}) copy-start(bf16[32,768]{1,0:T(8,128)(2,1)S(1)} %pad_maximum_fusion.7.rim_ref.own_rim) | copy-start | bytes 147460
  35.5 2.6 %collective-permute-start.2 = (bf16[512,896]{1,0:T(8,128)(2,1)S(1)}, bf16[512,896]{1,0:T(8,128)(2,1)S(1)}, u32[]{:S(2)}, u32[]{:S(2)}) collective-permute-start(bf16[512,896]{1,0:T(8,128)(2,1)S(1)} %get-tuple-element.53.x_ref.own_ref), channel_id=1, source_target_pairs={{0,4},{4,0},{8,12},{12,8},{16,20},{20,16},{24,28},{28,24},{32,36},... | collective-permute-start | bytes 2752520 | tf_op jit(solution)/shard_map/ppermute | solution.py:41
  35.8 14.0 %copy-start.17 = (f32[256]{0:T(256)}, f32[256]{0:T(256)S(1)}, u32[]{:S(2)}) copy-start(f32[256]{0:T(256)S(1)} %iota_convert_fusion) | copy-start | bytes 3076
  35.8 1.0 collective-permute-start.3
  36.8 13.0 %copy-start.18 = (bf16[2,896]{1,0:T(2,128)(2,1)}, bf16[2,896]{1,0:T(2,128)(2,1)S(1)}, u32[]{:S(2)}) copy-start(bf16[2,896]{1,0:T(2,128)(2,1)S(1)} %collective-permute-done.3) | copy-start | bytes 10756
  38.0 11.8 %copy-start.5 = (bf16[512,896]{1,0:T(8,128)(2,1)}, bf16[512,896]{1,0:T(8,128)(2,1)S(1)}, u32[]{:S(2)}) copy-start(bf16[512,896]{1,0:T(8,128)(2,1)S(1)} %collective-permute-done.2.other_ref) | copy-start | bytes 2752516
  38.0 11.8 %copy-start.14 = (bf16[14,896]{1,0:T(8,128)(2,1)}, bf16[14,896]{1,0:T(8,128)(2,1)S(1)}, u32[]{:S(2)}) copy-start(bf16[14,896]{1,0:T(8,128)(2,1)S(1)} %broadcast.543) | copy-start | bytes 75268
  38.1 11.7 %copy-start.7 = (bf16[32,896]{1,0:T(8,128)(2,1)}, bf16[32,896]{1,0:T(8,128)(2,1)S(1)}, u32[]{:S(2)}) copy-start(bf16[32,896]{1,0:T(8,128)(2,1)S(1)} %pad_maximum_fusion.3.rim_ref.own_rim) | copy-start | bytes 172036
  51.9 12.1 %copy-start.19 = (s32[256]{0:T(256)S(1)}, s32[256]{0:T(256)}, u32[]{:S(2)}) copy-start(s32[256]{0:T(256)} %param.14) | copy-start | bytes 3076
  51.9 12.1 %copy-start.20 = (bf16[256]{0:T(256)(128)(2,1)S(1)}, bf16[256]{0:T(256)(128)(2,1)}, u32[]{:S(2)}) copy-start(bf16[256]{0:T(256)(128)(2,1)} %param.15) | copy-start | bytes 1540
  51.9 42.0 %all-to-all-start.1 = ((bf16[32,32,1024]{2,1,0:T(8,128)(2,1)}), bf16[32,32,1024]{2,1,0:T(8,128)(2,1)S(1)}, u32[]{:S(2)}, u32[]{:S(2)}) async-start(bf16[32,32,1024]{2,1,0:T(8,128)(2,1)} %bitcast.19), calls=%async_computation.1 | async-start | bytes 4194304 | tf_op jit(solution)/shard_map/all_to_all | solution.py:443
  68.4 1.6 collective-permute-start.4
  69.5 15.8 %collective-permute-start.5 = (bf16[2,896]{1,0:T(2,128)(2,1)}, bf16[2,896]{1,0:T(2,128)(2,1)S(1)}, u32[]{:S(2)}, u32[]{:S(2)}) collective-permute-start(bf16[2,896]{1,0:T(2,128)(2,1)} %copy-done.18), channel_id=1, source_target_pairs={{0,4},{4,0},{8,12},{12,8},{16,20},{20,16},{24,28},{28,24},{32,36},... | collective-permute-start | bytes 10760 | tf_op jit(solution)/shard_map/ppermute | solution.py:41
  71.6 1.4 copy-start.2
  73.0 1.4 copy-start.4
  74.4 0.8 copy-start.10
  75.2 10.1 %copy-start.15 = (bf16[14,896]{1,0:T(8,128)(2,1)S(1)}, bf16[14,896]{1,0:T(8,128)(2,1)}, u32[]{:S(2)}) copy-start(bf16[14,896]{1,0:T(8,128)(2,1)} %copy-done.14) | copy-start | bytes 75268
  75.2 10.1 %copy-start.6 = (bf16[512,896]{1,0:T(8,128)(2,1)S(1)}, bf16[512,896]{1,0:T(8,128)(2,1)}, u32[]{:S(2)}) copy-start(bf16[512,896]{1,0:T(8,128)(2,1)} %copy-done.5) | copy-start | bytes 2752516
  75.2 10.2 %copy-start.8 = (bf16[32,896]{1,0:T(8,128)(2,1)S(1)}, bf16[32,896]{1,0:T(8,128)(2,1)}, u32[]{:S(2)}) copy-start(bf16[32,896]{1,0:T(8,128)(2,1)} %copy-done.7) | copy-start | bytes 172036
  85.3 8.6 %copy-start.11 = (f32[1024]{0:T(1024)S(1)}, f32[1024]{0:T(1024)}, u32[]{:S(2)}) copy-start(f32[1024]{0:T(1024)} %param.11) | copy-start | bytes 12292
  97.9 2.1 %collective-permute-start.6 = (bf16[512,512]{1,0:T(8,128)(2,1)S(1)}, bf16[512,512]{1,0:T(8,128)(2,1)S(1)}, u32[]{:S(2)}, u32[]{:S(2)}) collective-permute-start(bf16[512,512]{1,0:T(8,128)(2,1)S(1)} %get-tuple-element.64), channel_id=1, source_target_pairs={{0,4},{4,0},{8,12},{12,8},{16,20},{20,16},{24,28},{28,24},{32,36},... | collective-permute-start | bytes 1572872 | tf_op jit(solution)/shard_map/ppermute | solution.py:41
  98.0 1.9 collective-permute-start.7
  98.5 1.3 collective-permute-start.8
  99.9 8.6 %copy-start = (bf16[896,896]{1,0:T(8,128)(2,1)S(1)}, bf16[896,896]{1,0:T(8,128)(2,1)}, u32[]{:S(2)}) copy-start(bf16[896,896]{1,0:T(8,128)(2,1)} %fusion.1.order_ref) | copy-start | bytes 4816900
  99.9 8.6 %copy-start.12 = (f32[512,896]{1,0:T(8,128)S(1)}, f32[512,896]{1,0:T(8,128)}, u32[]{:S(2)}) copy-start(f32[512,896]{1,0:T(8,128)} %get-tuple-element.71.even_ref) | copy-start | bytes 5505028
  100.0 8.6 %copy-start.13 = (f32[512,896]{1,0:T(8,128)S(1)}, f32[512,896]{1,0:T(8,128)}, u32[]{:S(2)}) copy-start(f32[512,896]{1,0:T(8,128)} %get-tuple-element.72.odd_ref) | copy-start | bytes 5505028
  120.3 7.6 %collective-permute-start.9 = (bf16[448,1024]{1,0:T(8,128)(2,1)S(1)}, bf16[448,1024]{1,0:T(8,128)(2,1)S(1)}, u32[]{:S(2)}, u32[]{:S(2)}) collective-permute-start(bf16[448,1024]{1,0:T(8,128)(2,1)S(1)} %get-tuple-element.75), channel_id=1, source_target_pairs={{0,4},{4,0},{8,12},{12,8},{16,20},{20,16},{24,28},{28,24},{32,36},... | collective-permute-start | bytes 2752520 | tf_op jit(solution)/shard_map/ppermute | solution.py:41
  124.0 18.4 %collective-permute-start.19 = (bf16[5,128,896]{2,1,0:T(8,128)(2,1)S(1)}, bf16[5,128,896]{2,1,0:T(8,128)(2,1)S(1)}, u32[]{:S(2)}, u32[]{:S(2)}) collective-permute-start(bf16[5,128,896]{2,1,0:T(8,128)(2,1)S(1)} %get-tuple-element.67), channel_id=1, source_target_pairs={{0,16},{4,68},{8,24},{12,76},{16,0},{20,84},{24,8},{28,92},{32,48}... | collective-permute-start | bytes 3440648 | tf_op jit(solution)/shard_map/ppermute | solution.py:41
  124.7 28.9 %collective-permute-start.20 = (bf16[5,128,896]{2,1,0:T(8,128)(2,1)S(1)}, bf16[5,128,896]{2,1,0:T(8,128)(2,1)S(1)}, u32[]{:S(2)}, u32[]{:S(2)}) collective-permute-start(bf16[5,128,896]{2,1,0:T(8,128)(2,1)S(1)} %get-tuple-element.66), channel_id=1, source_target_pairs={{0,8},{4,36},{8,16},{12,44},{16,24},{20,52},{24,0},{28,60},{32,40}... | collective-permute-start | bytes 3440648 | tf_op jit(solution)/shard_map/ppermute | solution.py:41
  127.6 26.2 %collective-permute-start.21 = (bf16[5,128,896]{2,1,0:T(8,128)(2,1)S(1)}, bf16[5,128,896]{2,1,0:T(8,128)(2,1)S(1)}, u32[]{:S(2)}, u32[]{:S(2)}) collective-permute-start(bf16[5,128,896]{2,1,0:T(8,128)(2,1)S(1)} %get-tuple-element.68), channel_id=1, source_target_pairs={{0,24},{4,100},{8,0},{12,108},{16,8},{20,116},{24,16},{28,124},{32... | collective-permute-start | bytes 3440648 | tf_op jit(solution)/shard_map/ppermute | solution.py:41
  135.1 40.6 %collective-permute-start.10 = (bf16[3,112,768]{2,1,0:T(8,128)(2,1)S(1)}, bf16[3,112,768]{2,1,0:T(8,128)(2,1)S(1)}, u32[]{:S(2)}, u32[]{:S(2)}) collective-permute-start(bf16[3,112,768]{2,1,0:T(8,128)(2,1)S(1)} %get-tuple-element.78), channel_id=1, source_target_pairs={{0,16},{4,68},{8,24},{12,76},{16,0},{20,84},{24,8},{28,92},{32,48}... | collective-permute-start | bytes 1548296 | tf_op jit(solution)/shard_map/ppermute | solution.py:41
  136.9 41.9 %collective-permute-start.11 = (bf16[3,112,768]{2,1,0:T(8,128)(2,1)S(1)}, bf16[3,112,768]{2,1,0:T(8,128)(2,1)S(1)}, u32[]{:S(2)}, u32[]{:S(2)}) collective-permute-start(bf16[3,112,768]{2,1,0:T(8,128)(2,1)S(1)} %get-tuple-element.79), channel_id=1, source_target_pairs={{0,8},{4,36},{8,16},{12,44},{16,24},{20,52},{24,0},{28,60},{32,40}... | collective-permute-start | bytes 1548296 | tf_op jit(solution)/shard_map/ppermute | solution.py:41
  142.4 26.2 %collective-permute-start.13 = (bf16[2,112,768]{2,1,0:T(8,128)(2,1)S(1)}, bf16[2,112,768]{2,1,0:T(8,128)(2,1)S(1)}, u32[]{:S(2)}, u32[]{:S(2)}) collective-permute-start(bf16[2,112,768]{2,1,0:T(8,128)(2,1)S(1)} %get-tuple-element.83), channel_id=1, source_target_pairs={{0,16},{4,68},{8,24},{12,76},{16,0},{20,84},{24,8},{28,92},{32,48}... | collective-permute-start | bytes 1032200 | tf_op jit(solution)/shard_map/ppermute | solution.py:41
  153.7 18.4 %collective-permute-start.14 = (bf16[2,112,768]{2,1,0:T(8,128)(2,1)S(1)}, bf16[2,112,768]{2,1,0:T(8,128)(2,1)S(1)}, u32[]{:S(2)}, u32[]{:S(2)}) collective-permute-start(bf16[2,112,768]{2,1,0:T(8,128)(2,1)S(1)} %get-tuple-element.84), channel_id=1, source_target_pairs={{0,8},{4,36},{8,16},{12,44},{16,24},{20,52},{24,0},{28,60},{32,40}... | collective-permute-start | bytes 1032200 | tf_op jit(solution)/shard_map/ppermute | solution.py:41
  153.8 21.5 %collective-permute-start.15 = (bf16[2,112,768]{2,1,0:T(8,128)(2,1)S(1)}, bf16[2,112,768]{2,1,0:T(8,128)(2,1)S(1)}, u32[]{:S(2)}, u32[]{:S(2)}) collective-permute-start(bf16[2,112,768]{2,1,0:T(8,128)(2,1)S(1)} %get-tuple-element.85), channel_id=1, source_target_pairs={{0,24},{4,100},{8,0},{12,108},{16,8},{20,116},{24,16},{28,124},{32... | collective-permute-start | bytes 1032200 | tf_op jit(solution)/shard_map/ppermute | solution.py:41
  168.6 11.3 %collective-permute-start.12 = (bf16[3,112,768]{2,1,0:T(8,128)(2,1)S(1)}, bf16[3,112,768]{2,1,0:T(8,128)(2,1)S(1)}, u32[]{:S(2)}, u32[]{:S(2)}) collective-permute-start(bf16[3,112,768]{2,1,0:T(8,128)(2,1)S(1)} %get-tuple-element.80), channel_id=1, source_target_pairs={{0,24},{4,100},{8,0},{12,108},{16,8},{20,116},{24,16},{28,124},{32... | collective-permute-start | bytes 1548296 | tf_op jit(solution)/shard_map/ppermute | solution.py:41
  172.1 13.6 %collective-permute-start.22 = (bf16[5,32,896]{2,1,0:T(8,128)(2,1)S(1)}, bf16[5,32,896]{2,1,0:T(8,128)(2,1)S(1)}, u32[]{:S(2)}, u32[]{:S(2)}) collective-permute-start(bf16[5,32,896]{2,1,0:T(8,128)(2,1)S(1)} %get-tuple-element.89), channel_id=1, source_target_pairs={{0,64},{4,20},{8,72},{12,28},{16,80},{20,4},{24,88},{28,12},{32,96... | collective-permute-start | bytes 860168 | tf_op jit(solution)/shard_map/ppermute | solution.py:41
  175.3 13.0 %collective-permute-start.23 = (bf16[5,32,896]{2,1,0:T(8,128)(2,1)S(1)}, bf16[5,32,896]{2,1,0:T(8,128)(2,1)S(1)}, u32[]{:S(2)}, u32[]{:S(2)}) collective-permute-start(bf16[5,32,896]{2,1,0:T(8,128)(2,1)S(1)} %get-tuple-element.90), channel_id=1, source_target_pairs={{0,32},{4,12},{8,40},{12,20},{16,48},{20,28},{24,56},{28,4},{32,64... | collective-permute-start | bytes 860168 | tf_op jit(solution)/shard_map/ppermute | solution.py:41
  175.6 12.7 %collective-permute-start.24 = (bf16[5,32,896]{2,1,0:T(8,128)(2,1)S(1)}, bf16[5,32,896]{2,1,0:T(8,128)(2,1)S(1)}, u32[]{:S(2)}, u32[]{:S(2)}) collective-permute-start(bf16[5,32,896]{2,1,0:T(8,128)(2,1)S(1)} %get-tuple-element.91), channel_id=1, source_target_pairs={{0,96},{4,28},{8,104},{12,4},{16,112},{20,12},{24,120},{28,20},{32... | collective-permute-start | bytes 860168 | tf_op jit(solution)/shard_map/ppermute | solution.py:41
  180.3 8.9 %collective-permute-start.16 = (bf16[5,28,768]{2,1,0:T(8,128)(2,1)S(1)}, bf16[5,28,768]{2,1,0:T(8,128)(2,1)S(1)}, u32[]{:S(2)}, u32[]{:S(2)}) collective-permute-start(bf16[5,28,768]{2,1,0:T(8,128)(2,1)S(1)} %get-tuple-element.86), channel_id=1, source_target_pairs={{0,64},{4,20},{8,72},{12,28},{16,80},{20,4},{24,88},{28,12},{32,96... | collective-permute-start | bytes 645128 | tf_op jit(solution)/shard_map/ppermute | solution.py:41
  185.1 7.4 %collective-permute-start.17 = (bf16[5,28,768]{2,1,0:T(8,128)(2,1)S(1)}, bf16[5,28,768]{2,1,0:T(8,128)(2,1)S(1)}, u32[]{:S(2)}, u32[]{:S(2)}) collective-permute-start(bf16[5,28,768]{2,1,0:T(8,128)(2,1)S(1)} %get-tuple-element.87), channel_id=1, source_target_pairs={{0,32},{4,12},{8,40},{12,20},{16,48},{20,28},{24,56},{28,4},{32,64... | collective-permute-start | bytes 645128 | tf_op jit(solution)/shard_map/ppermute | solution.py:41
  185.6 6.8 %collective-permute-start.18 = (bf16[5,28,768]{2,1,0:T(8,128)(2,1)S(1)}, bf16[5,28,768]{2,1,0:T(8,128)(2,1)S(1)}, u32[]{:S(2)}, u32[]{:S(2)}) collective-permute-start(bf16[5,28,768]{2,1,0:T(8,128)(2,1)S(1)} %get-tuple-element.88), channel_id=1, source_target_pairs={{0,96},{4,28},{8,104},{12,4},{16,112},{20,12},{24,120},{28,20},{32... | collective-permute-start | bytes 645128 | tf_op jit(solution)/shard_map/ppermute | solution.py:41

commit v3 on v2

--- a/solution.py
+++ b/solution.py
@@ -80,16 +80,20 @@
 
 
 def conv_kernel(
-    taps, x_ref, rim_ref, w_hbm, pooled_ref, even_hbm, odd_hbm, w_ref, rimmed, piece, wide, acc, slopes, sem, out_sem
+    taps, x_hbm, rim_ref, w_hbm, pooled_ref, even_hbm, odd_hbm, w_ref, rimmed, piece, wide, acc, slopes, sem, out_sem
 ):
-    n, f = x_ref.shape
+    n, f = x_hbm.shape
+    block = pltpu.make_async_copy(x_hbm, rimmed.at[pl.ds(RIM, n)], sem.at[taps])
+    block.start()
     copies = [
         pltpu.make_async_copy(w_hbm.at[k], w_ref.at[pl.ds(k * f, f)], sem.at[k])
         for k in range(taps)
     ]
     for copy in copies:
         copy.start()
-    fill_rims(rimmed, x_ref, rim_ref)
+    rimmed[0:RIM] = rim_ref[0:RIM]
+    rimmed[RIM + n : 2 * RIM + n] = rim_ref[RIM : 2 * RIM]
+    block.wait()
 
     @pl.loop(0, n // PIECE)
     def _(m):
@@ -132,7 +136,7 @@
         functools.partial(conv_kernel, taps),
         out_shape=[jax.ShapeDtypeStruct((n // 2, c), BF)]
         + [pltpu.HBM((n // 2, c), F32)] * 2,
-        in_specs=[IN_VMEM, IN_VMEM, IN_PLACE],
+        in_specs=[IN_PLACE, IN_VMEM, IN_PLACE],
         out_specs=[IN_VMEM] + [pl.BlockSpec(memory_space=pltpu.HBM)] * 2,
         scratch_shapes=[
             VM((taps * f, c), BF),
@@ -141,7 +145,7 @@
             VM((n, taps * f), BF),
             VM((c // LANES, TILE, LANES), F32),
             VM((2, n // 2, c), F32),
-            pltpu.SemaphoreType.DMA((taps,)),
+            pltpu.SemaphoreType.DMA((taps + 1,)),
             pltpu.SemaphoreType.DMA((2, n // TILE)),
         ],
         compiler_params=params(),
@@ -410,6 +414,15 @@
     sent = jnp.dot(told, placed, preferred_element_type=F32).astype(BF)
     sent = sent.reshape(2, N_SEQ, capacity).transpose(1, 0, 2)
     heard = lax.all_to_all(sent, "seq", split_axis=0, concat_axis=0, tiled=True)
+    order_one = order_matrix(conv_one.shape[2], seq)
+    order_two = order_matrix(conv_two.shape[2], seq)
+
+    pooled, even_one, odd_one = conv_pool(in_hbm(features), feat_rim, conv_one)
+    pool_outer = outer_rim(pooled, odd)
+    pool_other = move(pooled, SIBLING)
+    pool_rim = rim_of(odd, jnp.where(odd, pool_other[-2:], pool_other[:2]), pool_outer)
+    embed, even_two, odd_two = conv_pool(pooled, pool_rim, conv_two)
+    heard, placed, _ = lax.optimization_barrier((heard, placed, pooled))
     accepts = (
         accept_row[None, :] == lax.broadcasted_iota(jnp.int32, (rows_c, records), 0)
     ).astype(BF)
@@ -418,15 +431,6 @@
         accepts * score_grad[None, :], placed, preferred_element_type=F32
     ).astype(BF)
 
-    order_one = order_matrix(conv_one.shape[2], seq)
-    order_two = order_matrix(conv_two.shape[2], seq)
-
-    pooled, even_one, odd_one = conv_pool(features, feat_rim, conv_one)
-    pool_outer = outer_rim(pooled, odd)
-    pool_other = move(pooled, SIBLING)
-    pool_rim = rim_of(odd, jnp.where(odd, pool_other[-2:], pool_other[:2]), pool_outer)
-    embed, even_two, odd_two = conv_pool(pooled, pool_rim, conv_two)
-    heard = lax.optimization_barrier((heard, pooled))[0]
     heard = heard.transpose(1, 0, 2).reshape(2, slots)
     donor_hit = heard[0:1].astype(F32) == lax.broadcasted_iota(
         jnp.int32, (rows_c, slots), 0

time: 194 us -> 193 us (level)
    unnamed x42 -> x40, local copies, waits for them, and re-layouts: 5.67 us -> 4.36 us
  transfers between devices with their start and end apart: 27 -> 27, of which waited for: 9 -> 10; matrix products, arithmetic and copies ran while one was open for 8% -> 8% of each run, Pallas kernels for 22% -> 23%
where the time goes in v3:
time: 193 us; the launch traced here: 192 us
  Pallas kernels  79.4 us (41%)
  starting transfers between devices  58.6 us (30%)
  waiting for transfers between devices  30.1 us (16%)
  other arithmetic  12.2 us (6%)
  local copies, waits for them, and re-layouts  6.87 us (4%)
  matrix products  3.49 us (2%)
    ppermute x25, starting transfers between devices, move(): return lax.ppermute(value, 'seq', pairs)  35.8 us
    ppermute x25, waiting for transfers between devices, move(): return lax.ppermute(value, 'seq', pairs)  28 us
    pallas_call x2, Pallas kernels, conv_pool(): pl.pallas_call(functools.partial(conv_kernel, taps), out_shape=[jax.Shape...  27 us
    pallas_call x3, Pallas kernels, grad_parts(): pl.pallas_call(grad_kernel, grid=(taps,), out_shape=[jax.ShapeDtypeStruct...  20.9 us
    pallas_call x2, Pallas kernels, windows_of(): pl.pallas_call(functools.partial(window_kernel, taps), grid=(2 * n // PIE...  15.9 us
    all_to_all x1, starting transfers between devices, body(): come = lax.all_to_all(gone, 'seq', split_axis=0, concat_axis=0, tiled=True)  12.3 us
    pallas_call x1, Pallas kernels, conv_back(): pl.pallas_call(functools.partial(back_kernel, taps), out_shape=[jax.Shape...  11.8 us
    all_to_all x1, starting transfers between devices, body(): heard = lax.all_to_all(sent, 'seq', split_axis=0, concat_axis=0, tiled=True)  10.4 us
  transfers between devices with their start and end apart: 27, of which 10 were waited for; matrix products, arithmetic and copies ran while one was open for 8% of the time, Pallas kernels for 23%

profile of v3, /device:TPU:0, one launch (start us, length us, event | category | flops | bytes accessed | tf_op | source)
XLA Modules:
  0.0 191.9 jit_solution(6466016184560626459)
XLA Ops:
  0.7 0.7 broadcast_select_fusion.16
  1.5 0.7 collective-permute-start.1
  2.1 0.7 convert_element_type.106
  3.5 0.9 convert_reduce_fusion
  4.4 0.7 multiply_add_fusion
  6.1 10.4 %all-to-all-start = ((bf16[32,2,16]{2,1,0:T(2,128)(2,1)}), bf16[32,2,16]{2,1,0:T(2,128)(2,1)S(1)}, u32[]{:S(2)}, u32[]{:S(2)}) async-start(bf16[32,2,16]{2,1,0:T(2,128)(2,1)} %copy.13), calls=%async_computation | async-start | bytes 32768 | tf_op jit(solution)/shard_map/all_to_all | solution.py:416
  16.8 0.7 copy-done.15
  17.5 15.4 %conv_pool.2 = (bf16[512,896]{1,0:T(8,128)(2,1)S(1)}, f32[512,896]{1,0:T(8,128)}, f32[512,896]{1,0:T(8,128)}) custom-call(bf16[1024,768]{1,0:T(8,128)(2,1)} %own_ref, bf16[32,768]{1,0:T(8,128)(2,1)S(1)} %pad_maximum_fusion.7.rim_ref.own_rim, bf16[5,768,896]{2,1,0:T(8,128)(2,1)} %w_hbm.3), custom_call_target="tpu_custom_call" | custom-call | flops 7046430720 | bytes 13041664 | tf_op jit(solution)/shard_map/conv_pool/pallas_call | solution.py:135
  34.6 0.8 collective-permute-done.2.other_ref
  35.5 11.6 %conv_pool.3 = (bf16[256,1024]{1,0:T(8,128)(2,1)S(1)}, f32[256,1024]{1,0:T(8,128)}, f32[256,1024]{1,0:T(8,128)}) custom-call(bf16[512,896]{1,0:T(8,128)(2,1)S(1)} %get-tuple-element.55.x_hbm.own_ref, bf16[32,896]{1,0:T(8,128)(2,1)S(1)} %pad_maximum_fusion.3.rim_ref.own_rim, bf16[5,896,1024]{2,1,0:T(8,128)(2,1)} %w_hbm.5), custom_call_target="tpu_custom_call" | custom-call | flops 4697620480 | bytes 12713984 | tf_op jit(solution)/shard_map/conv_pool/pallas_call | solution.py:135
  47.2 2.1 %convolution_convert_fusion = bf16[1024,1024]{1,0:T(8,128)(2,1)} fusion(bf16[256,1024]{0,1:T(8,128)(2,1)S(1)} %bitcast.22, bf16[256,1024]{1,0:T(8,128)(2,1)S(1)} %get-tuple-element.51), kind=kOutput, calls=%fused_computation.8 | convolution fusion | flops 537919488 | bytes 3145728 | tf_op jit(solution)/shard_map/dot_general | solution.py:444
  49.3 12.3 %all-to-all-start.1 = ((bf16[32,32,1024]{2,1,0:T(8,128)(2,1)}), bf16[32,32,1024]{2,1,0:T(8,128)(2,1)S(1)}, u32[]{:S(2)}, u32[]{:S(2)}) async-start(bf16[32,32,1024]{2,1,0:T(8,128)(2,1)} %bitcast.21), calls=%async_computation.1 | async-start | bytes 4194304 | tf_op jit(solution)/shard_map/all_to_all | solution.py:447
  61.7 1.5 fusion.1.order_ref
  63.2 1.8 fusion.order_hbm
  65.0 0.7 broadcast_in_dim.46
  65.8 0.9 convolution_convert_fusion.1.accept_ref
  67.0 0.8 compare_select_fusion.donor_ref
  68.4 0.7 broadcast_select_fusion.12
  69.1 0.8 pad_maximum_fusion.6.other_rim
  70.0 1.4 copy-done.1
  71.4 1.4 copy-done.3
  72.8 0.8 copy-done.9
  73.6 10.1 %windows.2.wide_ref = bf16[5,2048,768]{2,1,0:T(8,128)(2,1)} custom-call(bf16[1024,768]{1,0:T(8,128)(2,1)S(1)} %copy-done.1, bf16[32,768]{1,0:T(8,128)(2,1)S(1)} %copy-done.9, bf16[1024,768]{1,0:T(8,128)(2,1)S(1)} %copy-done.3, bf16[32,768]{1,0:T(8,128)(2,1)S(1)} %pad_maximum_fusion.6.other_rim), custom_call_target="tpu_custom_call" | custom-call | bytes 18874368 | tf_op jit(solution)/shard_map/windows/pallas_call | solution.py:302
  83.7 5.9 %windows.3.wide_ref = bf16[5,1024,896]{2,1,0:T(8,128)(2,1)} custom-call(bf16[512,896]{1,0:T(8,128)(2,1)S(1)} %get-tuple-element.55.x_hbm.own_ref, bf16[32,896]{1,0:T(8,128)(2,1)S(1)} %copy-done.7, bf16[512,896]{1,0:T(8,128)(2,1)S(1)} %copy-done.5, bf16[32,896]{1,0:T(8,128)(2,1)S(1)} %pad_maximum_fusion.2.other_rim), custom_call_target="tpu_custom_call" | custom-call | bytes 11010048 | tf_op jit(solution)/shard_map/windows/pallas_call | solution.py:302
  89.6 2.1 %all-to-all-done.1 = bf16[32,32,1024]{2,1,0:T(8,128)(2,1)S(1)} async-done(((bf16[32,32,1024]{2,1,0:T(8,128)(2,1)}), bf16[32,32,1024]{2,1,0:T(8,128)(2,1)S(1)}, u32[]{:S(2)}, u32[]{:S(2)}) %all-to-all-start.1) | async-done | bytes 2097184 | tf_op jit(solution)/shard_map/all_to_all | solution.py:447
  91.7 3.9 %head_back.1 = (bf16[512,1024]{1,0:T(8,128)(2,1)S(1)}, bf16[512,512]{1,0:T(8,128)(2,1)S(1)}, bf16[512,512]{1,0:T(8,128)(2,1)S(1)}) custom-call(bf16[256,512]{1,0:T(8,128)(2,1)S(1)} %compare_select_fusion.donor_ref, bf16[256,512]{1,0:T(8,128)(2,1)S(1)} %convolution_convert_fusion.1.accept_ref, bf16[32,32,1024]{2,1,0:T(8,128)(2,1)S(1)} %all-to-all-done.1, ...), custom_call_target="tpu_custom_call" | custom-call | flops 1610612736 | bytes 8388608 | tf_op jit(solution)/shard_map/head_back/pallas_call | solution.py:262
  97.7 8.5 %grad_parts.3 = (bf16[5,128,896]{2,1,0:T(8,128)(2,1)S(1)}, bf16[5,128,896]{2,1,0:T(8,128)(2,1)S(1)}, bf16[5,128,896]{2,1,0:T(8,128)(2,1)S(1)}, f32[5,128,896]{2,1,0:T(8,128)S(1)}) custom-call(bf16[512,512]{1,0:T(8,128)(2,1)S(1)} %get-tuple-element.65.mine_ref, bf16[512,512]{1,0:T(8,128)(2,1)S(1)} %collective-permute-done.6.got_ref, ...), custom_call_target="tpu_custom_call" | custom-call | flops 4697620480 | bytes 17104896 | tf_op jit(solution)/shard_map/grad_parts/pallas_call | solution.py:335
  106.2 11.8 %conv_back.1 = (bf16[448,1024]{1,0:T(8,128)(2,1)S(1)}, bf16[448,1024]{1,0:T(8,128)(2,1)S(1)}) custom-call(bf16[512,1024]{1,0:T(8,128)(2,1)S(1)} %get-tuple-element.72.g_ref, bf16[32,1024]{1,0:T(8,128)(2,1)S(1)} %pad_maximum_fusion.10.rim_ref, bf16[5,896,1024]{2,1,0:T(8,128)(2,1)} %w_hbm.5, f32[512,896]{1,0:T(8,128)S(1)} %copy-done.11, ...), custom_call_target="tpu_custom_call" | custom-call | flops 6341787648 | bytes 17334272 | tf_op jit(solution)/shard_map/conv_back/pallas_call | solution.py:204
  118.0 3.7 %collective-permute-start.9 = (bf16[448,1024]{1,0:T(8,128)(2,1)S(1)}, bf16[448,1024]{1,0:T(8,128)(2,1)S(1)}, u32[]{:S(2)}, u32[]{:S(2)}) collective-permute-start(bf16[448,1024]{1,0:T(8,128)(2,1)S(1)} %get-tuple-element.77), channel_id=1, source_target_pairs={{0,4},{4,0},{8,12},{12,8},{16,20},{20,16},{24,28},{28,24},{32,36},... | collective-permute-start | bytes 2752520 | tf_op jit(solution)/shard_map/ppermute | solution.py:41
  121.7 1.3 collective-permute-start.19
  123.0 2.7 %collective-permute-start.20 = (bf16[5,128,896]{2,1,0:T(8,128)(2,1)S(1)}, bf16[5,128,896]{2,1,0:T(8,128)(2,1)S(1)}, u32[]{:S(2)}, u32[]{:S(2)}) collective-permute-start(bf16[5,128,896]{2,1,0:T(8,128)(2,1)S(1)} %get-tuple-element.68), channel_id=1, source_target_pairs={{0,8},{4,36},{8,16},{12,44},{16,24},{20,52},{24,0},{28,60},{32,40}... | collective-permute-start | bytes 3440648 | tf_op jit(solution)/shard_map/ppermute | solution.py:41
  126.3 7.1 %grad_parts.4 = (bf16[3,112,768]{2,1,0:T(8,128)(2,1)S(1)}, bf16[3,112,768]{2,1,0:T(8,128)(2,1)S(1)}, bf16[3,112,768]{2,1,0:T(8,128)(2,1)S(1)}, f32[3,112,768]{2,1,0:T(8,128)S(1)}) custom-call(bf16[448,1024]{1,0:T(8,128)(2,1)S(1)} %get-tuple-element.83.mine_ref, bf16[448,1024]{1,0:T(8,128)(2,1)S(1)} %collective-permute-done.9.got_ref, ...), custom_call_target="tpu_custom_call" | custom-call | flops 4227858432 | bytes 14368768 | tf_op jit(solution)/shard_map/grad_parts/pallas_call | solution.py:335
  133.4 1.6 collective-permute-start.10
  135.2 5.2 %grad_parts.5 = (bf16[2,112,768]{2,1,0:T(8,128)(2,1)S(1)}, bf16[2,112,768]{2,1,0:T(8,128)(2,1)S(1)}, bf16[2,112,768]{2,1,0:T(8,128)(2,1)S(1)}, f32[2,112,768]{2,1,0:T(8,128)S(1)}) custom-call(bf16[448,1024]{1,0:T(8,128)(2,1)S(1)} %get-tuple-element.83.mine_ref, bf16[448,1024]{1,0:T(8,128)(2,1)S(1)} %collective-permute-done.9.got_ref, ...), custom_call_target="tpu_custom_call" | custom-call | flops 2818572288 | bytes 10190848 | tf_op jit(solution)/shard_map/grad_parts/pallas_call | solution.py:335
  140.5 3.9 %collective-permute-start.13 = (bf16[2,112,768]{2,1,0:T(8,128)(2,1)S(1)}, bf16[2,112,768]{2,1,0:T(8,128)(2,1)S(1)}, u32[]{:S(2)}, u32[]{:S(2)}) collective-permute-start(bf16[2,112,768]{2,1,0:T(8,128)(2,1)S(1)} %get-tuple-element.85), channel_id=1, source_target_pairs={{0,16},{4,68},{8,24},{12,76},{16,0},{20,84},{24,8},{28,92},{32,48}... | collective-permute-start | bytes 1032200 | tf_op jit(solution)/shard_map/ppermute | solution.py:41
  144.4 7.0 %collective-permute-done.20 = bf16[5,128,896]{2,1,0:T(8,128)(2,1)S(1)} collective-permute-done((bf16[5,128,896]{2,1,0:T(8,128)(2,1)S(1)}, bf16[5,128,896]{2,1,0:T(8,128)(2,1)S(1)}, u32[]{:S(2)}, u32[]{:S(2)}) %collective-permute-start.20) | collective-permute-done | bytes 1146912 | tf_op jit(solution)/shard_map/ppermute | solution.py:41
  151.9 2.7 %collective-permute-start.15 = (bf16[2,112,768]{2,1,0:T(8,128)(2,1)S(1)}, bf16[2,112,768]{2,1,0:T(8,128)(2,1)S(1)}, u32[]{:S(2)}, u32[]{:S(2)}) collective-permute-start(bf16[2,112,768]{2,1,0:T(8,128)(2,1)S(1)} %get-tuple-element.87), channel_id=1, source_target_pairs={{0,24},{4,100},{8,0},{12,108},{16,8},{20,116},{24,16},{28,124},{32... | collective-permute-start | bytes 1032200 | tf_op jit(solution)/shard_map/ppermute | solution.py:41
  155.1 11.2 %collective-permute-done.13 = bf16[2,112,768]{2,1,0:T(8,128)(2,1)S(1)} collective-permute-done((bf16[2,112,768]{2,1,0:T(8,128)(2,1)S(1)}, bf16[2,112,768]{2,1,0:T(8,128)(2,1)S(1)}, u32[]{:S(2)}, u32[]{:S(2)}) %collective-permute-start.13) | collective-permute-done | bytes 344096 | tf_op jit(solution)/shard_map/ppermute | solution.py:41
  166.4 3.4 %collective-permute-done.14 = bf16[2,112,768]{2,1,0:T(8,128)(2,1)S(1)} collective-permute-done((bf16[2,112,768]{2,1,0:T(8,128)(2,1)S(1)}, bf16[2,112,768]{2,1,0:T(8,128)(2,1)S(1)}, u32[]{:S(2)}, u32[]{:S(2)}) %collective-permute-start.14) | collective-permute-done | bytes 344096 | tf_op jit(solution)/shard_map/ppermute | solution.py:41
  169.8 3.4 %collective-permute-start.22 = (bf16[5,32,896]{2,1,0:T(8,128)(2,1)S(1)}, bf16[5,32,896]{2,1,0:T(8,128)(2,1)S(1)}, u32[]{:S(2)}, u32[]{:S(2)}) collective-permute-start(bf16[5,32,896]{2,1,0:T(8,128)(2,1)S(1)} %get-tuple-element.91), channel_id=1, source_target_pairs={{0,64},{4,20},{8,72},{12,28},{16,80},{20,4},{24,88},{28,12},{32,96... | collective-permute-start | bytes 860168 | tf_op jit(solution)/shard_map/ppermute | solution.py:41
  174.0 2.7 %collective-permute-start.24 = (bf16[5,32,896]{2,1,0:T(8,128)(2,1)S(1)}, bf16[5,32,896]{2,1,0:T(8,128)(2,1)S(1)}, u32[]{:S(2)}, u32[]{:S(2)}) collective-permute-start(bf16[5,32,896]{2,1,0:T(8,128)(2,1)S(1)} %get-tuple-element.93), channel_id=1, source_target_pairs={{0,96},{4,28},{8,104},{12,4},{16,112},{20,12},{24,120},{28,20},{32... | collective-permute-start | bytes 860168 | tf_op jit(solution)/shard_map/ppermute | solution.py:41
  177.6 5.2 %collective-permute-start.16 = (bf16[5,28,768]{2,1,0:T(8,128)(2,1)S(1)}, bf16[5,28,768]{2,1,0:T(8,128)(2,1)S(1)}, u32[]{:S(2)}, u32[]{:S(2)}) collective-permute-start(bf16[5,28,768]{2,1,0:T(8,128)(2,1)S(1)} %get-tuple-element.88), channel_id=1, source_target_pairs={{0,64},{4,20},{8,72},{12,28},{16,80},{20,4},{24,88},{28,12},{32,96... | collective-permute-start | bytes 645128 | tf_op jit(solution)/shard_map/ppermute | solution.py:41
  182.8 1.4 collective-permute-start.17
  184.2 1.9 collective-permute-start.18
  186.1 0.9 fusion.5
  187.0 3.2 %collective-permute-done.17 = bf16[5,28,768]{2,1,0:T(8,128)(2,1)S(1)} collective-permute-done((bf16[5,28,768]{2,1,0:T(8,128)(2,1)S(1)}, bf16[5,28,768]{2,1,0:T(8,128)(2,1)S(1)}, u32[]{:S(2)}, u32[]{:S(2)}) %collective-permute-start.17) | collective-permute-done | bytes 215072 | tf_op jit(solution)/shard_map/ppermute | solution.py:41
  190.2 0.8 collective-permute-done.18
  191.0 0.9 fusion.11
  (104 shorter events, 10.4 us)
Async XLA Ops:
  0.6 16.1 %collective-permute-start = (bf16[1024,768]{1,0:T(8,128)(2,1)}, bf16[1024,768]{1,0:T(8,128)(2,1)S(1)}, u32[]{:S(2)}, u32[]{:S(2)}) collective-permute-start(bf16[1024,768]{1,0:T(8,128)(2,1)} %own_ref), channel_id=1, source_target_pairs={{0,4},{4,0},{8,12},{12,8},{16,20},{20,16},{24,28},{28,24},{32,36},... | collective-permute-start | bytes 4718600 | tf_op jit(solution)/shard_map/ppermute | solution.py:41
  1.5 15.2 %collective-permute-start.1 = (bf16[2,768]{1,0:T(2,128)(2,1)S(1)}, bf16[2,768]{1,0:T(2,128)(2,1)S(1)}, u32[]{:S(2)}, u32[]{:S(2)}) collective-permute-start(bf16[2,768]{1,0:T(2,128)(2,1)S(1)} %broadcast_select_fusion.16), channel_id=1, source_target_pairs={{8,4},{16,12},{24,20},{32,28},{40,36},{48,44},{56,52},{64,60},{72,... | collective-permute-start | bytes 9224 | tf_op jit(solution)/shard_map/ppermute | solution.py:41
  6.1 27.8 %all-to-all-start = ((bf16[32,2,16]{2,1,0:T(2,128)(2,1)}), bf16[32,2,16]{2,1,0:T(2,128)(2,1)S(1)}, u32[]{:S(2)}, u32[]{:S(2)}) async-start(bf16[32,2,16]{2,1,0:T(2,128)(2,1)} %copy.13), calls=%async_computation | async-start | bytes 32768 | tf_op jit(solution)/shard_map/all_to_all | solution.py:416
  16.7 17.7 %copy-start.16 = (f32[256]{0:T(256)}, f32[256]{0:T(256)S(1)}, u32[]{:S(2)}) copy-start(f32[256]{0:T(256)S(1)} %iota_convert_fusion) | copy-start | bytes 3076
  16.7 16.2 %copy-start.18 = (bf16[2,768]{1,0:T(2,128)(2,1)}, bf16[2,768]{1,0:T(2,128)(2,1)S(1)}, u32[]{:S(2)}) copy-start(bf16[2,768]{1,0:T(2,128)(2,1)S(1)} %collective-permute-done.1) | copy-start | bytes 9220
  16.7 16.2 %copy-start.2 = (bf16[1024,768]{1,0:T(8,128)(2,1)}, bf16[1024,768]{1,0:T(8,128)(2,1)S(1)}, u32[]{:S(2)}) copy-start(bf16[1024,768]{1,0:T(8,128)(2,1)S(1)} %collective-permute-done.other_ref) | copy-start | bytes 4718596
  16.8 0.7 copy-start.15
  17.5 15.4 %copy-start.8 = (bf16[32,768]{1,0:T(8,128)(2,1)}, bf16[32,768]{1,0:T(8,128)(2,1)S(1)}, u32[]{:S(2)}) copy-start(bf16[32,768]{1,0:T(8,128)(2,1)S(1)} %pad_maximum_fusion.7.rim_ref.own_rim) | copy-start | bytes 147460
  17.5 16.5 %copy-start.19 = (s32[256]{0:T(256)S(1)}, s32[256]{0:T(256)}, u32[]{:S(2)}) copy-start(s32[256]{0:T(256)} %param.14) | copy-start | bytes 3076
  32.9 2.6 %collective-permute-start.2 = (bf16[512,896]{1,0:T(8,128)(2,1)S(1)}, bf16[512,896]{1,0:T(8,128)(2,1)S(1)}, u32[]{:S(2)}, u32[]{:S(2)}) collective-permute-start(bf16[512,896]{1,0:T(8,128)(2,1)S(1)} %get-tuple-element.55.x_hbm.own_ref), channel_id=1, source_target_pairs={{0,4},{4,0},{8,12},{12,8},{16,20},{20,16},{24,28},{28,24},{32,36},... | collective-permute-start | bytes 2752520 | tf_op jit(solution)/shard_map/ppermute | solution.py:41
  33.3 1.4 collective-permute-start.3
  34.6 0.8 copy-start.17
  35.4 11.7 %copy-start.4 = (bf16[512,896]{1,0:T(8,128)(2,1)}, bf16[512,896]{1,0:T(8,128)(2,1)S(1)}, u32[]{:S(2)}) copy-start(bf16[512,896]{1,0:T(8,128)(2,1)S(1)} %collective-permute-done.2.other_ref) | copy-start | bytes 2752516
  35.5 11.7 %copy-start.13 = (bf16[14,896]{1,0:T(8,128)(2,1)}, bf16[14,896]{1,0:T(8,128)(2,1)S(1)}, u32[]{:S(2)}) copy-start(bf16[14,896]{1,0:T(8,128)(2,1)S(1)} %broadcast.543) | copy-start | bytes 75268
  35.5 11.6 %copy-start.6 = (bf16[32,896]{1,0:T(8,128)(2,1)}, bf16[32,896]{1,0:T(8,128)(2,1)S(1)}, u32[]{:S(2)}) copy-start(bf16[32,896]{1,0:T(8,128)(2,1)S(1)} %pad_maximum_fusion.3.rim_ref.own_rim) | copy-start | bytes 172036
  49.3 42.4 %all-to-all-start.1 = ((bf16[32,32,1024]{2,1,0:T(8,128)(2,1)}), bf16[32,32,1024]{2,1,0:T(8,128)(2,1)S(1)}, u32[]{:S(2)}, u32[]{:S(2)}) async-start(bf16[32,32,1024]{2,1,0:T(8,128)(2,1)} %bitcast.21), calls=%async_computation.1 | async-start | bytes 4194304 | tf_op jit(solution)/shard_map/all_to_all | solution.py:447
  66.7 1.7 collective-permute-start.4
  67.9 15.8 %collective-permute-start.5 = (bf16[2,896]{1,0:T(2,128)(2,1)}, bf16[2,896]{1,0:T(2,128)(2,1)S(1)}, u32[]{:S(2)}, u32[]{:S(2)}) collective-permute-start(bf16[2,896]{1,0:T(2,128)(2,1)} %copy-done.17), channel_id=1, source_target_pairs={{0,4},{4,0},{8,12},{12,8},{16,20},{20,16},{24,28},{28,24},{32,36},... | collective-permute-start | bytes 10760 | tf_op jit(solution)/shard_map/ppermute | solution.py:41
  69.9 1.4 copy-start.1
  71.4 1.4 copy-start.3
  72.8 0.8 copy-start.9
  73.6 10.1 %copy-start.14 = (bf16[14,896]{1,0:T(8,128)(2,1)S(1)}, bf16[14,896]{1,0:T(8,128)(2,1)}, u32[]{:S(2)}) copy-start(bf16[14,896]{1,0:T(8,128)(2,1)} %copy-done.13) | copy-start | bytes 75268
  73.6 10.1 %copy-start.5 = (bf16[512,896]{1,0:T(8,128)(2,1)S(1)}, bf16[512,896]{1,0:T(8,128)(2,1)}, u32[]{:S(2)}) copy-start(bf16[512,896]{1,0:T(8,128)(2,1)} %copy-done.4) | copy-start | bytes 2752516
  73.6 10.1 %copy-start.7 = (bf16[32,896]{1,0:T(8,128)(2,1)S(1)}, bf16[32,896]{1,0:T(8,128)(2,1)}, u32[]{:S(2)}) copy-start(bf16[32,896]{1,0:T(8,128)(2,1)} %copy-done.6) | copy-start | bytes 172036
  83.7 7.9 %copy-start.10 = (f32[1024]{0:T(1024)S(1)}, f32[1024]{0:T(1024)}, u32[]{:S(2)}) copy-start(f32[1024]{0:T(1024)} %param.11) | copy-start | bytes 12292
  95.6 2.1 %collective-permute-start.6 = (bf16[512,512]{1,0:T(8,128)(2,1)S(1)}, bf16[512,512]{1,0:T(8,128)(2,1)S(1)}, u32[]{:S(2)}, u32[]{:S(2)}) collective-permute-start(bf16[512,512]{1,0:T(8,128)(2,1)S(1)} %get-tuple-element.66), channel_id=1, source_target_pairs={{0,4},{4,0},{8,12},{12,8},{16,20},{20,16},{24,28},{28,24},{32,36},... | collective-permute-start | bytes 1572872 | tf_op jit(solution)/shard_map/ppermute | solution.py:41
  95.7 1.9 collective-permute-start.7
  96.2 1.3 collective-permute-start.8
  97.6 8.6 %copy-start = (bf16[896,896]{1,0:T(8,128)(2,1)S(1)}, bf16[896,896]{1,0:T(8,128)(2,1)}, u32[]{:S(2)}) copy-start(bf16[896,896]{1,0:T(8,128)(2,1)} %fusion.1.order_ref) | copy-start | bytes 4816900
  97.6 8.6 %copy-start.11 = (f32[512,896]{1,0:T(8,128)S(1)}, f32[512,896]{1,0:T(8,128)}, u32[]{:S(2)}) copy-start(f32[512,896]{1,0:T(8,128)} %get-tuple-element.73.even_ref) | copy-start | bytes 5505028
  97.7 8.6 %copy-start.12 = (f32[512,896]{1,0:T(8,128)S(1)}, f32[512,896]{1,0:T(8,128)}, u32[]{:S(2)}) copy-start(f32[512,896]{1,0:T(8,128)} %get-tuple-element.74.odd_ref) | copy-start | bytes 5505028
  118.0 8.3 %collective-permute-start.9 = (bf16[448,1024]{1,0:T(8,128)(2,1)S(1)}, bf16[448,1024]{1,0:T(8,128)(2,1)S(1)}, u32[]{:S(2)}, u32[]{:S(2)}) collective-permute-start(bf16[448,1024]{1,0:T(8,128)(2,1)S(1)} %get-tuple-element.77), channel_id=1, source_target_pairs={{0,4},{4,0},{8,12},{12,8},{16,20},{20,16},{24,28},{28,24},{32,36},... | collective-permute-start | bytes 2752520 | tf_op jit(solution)/shard_map/ppermute | solution.py:41
  121.7 18.8 %collective-permute-start.19 = (bf16[5,128,896]{2,1,0:T(8,128)(2,1)S(1)}, bf16[5,128,896]{2,1,0:T(8,128)(2,1)S(1)}, u32[]{:S(2)}, u32[]{:S(2)}) collective-permute-start(bf16[5,128,896]{2,1,0:T(8,128)(2,1)S(1)} %get-tuple-element.69), channel_id=1, source_target_pairs={{0,16},{4,68},{8,24},{12,76},{16,0},{20,84},{24,8},{28,92},{32,48}... | collective-permute-start | bytes 3440648 | tf_op jit(solution)/shard_map/ppermute | solution.py:41
  123.0 28.3 %collective-permute-start.20 = (bf16[5,128,896]{2,1,0:T(8,128)(2,1)S(1)}, bf16[5,128,896]{2,1,0:T(8,128)(2,1)S(1)}, u32[]{:S(2)}, u32[]{:S(2)}) collective-permute-start(bf16[5,128,896]{2,1,0:T(8,128)(2,1)S(1)} %get-tuple-element.68), channel_id=1, source_target_pairs={{0,8},{4,36},{8,16},{12,44},{16,24},{20,52},{24,0},{28,60},{32,40}... | collective-permute-start | bytes 3440648 | tf_op jit(solution)/shard_map/ppermute | solution.py:41
  125.7 26.2 %collective-permute-start.21 = (bf16[5,128,896]{2,1,0:T(8,128)(2,1)S(1)}, bf16[5,128,896]{2,1,0:T(8,128)(2,1)S(1)}, u32[]{:S(2)}, u32[]{:S(2)}) collective-permute-start(bf16[5,128,896]{2,1,0:T(8,128)(2,1)S(1)} %get-tuple-element.70), channel_id=1, source_target_pairs={{0,24},{4,100},{8,0},{12,108},{16,8},{20,116},{24,16},{28,124},{32... | collective-permute-start | bytes 3440648 | tf_op jit(solution)/shard_map/ppermute | solution.py:41
  133.4 40.6 %collective-permute-start.10 = (bf16[3,112,768]{2,1,0:T(8,128)(2,1)S(1)}, bf16[3,112,768]{2,1,0:T(8,128)(2,1)S(1)}, u32[]{:S(2)}, u32[]{:S(2)}) collective-permute-start(bf16[3,112,768]{2,1,0:T(8,128)(2,1)S(1)} %get-tuple-element.80), channel_id=1, source_target_pairs={{0,16},{4,68},{8,24},{12,76},{16,0},{20,84},{24,8},{28,92},{32,48}... | collective-permute-start | bytes 1548296 | tf_op jit(solution)/shard_map/ppermute | solution.py:41
  135.0 41.7 %collective-permute-start.11 = (bf16[3,112,768]{2,1,0:T(8,128)(2,1)S(1)}, bf16[3,112,768]{2,1,0:T(8,128)(2,1)S(1)}, u32[]{:S(2)}, u32[]{:S(2)}) collective-permute-start(bf16[3,112,768]{2,1,0:T(8,128)(2,1)S(1)} %get-tuple-element.81), channel_id=1, source_target_pairs={{0,8},{4,36},{8,16},{12,44},{16,24},{20,52},{24,0},{28,60},{32,40}... | collective-permute-start | bytes 1548296 | tf_op jit(solution)/shard_map/ppermute | solution.py:41
  140.5 25.8 %collective-permute-start.13 = (bf16[2,112,768]{2,1,0:T(8,128)(2,1)S(1)}, bf16[2,112,768]{2,1,0:T(8,128)(2,1)S(1)}, u32[]{:S(2)}, u32[]{:S(2)}) collective-permute-start(bf16[2,112,768]{2,1,0:T(8,128)(2,1)S(1)} %get-tuple-element.85), channel_id=1, source_target_pairs={{0,16},{4,68},{8,24},{12,76},{16,0},{20,84},{24,8},{28,92},{32,48}... | collective-permute-start | bytes 1032200 | tf_op jit(solution)/shard_map/ppermute | solution.py:41
  151.4 18.4 %collective-permute-start.14 = (bf16[2,112,768]{2,1,0:T(8,128)(2,1)S(1)}, bf16[2,112,768]{2,1,0:T(8,128)(2,1)S(1)}, u32[]{:S(2)}, u32[]{:S(2)}) collective-permute-start(bf16[2,112,768]{2,1,0:T(8,128)(2,1)S(1)} %get-tuple-element.86), channel_id=1, source_target_pairs={{0,8},{4,36},{8,16},{12,44},{16,24},{20,52},{24,0},{28,60},{32,40}... | collective-permute-start | bytes 1032200 | tf_op jit(solution)/shard_map/ppermute | solution.py:41
  151.9 21.4 %collective-permute-start.15 = (bf16[2,112,768]{2,1,0:T(8,128)(2,1)S(1)}, bf16[2,112,768]{2,1,0:T(8,128)(2,1)S(1)}, u32[]{:S(2)}, u32[]{:S(2)}) collective-permute-start(bf16[2,112,768]{2,1,0:T(8,128)(2,1)S(1)} %get-tuple-element.87), channel_id=1, source_target_pairs={{0,24},{4,100},{8,0},{12,108},{16,8},{20,116},{24,16},{28,124},{32... | collective-permute-start | bytes 1032200 | tf_op jit(solution)/shard_map/ppermute | solution.py:41
  166.3 10.9 %collective-permute-start.12 = (bf16[3,112,768]{2,1,0:T(8,128)(2,1)S(1)}, bf16[3,112,768]{2,1,0:T(8,128)(2,1)S(1)}, u32[]{:S(2)}, u32[]{:S(2)}) collective-permute-start(bf16[3,112,768]{2,1,0:T(8,128)(2,1)S(1)} %get-tuple-element.82), channel_id=1, source_target_pairs={{0,24},{4,100},{8,0},{12,108},{16,8},{20,116},{24,16},{28,124},{32... | collective-permute-start | bytes 1548296 | tf_op jit(solution)/shard_map/ppermute | solution.py:41
  169.8 14.4 %collective-permute-start.22 = (bf16[5,32,896]{2,1,0:T(8,128)(2,1)S(1)}, bf16[5,32,896]{2,1,0:T(8,128)(2,1)S(1)}, u32[]{:S(2)}, u32[]{:S(2)}) collective-permute-start(bf16[5,32,896]{2,1,0:T(8,128)(2,1)S(1)} %get-tuple-element.91), channel_id=1, source_target_pairs={{0,64},{4,20},{8,72},{12,28},{16,80},{20,4},{24,88},{28,12},{32,96... | collective-permute-start | bytes 860168 | tf_op jit(solution)/shard_map/ppermute | solution.py:41
  173.2 12.9 %collective-permute-start.23 = (bf16[5,32,896]{2,1,0:T(8,128)(2,1)S(1)}, bf16[5,32,896]{2,1,0:T(8,128)(2,1)S(1)}, u32[]{:S(2)}, u32[]{:S(2)}) collective-permute-start(bf16[5,32,896]{2,1,0:T(8,128)(2,1)S(1)} %get-tuple-element.92), channel_id=1, source_target_pairs={{0,32},{4,12},{8,40},{12,20},{16,48},{20,28},{24,56},{28,4},{32,64... | collective-permute-start | bytes 860168 | tf_op jit(solution)/shard_map/ppermute | solution.py:41
  174.0 12.1 %collective-permute-start.24 = (bf16[5,32,896]{2,1,0:T(8,128)(2,1)S(1)}, bf16[5,32,896]{2,1,0:T(8,128)(2,1)S(1)}, u32[]{:S(2)}, u32[]{:S(2)}) collective-permute-start(bf16[5,32,896]{2,1,0:T(8,128)(2,1)S(1)} %get-tuple-element.93), channel_id=1, source_target_pairs={{0,96},{4,28},{8,104},{12,4},{16,112},{20,12},{24,120},{28,20},{32... | collective-permute-start | bytes 860168 | tf_op jit(solution)/shard_map/ppermute | solution.py:41
  177.6 9.4 %collective-permute-start.16 = (bf16[5,28,768]{2,1,0:T(8,128)(2,1)S(1)}, bf16[5,28,768]{2,1,0:T(8,128)(2,1)S(1)}, u32[]{:S(2)}, u32[]{:S(2)}) collective-permute-start(bf16[5,28,768]{2,1,0:T(8,128)(2,1)S(1)} %get-tuple-element.88), channel_id=1, source_target_pairs={{0,64},{4,20},{8,72},{12,28},{16,80},{20,4},{24,88},{28,12},{32,96... | collective-permute-start | bytes 645128 | tf_op jit(solution)/shard_map/ppermute | solution.py:41
  182.8 7.4 %collective-permute-start.17 = (bf16[5,28,768]{2,1,0:T(8,128)(2,1)S(1)}, bf16[5,28,768]{2,1,0:T(8,128)(2,1)S(1)}, u32[]{:S(2)}, u32[]{:S(2)}) collective-permute-start(bf16[5,28,768]{2,1,0:T(8,128)(2,1)S(1)} %get-tuple-element.89), channel_id=1, source_target_pairs={{0,32},{4,12},{8,40},{12,20},{16,48},{20,28},{24,56},{28,4},{32,64... | collective-permute-start | bytes 645128 | tf_op jit(solution)/shard_map/ppermute | solution.py:41
  184.2 6.8 %collective-permute-start.18 = (bf16[5,28,768]{2,1,0:T(8,128)(2,1)S(1)}, bf16[5,28,768]{2,1,0:T(8,128)(2,1)S(1)}, u32[]{:S(2)}, u32[]{:S(2)}) collective-permute-start(bf16[5,28,768]{2,1,0:T(8,128)(2,1)S(1)} %get-tuple-element.90), channel_id=1, source_target_pairs={{0,96},{4,28},{8,104},{12,4},{16,112},{20,12},{24,120},{28,20},{32... | collective-permute-start | bytes 645128 | tf_op jit(solution)/shard_map/ppermute | solution.py:41

commit v4 on v3

--- a/solution.py
+++ b/solution.py
@@ -67,9 +67,9 @@
 def gelu_both(v):
     c, a = 0.7978845608028654, 0.044715
     sq = v * v
-    t = jnp.tanh(c * v * (1.0 + a * sq))
-    up = 0.5 * (1.0 + t)
-    return v * up, up + 0.5 * v * (1.0 - t * t) * (c * (1.0 + 3.0 * a * sq))
+    up = 0.5 + 0.5 * jnp.tanh(v * (c + (c * a) * sq))
+    out = v * up
+    return out, 0.5 * up + out * (1.0 - up) * (c + (3.0 * a * c) * sq)
 
 
 def fill_rims(rimmed, block_ref, rim_ref):
@@ -106,21 +106,32 @@
     for copy in copies:
         copy.wait()
 
-    @pl.loop(0, n // TILE)
-    def _(m):
-        r = pl.multiple_of(m * TILE, TILE)
+    def product(m):
+        rows = pl.ds(pl.multiple_of(m * TILE, TILE), TILE)
+        total = jnp.dot(wide[rows, :], w_ref[...], preferred_element_type=F32)
+        for j in range(acc.shape[1]):
+            acc[m % 2, j] = total[:, j * LANES : (j + 1) * LANES]
+
+    def finish(m):
         q = pl.ds(pl.multiple_of(m * (TILE // 2), TILE // 2), TILE // 2)
-        total = jnp.dot(wide[pl.ds(r, TILE), :], w_ref[...], preferred_element_type=F32)
-        for j in range(acc.shape[0]):
+        for j in range(acc.shape[1]):
             cols = slice(j * LANES, (j + 1) * LANES)
-            acc[j] = total[:, cols]
-            even, even_slope = gelu_both(acc[j, pl.ds(0, TILE // 2, stride=2), :])
-            odd, odd_slope = gelu_both(acc[j, pl.ds(1, TILE // 2, stride=2), :])
+            even, even_slope = gelu_both(acc[m % 2, j, pl.ds(0, TILE // 2, stride=2), :])
+            odd, odd_slope = gelu_both(acc[m % 2, j, pl.ds(1, TILE // 2, stride=2), :])
             pooled_ref[q, cols] = ((even + odd) * 0.5).astype(BF)
-            slopes[0, q, cols] = even_slope * 0.5
-            slopes[1, q, cols] = odd_slope * 0.5
+            slopes[0, q, cols] = even_slope
+            slopes[1, q, cols] = odd_slope
         for side, out in enumerate((even_hbm, odd_hbm)):
             pltpu.make_async_copy(slopes.at[side, q], out.at[q], out_sem.at[side, m]).start()
+
+    product(0)
+
+    @pl.loop(1, n // TILE)
+    def _(m):
+        finish(m - 1)
+        product(m)
+
+    finish(n // TILE - 1)
 
     @pl.loop(0, n // TILE)
     def _(m):
@@ -143,7 +154,7 @@
             VM((n + 2 * RIM, f), BF),
             VM((PIECE + 2 * RIM, f), F32),
             VM((n, taps * f), BF),
-            VM((c // LANES, TILE, LANES), F32),
+            VM((2, c // LANES, TILE, LANES), F32),
             VM((2, n // 2, c), F32),
             pltpu.SemaphoreType.DMA((taps + 1,)),
             pltpu.SemaphoreType.DMA((2, n // TILE)),
@@ -242,13 +253,14 @@
         accept_ref[...], come_ref[:, each:, :].reshape(slots, c), preferred_element_type=F32
     )
     total = total * head_ref[...]
-    for copy in copies:
-        copy.wait()
+    copies[0].wait()
+    copies[1].wait()
     for j in range(pairs.shape[0]):
         cols = slice(j * LANES, (j + 1) * LANES)
         pairs[j, pl.ds(0, n, stride=2), :] = total[:, cols] * slopes[0, :, cols]
         pairs[j, pl.ds(1, n, stride=2), :] = total[:, cols] * slopes[1, :, cols]
         g_ref[:, cols] = pairs[j].astype(BF)
+    copies[2].wait()
     turned = lax.dot_general(
         order_ref[...], g_ref[...], (((1,), (1,)), ((), ())), preferred_element_type=F32
     )

time: 193 us -> 191 us (0.990)
  no operation moved by 1% of the time
where the time goes in v4:
time: 191 us; the launch traced here: 190 us
  Pallas kernels  78.1 us (41%)
  starting transfers between devices  58.2 us (30%)
  waiting for transfers between devices  30.3 us (16%)
  other arithmetic  12.2 us (6%)
  local copies, waits for them, and re-layouts  6.87 us (4%)
  matrix products  3.5 us (2%)
    ppermute x25, starting transfers between devices, move(): return lax.ppermute(value, 'seq', pairs)  35.5 us
    ppermute x25, waiting for transfers between devices, move(): return lax.ppermute(value, 'seq', pairs)  28 us
    pallas_call x2, Pallas kernels, conv_pool(): pl.pallas_call(functools.partial(conv_kernel, taps), out_shape=[jax.Shape...  25.9 us
    pallas_call x3, Pallas kernels, grad_parts(): pl.pallas_call(grad_kernel, grid=(taps,), out_shape=[jax.ShapeDtypeStruct...  20.9 us
    pallas_call x2, Pallas kernels, windows_of(): pl.pallas_call(functools.partial(window_kernel, taps), grid=(2 * n // PIE...  15.9 us
    all_to_all x1, starting transfers between devices, body(): come = lax.all_to_all(gone, 'seq', split_axis=0, concat_axis=0, tiled=True)  12.3 us
    pallas_call x1, Pallas kernels, conv_back(): pl.pallas_call(functools.partial(back_kernel, taps), out_shape=[jax.Shape...  11.8 us
    all_to_all x1, starting transfers between devices, body(): heard = lax.all_to_all(sent, 'seq', split_axis=0, concat_axis=0, tiled=True)  10.4 us
  transfers between devices with their start and end apart: 27, of which 10 were waited for; matrix products, arithmetic and copies ran while one was open for 8% of the time, Pallas kernels for 23%

profile of v4, /device:TPU:0, one launch (start us, length us, event | category | flops | bytes accessed | tf_op | source)
XLA Modules:
  0.0 190.4 jit_solution(8993114472320637671)
XLA Ops:
  0.7 0.7 broadcast_select_fusion.16
  2.1 0.7 convert_element_type.106
  3.5 0.9 convert_reduce_fusion
  4.4 0.7 multiply_add_fusion
  6.1 10.4 %all-to-all-start = ((bf16[32,2,16]{2,1,0:T(2,128)(2,1)}), bf16[32,2,16]{2,1,0:T(2,128)(2,1)S(1)}, u32[]{:S(2)}, u32[]{:S(2)}) async-start(bf16[32,2,16]{2,1,0:T(2,128)(2,1)} %copy.13), calls=%async_computation | async-start | bytes 32768 | tf_op jit(solution)/shard_map/all_to_all | solution.py:428
  17.5 14.8 %conv_pool.2 = (bf16[512,896]{1,0:T(8,128)(2,1)S(1)}, f32[512,896]{1,0:T(8,128)}, f32[512,896]{1,0:T(8,128)}) custom-call(bf16[1024,768]{1,0:T(8,128)(2,1)} %own_ref, bf16[32,768]{1,0:T(8,128)(2,1)S(1)} %pad_maximum_fusion.7.rim_ref.own_rim, bf16[5,768,896]{2,1,0:T(8,128)(2,1)} %w_hbm.3), custom_call_target="tpu_custom_call" | custom-call | flops 7046430720 | bytes 13041664 | tf_op jit(solution)/shard_map/conv_pool/pallas_call | solution.py:146
  32.7 0.8 collective-permute-start.3
  35.0 11.0 %conv_pool.3 = (bf16[256,1024]{1,0:T(8,128)(2,1)S(1)}, f32[256,1024]{1,0:T(8,128)}, f32[256,1024]{1,0:T(8,128)}) custom-call(bf16[512,896]{1,0:T(8,128)(2,1)S(1)} %get-tuple-element.55.x_hbm.own_ref, bf16[32,896]{1,0:T(8,128)(2,1)S(1)} %pad_maximum_fusion.3.rim_ref.own_rim, bf16[5,896,1024]{2,1,0:T(8,128)(2,1)} %w_hbm.5), custom_call_target="tpu_custom_call" | custom-call | flops 4697620480 | bytes 12713984 | tf_op jit(solution)/shard_map/conv_pool/pallas_call | solution.py:146
  46.1 2.1 %convolution_convert_fusion = bf16[1024,1024]{1,0:T(8,128)(2,1)} fusion(bf16[256,1024]{0,1:T(8,128)(2,1)S(1)} %bitcast.22, bf16[256,1024]{1,0:T(8,128)(2,1)S(1)} %get-tuple-element.51), kind=kOutput, calls=%fused_computation.8 | convolution fusion | flops 537919488 | bytes 3145728 | tf_op jit(solution)/shard_map/dot_general | solution.py:456
  48.2 12.3 %all-to-all-start.1 = ((bf16[32,32,1024]{2,1,0:T(8,128)(2,1)}), bf16[32,32,1024]{2,1,0:T(8,128)(2,1)S(1)}, u32[]{:S(2)}, u32[]{:S(2)}) async-start(bf16[32,32,1024]{2,1,0:T(8,128)(2,1)} %bitcast.21), calls=%async_computation.1 | async-start | bytes 4194304 | tf_op jit(solution)/shard_map/all_to_all | solution.py:459
  60.6 1.5 fusion.1.order_ref
  62.1 1.8 fusion.order_hbm
  63.9 0.7 broadcast_in_dim.46
  64.7 0.9 convolution_convert_fusion.1.accept_ref
  65.9 0.8 compare_select_fusion.donor_ref
  67.1 0.7 broadcast_select_fusion.12
  67.8 0.8 pad_maximum_fusion.6.other_rim
  68.7 1.4 copy-done.1
  70.1 1.4 copy-done.3
  71.5 0.8 copy-done.9
  72.3 10.1 %windows.2.wide_ref = bf16[5,2048,768]{2,1,0:T(8,128)(2,1)} custom-call(bf16[1024,768]{1,0:T(8,128)(2,1)S(1)} %copy-done.1, bf16[32,768]{1,0:T(8,128)(2,1)S(1)} %copy-done.9, bf16[1024,768]{1,0:T(8,128)(2,1)S(1)} %copy-done.3, bf16[32,768]{1,0:T(8,128)(2,1)S(1)} %pad_maximum_fusion.6.other_rim), custom_call_target="tpu_custom_call" | custom-call | bytes 18874368 | tf_op jit(solution)/shard_map/windows/pallas_call | solution.py:314
  82.4 5.9 %windows.3.wide_ref = bf16[5,1024,896]{2,1,0:T(8,128)(2,1)} custom-call(bf16[512,896]{1,0:T(8,128)(2,1)S(1)} %get-tuple-element.55.x_hbm.own_ref, bf16[32,896]{1,0:T(8,128)(2,1)S(1)} %copy-done.7, bf16[512,896]{1,0:T(8,128)(2,1)S(1)} %copy-done.5, bf16[32,896]{1,0:T(8,128)(2,1)S(1)} %pad_maximum_fusion.2.other_rim), custom_call_target="tpu_custom_call" | custom-call | bytes 11010048 | tf_op jit(solution)/shard_map/windows/pallas_call | solution.py:314
  88.3 2.2 %all-to-all-done.1 = bf16[32,32,1024]{2,1,0:T(8,128)(2,1)S(1)} async-done(((bf16[32,32,1024]{2,1,0:T(8,128)(2,1)}), bf16[32,32,1024]{2,1,0:T(8,128)(2,1)S(1)}, u32[]{:S(2)}, u32[]{:S(2)}) %all-to-all-start.1) | async-done | bytes 2097184 | tf_op jit(solution)/shard_map/all_to_all | solution.py:459
  90.5 3.7 %head_back.1 = (bf16[512,1024]{1,0:T(8,128)(2,1)S(1)}, bf16[512,512]{1,0:T(8,128)(2,1)S(1)}, bf16[512,512]{1,0:T(8,128)(2,1)S(1)}) custom-call(bf16[256,512]{1,0:T(8,128)(2,1)S(1)} %compare_select_fusion.donor_ref, bf16[256,512]{1,0:T(8,128)(2,1)S(1)} %convolution_convert_fusion.1.accept_ref, bf16[32,32,1024]{2,1,0:T(8,128)(2,1)S(1)} %all-to-all-done.1, ...), custom_call_target="tpu_custom_call" | custom-call | flops 1610612736 | bytes 8388608 | tf_op jit(solution)/shard_map/head_back/pallas_call | solution.py:274
  94.9 0.9 collective-permute-start.8
  96.4 8.5 %grad_parts.3 = (bf16[5,128,896]{2,1,0:T(8,128)(2,1)S(1)}, bf16[5,128,896]{2,1,0:T(8,128)(2,1)S(1)}, bf16[5,128,896]{2,1,0:T(8,128)(2,1)S(1)}, f32[5,128,896]{2,1,0:T(8,128)S(1)}) custom-call(bf16[512,512]{1,0:T(8,128)(2,1)S(1)} %get-tuple-element.65.mine_ref, bf16[512,512]{1,0:T(8,128)(2,1)S(1)} %collective-permute-done.6.got_ref, ...), custom_call_target="tpu_custom_call" | custom-call | flops 4697620480 | bytes 17104896 | tf_op jit(solution)/shard_map/grad_parts/pallas_call | solution.py:347
  104.9 11.8 %conv_back.1 = (bf16[448,1024]{1,0:T(8,128)(2,1)S(1)}, bf16[448,1024]{1,0:T(8,128)(2,1)S(1)}) custom-call(bf16[512,1024]{1,0:T(8,128)(2,1)S(1)} %get-tuple-element.72.g_ref, bf16[32,1024]{1,0:T(8,128)(2,1)S(1)} %pad_maximum_fusion.10.rim_ref, bf16[5,896,1024]{2,1,0:T(8,128)(2,1)} %w_hbm.5, f32[512,896]{1,0:T(8,128)S(1)} %copy-done.11, ...), custom_call_target="tpu_custom_call" | custom-call | flops 6341787648 | bytes 17334272 | tf_op jit(solution)/shard_map/conv_back/pallas_call | solution.py:215
  116.7 3.7 %collective-permute-start.9 = (bf16[448,1024]{1,0:T(8,128)(2,1)S(1)}, bf16[448,1024]{1,0:T(8,128)(2,1)S(1)}, u32[]{:S(2)}, u32[]{:S(2)}) collective-permute-start(bf16[448,1024]{1,0:T(8,128)(2,1)S(1)} %get-tuple-element.77), channel_id=1, source_target_pairs={{0,4},{4,0},{8,12},{12,8},{16,20},{20,16},{24,28},{28,24},{32,36},... | collective-permute-start | bytes 2752520 | tf_op jit(solution)/shard_map/ppermute | solution.py:41
  120.4 1.2 collective-permute-start.19
  121.6 2.7 %collective-permute-start.20 = (bf16[5,128,896]{2,1,0:T(8,128)(2,1)S(1)}, bf16[5,128,896]{2,1,0:T(8,128)(2,1)S(1)}, u32[]{:S(2)}, u32[]{:S(2)}) collective-permute-start(bf16[5,128,896]{2,1,0:T(8,128)(2,1)S(1)} %get-tuple-element.68), channel_id=1, source_target_pairs={{0,8},{4,36},{8,16},{12,44},{16,24},{20,52},{24,0},{28,60},{32,40}... | collective-permute-start | bytes 3440648 | tf_op jit(solution)/shard_map/ppermute | solution.py:41
  124.8 7.1 %grad_parts.4 = (bf16[3,112,768]{2,1,0:T(8,128)(2,1)S(1)}, bf16[3,112,768]{2,1,0:T(8,128)(2,1)S(1)}, bf16[3,112,768]{2,1,0:T(8,128)(2,1)S(1)}, f32[3,112,768]{2,1,0:T(8,128)S(1)}) custom-call(bf16[448,1024]{1,0:T(8,128)(2,1)S(1)} %get-tuple-element.83.mine_ref, bf16[448,1024]{1,0:T(8,128)(2,1)S(1)} %collective-permute-done.9.got_ref, ...), custom_call_target="tpu_custom_call" | custom-call | flops 4227858432 | bytes 14368768 | tf_op jit(solution)/shard_map/grad_parts/pallas_call | solution.py:347
  131.9 1.6 collective-permute-start.10
  133.5 5.2 %grad_parts.5 = (bf16[2,112,768]{2,1,0:T(8,128)(2,1)S(1)}, bf16[2,112,768]{2,1,0:T(8,128)(2,1)S(1)}, bf16[2,112,768]{2,1,0:T(8,128)(2,1)S(1)}, f32[2,112,768]{2,1,0:T(8,128)S(1)}) custom-call(bf16[448,1024]{1,0:T(8,128)(2,1)S(1)} %get-tuple-element.83.mine_ref, bf16[448,1024]{1,0:T(8,128)(2,1)S(1)} %collective-permute-done.9.got_ref, ...), custom_call_target="tpu_custom_call" | custom-call | flops 2818572288 | bytes 10190848 | tf_op jit(solution)/shard_map/grad_parts/pallas_call | solution.py:347
  138.8 4.1 %collective-permute-start.13 = (bf16[2,112,768]{2,1,0:T(8,128)(2,1)S(1)}, bf16[2,112,768]{2,1,0:T(8,128)(2,1)S(1)}, u32[]{:S(2)}, u32[]{:S(2)}) collective-permute-start(bf16[2,112,768]{2,1,0:T(8,128)(2,1)S(1)} %get-tuple-element.85), channel_id=1, source_target_pairs={{0,16},{4,68},{8,24},{12,76},{16,0},{20,84},{24,8},{28,92},{32,48}... | collective-permute-start | bytes 1032200 | tf_op jit(solution)/shard_map/ppermute | solution.py:41
  142.9 7.1 %collective-permute-done.20 = bf16[5,128,896]{2,1,0:T(8,128)(2,1)S(1)} collective-permute-done((bf16[5,128,896]{2,1,0:T(8,128)(2,1)S(1)}, bf16[5,128,896]{2,1,0:T(8,128)(2,1)S(1)}, u32[]{:S(2)}, u32[]{:S(2)}) %collective-permute-start.20) | collective-permute-done | bytes 1146912 | tf_op jit(solution)/shard_map/ppermute | solution.py:41
  150.4 2.9 %collective-permute-start.15 = (bf16[2,112,768]{2,1,0:T(8,128)(2,1)S(1)}, bf16[2,112,768]{2,1,0:T(8,128)(2,1)S(1)}, u32[]{:S(2)}, u32[]{:S(2)}) collective-permute-start(bf16[2,112,768]{2,1,0:T(8,128)(2,1)S(1)} %get-tuple-element.87), channel_id=1, source_target_pairs={{0,24},{4,100},{8,0},{12,108},{16,8},{20,116},{24,16},{28,124},{32... | collective-permute-start | bytes 1032200 | tf_op jit(solution)/shard_map/ppermute | solution.py:41
  153.8 11.2 %collective-permute-done.13 = bf16[2,112,768]{2,1,0:T(8,128)(2,1)S(1)} collective-permute-done((bf16[2,112,768]{2,1,0:T(8,128)(2,1)S(1)}, bf16[2,112,768]{2,1,0:T(8,128)(2,1)S(1)}, u32[]{:S(2)}, u32[]{:S(2)}) %collective-permute-start.13) | collective-permute-done | bytes 344096 | tf_op jit(solution)/shard_map/ppermute | solution.py:41
  165.1 3.4 %collective-permute-done.14 = bf16[2,112,768]{2,1,0:T(8,128)(2,1)S(1)} collective-permute-done((bf16[2,112,768]{2,1,0:T(8,128)(2,1)S(1)}, bf16[2,112,768]{2,1,0:T(8,128)(2,1)S(1)}, u32[]{:S(2)}, u32[]{:S(2)}) %collective-permute-start.14) | collective-permute-done | bytes 344096 | tf_op jit(solution)/shard_map/ppermute | solution.py:41
  168.5 3.2 %collective-permute-start.22 = (bf16[5,32,896]{2,1,0:T(8,128)(2,1)S(1)}, bf16[5,32,896]{2,1,0:T(8,128)(2,1)S(1)}, u32[]{:S(2)}, u32[]{:S(2)}) collective-permute-start(bf16[5,32,896]{2,1,0:T(8,128)(2,1)S(1)} %get-tuple-element.91), channel_id=1, source_target_pairs={{0,64},{4,20},{8,72},{12,28},{16,80},{20,4},{24,88},{28,12},{32,96... | collective-permute-start | bytes 860168 | tf_op jit(solution)/shard_map/ppermute | solution.py:41
  172.5 2.7 %collective-permute-start.24 = (bf16[5,32,896]{2,1,0:T(8,128)(2,1)S(1)}, bf16[5,32,896]{2,1,0:T(8,128)(2,1)S(1)}, u32[]{:S(2)}, u32[]{:S(2)}) collective-permute-start(bf16[5,32,896]{2,1,0:T(8,128)(2,1)S(1)} %get-tuple-element.93), channel_id=1, source_target_pairs={{0,96},{4,28},{8,104},{12,4},{16,112},{20,12},{24,120},{28,20},{32... | collective-permute-start | bytes 860168 | tf_op jit(solution)/shard_map/ppermute | solution.py:41
  175.2 0.8 collective-permute-done.12
  176.5 4.8 %collective-permute-start.16 = (bf16[5,28,768]{2,1,0:T(8,128)(2,1)S(1)}, bf16[5,28,768]{2,1,0:T(8,128)(2,1)S(1)}, u32[]{:S(2)}, u32[]{:S(2)}) collective-permute-start(bf16[5,28,768]{2,1,0:T(8,128)(2,1)S(1)} %get-tuple-element.88), channel_id=1, source_target_pairs={{0,64},{4,20},{8,72},{12,28},{16,80},{20,4},{24,88},{28,12},{32,96... | collective-permute-start | bytes 645128 | tf_op jit(solution)/shard_map/ppermute | solution.py:41
  181.3 1.4 collective-permute-start.17
  182.7 1.9 collective-permute-start.18
  184.6 0.9 fusion.5
  185.5 3.2 %collective-permute-done.17 = bf16[5,28,768]{2,1,0:T(8,128)(2,1)S(1)} collective-permute-done((bf16[5,28,768]{2,1,0:T(8,128)(2,1)S(1)}, bf16[5,28,768]{2,1,0:T(8,128)(2,1)S(1)}, u32[]{:S(2)}, u32[]{:S(2)}) %collective-permute-start.17) | collective-permute-done | bytes 215072 | tf_op jit(solution)/shard_map/ppermute | solution.py:41
  188.7 0.8 collective-permute-done.18
  189.5 0.9 fusion.11
  (104 shorter events, 9.8 us)
Async XLA Ops:
  0.6 16.1 %collective-permute-start = (bf16[1024,768]{1,0:T(8,128)(2,1)}, bf16[1024,768]{1,0:T(8,128)(2,1)S(1)}, u32[]{:S(2)}, u32[]{:S(2)}) collective-permute-start(bf16[1024,768]{1,0:T(8,128)(2,1)} %own_ref), channel_id=1, source_target_pairs={{0,4},{4,0},{8,12},{12,8},{16,20},{20,16},{24,28},{28,24},{32,36},... | collective-permute-start | bytes 4718600 | tf_op jit(solution)/shard_map/ppermute | solution.py:41
  1.5 15.2 %collective-permute-start.1 = (bf16[2,768]{1,0:T(2,128)(2,1)S(1)}, bf16[2,768]{1,0:T(2,128)(2,1)S(1)}, u32[]{:S(2)}, u32[]{:S(2)}) collective-permute-start(bf16[2,768]{1,0:T(2,128)(2,1)S(1)} %broadcast_select_fusion.16), channel_id=1, source_target_pairs={{8,4},{16,12},{24,20},{32,28},{40,36},{48,44},{56,52},{64,60},{72,... | collective-permute-start | bytes 9224 | tf_op jit(solution)/shard_map/ppermute | solution.py:41
  6.1 27.5 %all-to-all-start = ((bf16[32,2,16]{2,1,0:T(2,128)(2,1)}), bf16[32,2,16]{2,1,0:T(2,128)(2,1)S(1)}, u32[]{:S(2)}, u32[]{:S(2)}) async-start(bf16[32,2,16]{2,1,0:T(2,128)(2,1)} %copy.13), calls=%async_computation | async-start | bytes 32768 | tf_op jit(solution)/shard_map/all_to_all | solution.py:428
  16.7 17.4 %copy-start.16 = (f32[256]{0:T(256)}, f32[256]{0:T(256)S(1)}, u32[]{:S(2)}) copy-start(f32[256]{0:T(256)S(1)} %iota_convert_fusion) | copy-start | bytes 3076
  16.7 15.6 %copy-start.18 = (bf16[2,768]{1,0:T(2,128)(2,1)}, bf16[2,768]{1,0:T(2,128)(2,1)S(1)}, u32[]{:S(2)}) copy-start(bf16[2,768]{1,0:T(2,128)(2,1)S(1)} %collective-permute-done.1) | copy-start | bytes 9220
  16.7 15.6 %copy-start.2 = (bf16[1024,768]{1,0:T(8,128)(2,1)}, bf16[1024,768]{1,0:T(8,128)(2,1)S(1)}, u32[]{:S(2)}) copy-start(bf16[1024,768]{1,0:T(8,128)(2,1)S(1)} %collective-permute-done.other_ref) | copy-start | bytes 4718596
  16.8 0.7 copy-start.15
  17.5 14.9 %copy-start.8 = (bf16[32,768]{1,0:T(8,128)(2,1)}, bf16[32,768]{1,0:T(8,128)(2,1)S(1)}, u32[]{:S(2)}) copy-start(bf16[32,768]{1,0:T(8,128)(2,1)S(1)} %pad_maximum_fusion.7.rim_ref.own_rim) | copy-start | bytes 147460
  17.5 16.1 %copy-start.19 = (s32[256]{0:T(256)S(1)}, s32[256]{0:T(256)}, u32[]{:S(2)}) copy-start(s32[256]{0:T(256)} %param.14) | copy-start | bytes 3076
  32.4 2.6 %collective-permute-start.2 = (bf16[512,896]{1,0:T(8,128)(2,1)S(1)}, bf16[512,896]{1,0:T(8,128)(2,1)S(1)}, u32[]{:S(2)}, u32[]{:S(2)}) collective-permute-start(bf16[512,896]{1,0:T(8,128)(2,1)S(1)} %get-tuple-element.55.x_hbm.own_ref), channel_id=1, source_target_pairs={{0,4},{4,0},{8,12},{12,8},{16,20},{20,16},{24,28},{28,24},{32,36},... | collective-permute-start | bytes 2752520 | tf_op jit(solution)/shard_map/ppermute | solution.py:41
  32.7 1.5 collective-permute-start.3
  34.3 0.7 copy-start.17
  34.9 11.1 %copy-start.4 = (bf16[512,896]{1,0:T(8,128)(2,1)}, bf16[512,896]{1,0:T(8,128)(2,1)S(1)}, u32[]{:S(2)}) copy-start(bf16[512,896]{1,0:T(8,128)(2,1)S(1)} %collective-permute-done.2.other_ref) | copy-start | bytes 2752516
  35.0 11.1 %copy-start.13 = (bf16[14,896]{1,0:T(8,128)(2,1)}, bf16[14,896]{1,0:T(8,128)(2,1)S(1)}, u32[]{:S(2)}) copy-start(bf16[14,896]{1,0:T(8,128)(2,1)S(1)} %broadcast.543) | copy-start | bytes 75268
  35.0 11.1 %copy-start.6 = (bf16[32,896]{1,0:T(8,128)(2,1)}, bf16[32,896]{1,0:T(8,128)(2,1)S(1)}, u32[]{:S(2)}) copy-start(bf16[32,896]{1,0:T(8,128)(2,1)S(1)} %pad_maximum_fusion.3.rim_ref.own_rim) | copy-start | bytes 172036
  48.2 42.4 %all-to-all-start.1 = ((bf16[32,32,1024]{2,1,0:T(8,128)(2,1)}), bf16[32,32,1024]{2,1,0:T(8,128)(2,1)S(1)}, u32[]{:S(2)}, u32[]{:S(2)}) async-start(bf16[32,32,1024]{2,1,0:T(8,128)(2,1)} %bitcast.21), calls=%async_computation.1 | async-start | bytes 4194304 | tf_op jit(solution)/shard_map/all_to_all | solution.py:459
  65.6 1.5 collective-permute-start.4
  66.8 15.6 %collective-permute-start.5 = (bf16[2,896]{1,0:T(2,128)(2,1)}, bf16[2,896]{1,0:T(2,128)(2,1)S(1)}, u32[]{:S(2)}, u32[]{:S(2)}) collective-permute-start(bf16[2,896]{1,0:T(2,128)(2,1)} %copy-done.17), channel_id=1, source_target_pairs={{0,4},{4,0},{8,12},{12,8},{16,20},{20,16},{24,28},{28,24},{32,36},... | collective-permute-start | bytes 10760 | tf_op jit(solution)/shard_map/ppermute | solution.py:41
  68.7 1.4 copy-start.1
  70.1 1.4 copy-start.3
  71.5 0.8 copy-start.9
  72.3 10.1 %copy-start.14 = (bf16[14,896]{1,0:T(8,128)(2,1)S(1)}, bf16[14,896]{1,0:T(8,128)(2,1)}, u32[]{:S(2)}) copy-start(bf16[14,896]{1,0:T(8,128)(2,1)} %copy-done.13) | copy-start | bytes 75268
  72.3 10.1 %copy-start.5 = (bf16[512,896]{1,0:T(8,128)(2,1)S(1)}, bf16[512,896]{1,0:T(8,128)(2,1)}, u32[]{:S(2)}) copy-start(bf16[512,896]{1,0:T(8,128)(2,1)} %copy-done.4) | copy-start | bytes 2752516
  72.3 10.1 %copy-start.7 = (bf16[32,896]{1,0:T(8,128)(2,1)S(1)}, bf16[32,896]{1,0:T(8,128)(2,1)}, u32[]{:S(2)}) copy-start(bf16[32,896]{1,0:T(8,128)(2,1)} %copy-done.6) | copy-start | bytes 172036
  82.4 8.1 %copy-start.10 = (f32[1024]{0:T(1024)S(1)}, f32[1024]{0:T(1024)}, u32[]{:S(2)}) copy-start(f32[1024]{0:T(1024)} %param.11) | copy-start | bytes 12292
  94.2 2.1 %collective-permute-start.6 = (bf16[512,512]{1,0:T(8,128)(2,1)S(1)}, bf16[512,512]{1,0:T(8,128)(2,1)S(1)}, u32[]{:S(2)}, u32[]{:S(2)}) collective-permute-start(bf16[512,512]{1,0:T(8,128)(2,1)S(1)} %get-tuple-element.66), channel_id=1, source_target_pairs={{0,4},{4,0},{8,12},{12,8},{16,20},{20,16},{24,28},{28,24},{32,36},... | collective-permute-start | bytes 1572872 | tf_op jit(solution)/shard_map/ppermute | solution.py:41
  94.4 1.9 collective-permute-start.7
  94.9 1.3 collective-permute-start.8
  96.3 8.6 %copy-start = (bf16[896,896]{1,0:T(8,128)(2,1)S(1)}, bf16[896,896]{1,0:T(8,128)(2,1)}, u32[]{:S(2)}) copy-start(bf16[896,896]{1,0:T(8,128)(2,1)} %fusion.1.order_ref) | copy-start | bytes 4816900
  96.3 8.6 %copy-start.11 = (f32[512,896]{1,0:T(8,128)S(1)}, f32[512,896]{1,0:T(8,128)}, u32[]{:S(2)}) copy-start(f32[512,896]{1,0:T(8,128)} %get-tuple-element.73.even_ref) | copy-start | bytes 5505028
  96.3 8.6 %copy-start.12 = (f32[512,896]{1,0:T(8,128)S(1)}, f32[512,896]{1,0:T(8,128)}, u32[]{:S(2)}) copy-start(f32[512,896]{1,0:T(8,128)} %get-tuple-element.74.odd_ref) | copy-start | bytes 5505028
  116.7 8.1 %collective-permute-start.9 = (bf16[448,1024]{1,0:T(8,128)(2,1)S(1)}, bf16[448,1024]{1,0:T(8,128)(2,1)S(1)}, u32[]{:S(2)}, u32[]{:S(2)}) collective-permute-start(bf16[448,1024]{1,0:T(8,128)(2,1)S(1)} %get-tuple-element.77), channel_id=1, source_target_pairs={{0,4},{4,0},{8,12},{12,8},{16,20},{20,16},{24,28},{28,24},{32,36},... | collective-permute-start | bytes 2752520 | tf_op jit(solution)/shard_map/ppermute | solution.py:41
  120.4 18.4 %collective-permute-start.19 = (bf16[5,128,896]{2,1,0:T(8,128)(2,1)S(1)}, bf16[5,128,896]{2,1,0:T(8,128)(2,1)S(1)}, u32[]{:S(2)}, u32[]{:S(2)}) collective-permute-start(bf16[5,128,896]{2,1,0:T(8,128)(2,1)S(1)} %get-tuple-element.69), channel_id=1, source_target_pairs={{0,16},{4,68},{8,24},{12,76},{16,0},{20,84},{24,8},{28,92},{32,48}... | collective-permute-start | bytes 3440648 | tf_op jit(solution)/shard_map/ppermute | solution.py:41
  121.6 28.5 %collective-permute-start.20 = (bf16[5,128,896]{2,1,0:T(8,128)(2,1)S(1)}, bf16[5,128,896]{2,1,0:T(8,128)(2,1)S(1)}, u32[]{:S(2)}, u32[]{:S(2)}) collective-permute-start(bf16[5,128,896]{2,1,0:T(8,128)(2,1)S(1)} %get-tuple-element.68), channel_id=1, source_target_pairs={{0,8},{4,36},{8,16},{12,44},{16,24},{20,52},{24,0},{28,60},{32,40}... | collective-permute-start | bytes 3440648 | tf_op jit(solution)/shard_map/ppermute | solution.py:41
  124.2 26.2 %collective-permute-start.21 = (bf16[5,128,896]{2,1,0:T(8,128)(2,1)S(1)}, bf16[5,128,896]{2,1,0:T(8,128)(2,1)S(1)}, u32[]{:S(2)}, u32[]{:S(2)}) collective-permute-start(bf16[5,128,896]{2,1,0:T(8,128)(2,1)S(1)} %get-tuple-element.70), channel_id=1, source_target_pairs={{0,24},{4,100},{8,0},{12,108},{16,8},{20,116},{24,16},{28,124},{32... | collective-permute-start | bytes 3440648 | tf_op jit(solution)/shard_map/ppermute | solution.py:41
  131.9 40.6 %collective-permute-start.10 = (bf16[3,112,768]{2,1,0:T(8,128)(2,1)S(1)}, bf16[3,112,768]{2,1,0:T(8,128)(2,1)S(1)}, u32[]{:S(2)}, u32[]{:S(2)}) collective-permute-start(bf16[3,112,768]{2,1,0:T(8,128)(2,1)S(1)} %get-tuple-element.80), channel_id=1, source_target_pairs={{0,16},{4,68},{8,24},{12,76},{16,0},{20,84},{24,8},{28,92},{32,48}... | collective-permute-start | bytes 1548296 | tf_op jit(solution)/shard_map/ppermute | solution.py:41
  133.5 41.7 %collective-permute-start.11 = (bf16[3,112,768]{2,1,0:T(8,128)(2,1)S(1)}, bf16[3,112,768]{2,1,0:T(8,128)(2,1)S(1)}, u32[]{:S(2)}, u32[]{:S(2)}) collective-permute-start(bf16[3,112,768]{2,1,0:T(8,128)(2,1)S(1)} %get-tuple-element.81), channel_id=1, source_target_pairs={{0,8},{4,36},{8,16},{12,44},{16,24},{20,52},{24,0},{28,60},{32,40}... | collective-permute-start | bytes 1548296 | tf_op jit(solution)/shard_map/ppermute | solution.py:41
  138.8 26.2 %collective-permute-start.13 = (bf16[2,112,768]{2,1,0:T(8,128)(2,1)S(1)}, bf16[2,112,768]{2,1,0:T(8,128)(2,1)S(1)}, u32[]{:S(2)}, u32[]{:S(2)}) collective-permute-start(bf16[2,112,768]{2,1,0:T(8,128)(2,1)S(1)} %get-tuple-element.85), channel_id=1, source_target_pairs={{0,16},{4,68},{8,24},{12,76},{16,0},{20,84},{24,8},{28,92},{32,48}... | collective-permute-start | bytes 1032200 | tf_op jit(solution)/shard_map/ppermute | solution.py:41
  150.0 18.4 %collective-permute-start.14 = (bf16[2,112,768]{2,1,0:T(8,128)(2,1)S(1)}, bf16[2,112,768]{2,1,0:T(8,128)(2,1)S(1)}, u32[]{:S(2)}, u32[]{:S(2)}) collective-permute-start(bf16[2,112,768]{2,1,0:T(8,128)(2,1)S(1)} %get-tuple-element.86), channel_id=1, source_target_pairs={{0,8},{4,36},{8,16},{12,44},{16,24},{20,52},{24,0},{28,60},{32,40}... | collective-permute-start | bytes 1032200 | tf_op jit(solution)/shard_map/ppermute | solution.py:41
  150.4 21.3 %collective-permute-start.15 = (bf16[2,112,768]{2,1,0:T(8,128)(2,1)S(1)}, bf16[2,112,768]{2,1,0:T(8,128)(2,1)S(1)}, u32[]{:S(2)}, u32[]{:S(2)}) collective-permute-start(bf16[2,112,768]{2,1,0:T(8,128)(2,1)S(1)} %get-tuple-element.87), channel_id=1, source_target_pairs={{0,24},{4,100},{8,0},{12,108},{16,8},{20,116},{24,16},{28,124},{32... | collective-permute-start | bytes 1032200 | tf_op jit(solution)/shard_map/ppermute | solution.py:41
  165.0 11.0 %collective-permute-start.12 = (bf16[3,112,768]{2,1,0:T(8,128)(2,1)S(1)}, bf16[3,112,768]{2,1,0:T(8,128)(2,1)S(1)}, u32[]{:S(2)}, u32[]{:S(2)}) collective-permute-start(bf16[3,112,768]{2,1,0:T(8,128)(2,1)S(1)} %get-tuple-element.82), channel_id=1, source_target_pairs={{0,24},{4,100},{8,0},{12,108},{16,8},{20,116},{24,16},{28,124},{32... | collective-permute-start | bytes 1548296 | tf_op jit(solution)/shard_map/ppermute | solution.py:41
  168.5 14.2 %collective-permute-start.22 = (bf16[5,32,896]{2,1,0:T(8,128)(2,1)S(1)}, bf16[5,32,896]{2,1,0:T(8,128)(2,1)S(1)}, u32[]{:S(2)}, u32[]{:S(2)}) collective-permute-start(bf16[5,32,896]{2,1,0:T(8,128)(2,1)S(1)} %get-tuple-element.91), channel_id=1, source_target_pairs={{0,64},{4,20},{8,72},{12,28},{16,80},{20,4},{24,88},{28,12},{32,96... | collective-permute-start | bytes 860168 | tf_op jit(solution)/shard_map/ppermute | solution.py:41
  171.7 12.8 %collective-permute-start.23 = (bf16[5,32,896]{2,1,0:T(8,128)(2,1)S(1)}, bf16[5,32,896]{2,1,0:T(8,128)(2,1)S(1)}, u32[]{:S(2)}, u32[]{:S(2)}) collective-permute-start(bf16[5,32,896]{2,1,0:T(8,128)(2,1)S(1)} %get-tuple-element.92), channel_id=1, source_target_pairs={{0,32},{4,12},{8,40},{12,20},{16,48},{20,28},{24,56},{28,4},{32,64... | collective-permute-start | bytes 860168 | tf_op jit(solution)/shard_map/ppermute | solution.py:41
  172.5 12.1 %collective-permute-start.24 = (bf16[5,32,896]{2,1,0:T(8,128)(2,1)S(1)}, bf16[5,32,896]{2,1,0:T(8,128)(2,1)S(1)}, u32[]{:S(2)}, u32[]{:S(2)}) collective-permute-start(bf16[5,32,896]{2,1,0:T(8,128)(2,1)S(1)} %get-tuple-element.93), channel_id=1, source_target_pairs={{0,96},{4,28},{8,104},{12,4},{16,112},{20,12},{24,120},{28,20},{32... | collective-permute-start | bytes 860168 | tf_op jit(solution)/shard_map/ppermute | solution.py:41
  176.5 9.0 %collective-permute-start.16 = (bf16[5,28,768]{2,1,0:T(8,128)(2,1)S(1)}, bf16[5,28,768]{2,1,0:T(8,128)(2,1)S(1)}, u32[]{:S(2)}, u32[]{:S(2)}) collective-permute-start(bf16[5,28,768]{2,1,0:T(8,128)(2,1)S(1)} %get-tuple-element.88), channel_id=1, source_target_pairs={{0,64},{4,20},{8,72},{12,28},{16,80},{20,4},{24,88},{28,12},{32,96... | collective-permute-start | bytes 645128 | tf_op jit(solution)/shard_map/ppermute | solution.py:41
  181.3 7.4 %collective-permute-start.17 = (bf16[5,28,768]{2,1,0:T(8,128)(2,1)S(1)}, bf16[5,28,768]{2,1,0:T(8,128)(2,1)S(1)}, u32[]{:S(2)}, u32[]{:S(2)}) collective-permute-start(bf16[5,28,768]{2,1,0:T(8,128)(2,1)S(1)} %get-tuple-element.89), channel_id=1, source_target_pairs={{0,32},{4,12},{8,40},{12,20},{16,48},{20,28},{24,56},{28,4},{32,64... | collective-permute-start | bytes 645128 | tf_op jit(solution)/shard_map/ppermute | solution.py:41
  182.7 6.8 %collective-permute-start.18 = (bf16[5,28,768]{2,1,0:T(8,128)(2,1)S(1)}, bf16[5,28,768]{2,1,0:T(8,128)(2,1)S(1)}, u32[]{:S(2)}, u32[]{:S(2)}) collective-permute-start(bf16[5,28,768]{2,1,0:T(8,128)(2,1)S(1)} %get-tuple-element.90), channel_id=1, source_target_pairs={{0,96},{4,28},{8,104},{12,4},{16,112},{20,12},{24,120},{28,20},{32... | collective-permute-start | bytes 645128 | tf_op jit(solution)/shard_map/ppermute | solution.py:41
